TPU v7x, 32 devices: a whole 2x2x4 slice. The times are simulated.
32 devices in a mesh: gx: 8 (over y, x, core), gy: 4 (over z).
Axes of the slice: x: 2, y: 2, z: 4, core: 2. Of those that a mesh axis runs over, the one named last changes fastest.
Arguments:
- node_features: bfloat16 [16, 8, 64, 512], P('gx', 'gy'), may hold values from -6 to 6
- edge_features: bfloat16 [3, 16, 8, 64, 512], P(None, 'gx', 'gy'), may hold values from -6 to 6
- open_faces: int32 [3, 16, 8, 64], P(None, 'gx', 'gy'), may hold values 0 or 1
- edge_weight: bfloat16 [1536, 512], replicated, may hold values from -0.15625 to 0.15625
- node_weight: bfloat16 [512, 512], replicated, may hold values from -0.25 to 0.25
- cotangent: bfloat16 [16, 8, 64, 512], P('gx', 'gy'), may hold values from -6 to 6
Outputs:
- new_nodes: bfloat16 [16, 8, 64, 512], P('gx', 'gy')
- node_grad: bfloat16 [16, 8, 64, 512], P('gx', 'gy')
- edge_weight_grad: float32 [786432], P(('gx', 'gy'))
- node_weight_grad: float32 [262144], P(('gx', 'gy'))
All inputs are finite; a program needn't handle non-finite values. No bound on the sum of `open_faces` on one device may be relied on, other than what follows from the above.
Results may differ from a plain program's by a relative error of at most 0.013.
Values may be sent and summed in bfloat16 or wider, within the bound.
No kernel may reach another device: no remote copies, remote signals or barrier semaphores. Data moves between devices by JAX's collectives and lax.ppermute only.
A program may use at most 64 MiB of HBM per device.

v0:
```python
import jax
import jax.numpy as jnp
from jax import lax
from jax.sharding import PartitionSpec as P


def passed_along(value, axis, steps):
    count = lax.axis_size(axis)
    first, last = (max(0, -steps), min(count, count - steps))
    return lax.ppermute(value, axis, [(source, source + steps) for source in range(first, last)])


def silu_slope(values):
    sigmoid = jax.nn.sigmoid(values)
    return sigmoid * (1.0 + values * (1.0 - sigmoid))


def local(node_features, edge_features, open_faces, edge_weight, node_weight, cotangent):
    extent_first, extent_second, depth, features = node_features.shape
    total_first = extent_first * lax.axis_size("gx")
    total_second = extent_second * lax.axis_size("gy")
    place_first = lax.axis_index("gx") * extent_first + jnp.arange(extent_first)
    place_second = lax.axis_index("gy") * extent_second + jnp.arange(extent_second)
    inside_first = (place_first < total_first - 1).astype(jnp.float32)
    inside_second = (place_second < total_second - 1).astype(jnp.float32)
    inside_third = (jnp.arange(depth) < depth - 1).astype(jnp.float32)
    masks = open_faces.astype(jnp.float32)
    open_first = masks[0] * inside_first[:, None, None]
    open_second = masks[1] * inside_second[None, :, None]
    open_third = masks[2] * inside_third[None, None, :]
    open_all = jnp.stack([open_first, open_second, open_third])
    upper_first = passed_along(node_features[0:1], "gx", -1)
    upper_second = passed_along(node_features[:, 0:1], "gy", -1)
    zero_plane = jnp.zeros((extent_first, extent_second, 1, features), jnp.bfloat16)
    beside = [
        jnp.concatenate([node_features[1:], upper_first], axis=0),
        jnp.concatenate([node_features[:, 1:], upper_second], axis=1),
        jnp.concatenate([node_features[:, :, 1:], zero_plane], axis=2),
    ]
    inputs_all = jnp.concatenate(
        [
            jnp.concatenate([node_features, beside[direction], edge_features[direction]], axis=-1)
            for direction in range(3)
        ],
        axis=0,
    )
    flat_inputs = inputs_all.reshape(-1, 3 * features)
    preact = jnp.dot(flat_inputs, edge_weight, preferred_element_type=jnp.float32)
    preact = preact.reshape(3, extent_first, extent_second, depth, features)
    message = (jax.nn.silu(preact) * open_all[..., None]).astype(jnp.bfloat16)
    widened = message.astype(jnp.float32)
    zero_wide = jnp.zeros((extent_first, extent_second, 1, features), jnp.float32)
    summed = widened[0] + widened[1] + widened[2]
    summed = summed - jnp.concatenate([zero_wide, widened[2, :, :, :-1]], axis=2)
    from_first = passed_along(message[0, -1:], "gx", 1)
    from_second = passed_along(message[1, :, -1:], "gy", 1)
    entering_first = from_first.astype(jnp.float32)
    entering_second = from_second.astype(jnp.float32)
    summed = summed - jnp.concatenate([entering_first, widened[0, :-1]], axis=0)
    summed = summed - jnp.concatenate([entering_second, widened[1, :, :-1]], axis=1)
    summed_half = summed.astype(jnp.bfloat16)
    flat_summed = summed_half.reshape(-1, features)
    update = jnp.dot(flat_summed, node_weight, preferred_element_type=jnp.float32).reshape(
        node_features.shape
    )
    new_nodes = (node_features.astype(jnp.float32) + jax.nn.silu(update)).astype(jnp.bfloat16)
    grad_update = (cotangent.astype(jnp.float32) * silu_slope(update)).astype(jnp.bfloat16)
    flat_update = grad_update.reshape(-1, features)
    node_weight_grad = lax.dot_general(
        flat_summed, flat_update, (((0,), (0,)), ((), ())), preferred_element_type=jnp.float32
    )
    node_flat = node_weight_grad.reshape(-1)
    grad_summed = lax.dot_general(
        flat_update, node_weight, (((1,), (1,)), ((), ())), preferred_element_type=jnp.float32
    )
    grad_summed = grad_summed.reshape(node_features.shape).astype(jnp.bfloat16)
    grad_upper_first = passed_along(grad_summed[0:1], "gx", -1)
    grad_upper_second = passed_along(grad_summed[:, 0:1], "gy", -1)
    beside_grad = jnp.stack(
        [
            jnp.concatenate([grad_summed[1:], grad_upper_first], axis=0),
            jnp.concatenate([grad_summed[:, 1:], grad_upper_second], axis=1),
            jnp.concatenate([grad_summed[:, :, 1:], zero_plane], axis=2),
        ]
    )
    grad_message = grad_summed.astype(jnp.float32)[None] - beside_grad.astype(jnp.float32)
    grad_preact = (grad_message * open_all[..., None] * silu_slope(preact)).astype(jnp.bfloat16)
    flat_grad = grad_preact.reshape(-1, features)
    edge_weight_grad = lax.dot_general(
        flat_inputs, flat_grad, (((0,), (0,)), ((), ())), preferred_element_type=jnp.float32
    )
    backward = lax.dot_general(
        flat_grad,
        edge_weight[: 2 * features],
        (((1,), (1,)), ((), ())),
        preferred_element_type=jnp.float32,
    )
    backward = backward.reshape(3, extent_first, extent_second, depth, 2 * features)
    own_terms = backward[..., :features]
    toward = backward[..., features:]
    node_grad = cotangent.astype(jnp.float32) + own_terms[0] + own_terms[1] + own_terms[2]
    node_grad = node_grad + jnp.concatenate([zero_wide, toward[2, :, :, :-1]], axis=2)
    lower_first = passed_along(toward[0, -1:].astype(jnp.bfloat16), "gx", 1).astype(jnp.float32)
    lower_second = passed_along(toward[1, :, -1:].astype(jnp.bfloat16), "gy", 1).astype(jnp.float32)
    node_grad = node_grad + jnp.concatenate([lower_first, toward[0, :-1]], axis=0)
    node_grad = node_grad + jnp.concatenate([lower_second, toward[1, :, :-1]], axis=1)
    edge_flat = edge_weight_grad.reshape(-1)
    edge_part, node_part = (
        lax.psum_scatter(edge_flat, ("gx", "gy"), scatter_dimension=0, tiled=True),
        lax.psum_scatter(node_flat, ("gx", "gy"), scatter_dimension=0, tiled=True),
    )
    return (new_nodes, node_grad.astype(jnp.bfloat16), edge_part, node_part)


def solution(mesh):
    placed = (
        P("gx", "gy", None, None),
        P(None, "gx", "gy", None, None),
        P(None, "gx", "gy", None),
        P(),
        P(),
        P("gx", "gy", None, None),
    )
    return jax.shard_map(
        local,
        mesh=mesh,
        in_specs=placed,
        out_specs=(
            P("gx", "gy", None, None),
            P("gx", "gy", None, None),
            P(("gx", "gy")),
            P(("gx", "gy")),
        ),
        check_vma=False,
    )
```

profile of v0, /device:TPU:0, one launch (start us, length us, event | category | flops | bytes accessed | tf_op | source)
XLA Modules:
  0.0 200.6 jit_solution(1359634982088130227)
XLA Ops:
  7.2 0.0 copy-start
  7.2 0.0 copy-start.1
  7.2 0.0 all-reduce.9.cloned.1.call-start
  7.2 1.1 fusion.34
  8.3 1.3 collective-permute-start.1
  9.6 1.0 fusion.33
  10.6 1.3 collective-permute-start
  11.9 0.7 convert_element_type.98
  12.6 1.2 slice_bitcast_fusion.11
  13.8 0.1 slice_multiply_fusion.2
  13.9 0.0 copy-done.1
  13.9 0.0 copy-start.2
  13.9 0.1 slice.117
  14.0 2.8 %collective-permute-done.1 = bf16[2,1,64,512]{3,2,1,0:T(8,128)(2,1)S(1)} collective-permute-done((bf16[2,1,64,512]{3,2,1,0:T(8,128)(2,1)S(1)}, bf16[2,1,64,512]{3,2,1,0:T(8,128)(2,1)S(1)}, u32[]{:S(2)}, u32[]{:S(2)}) %collective-permute-start.1) | collective-permute-done | bytes 131104 | tf_op jit(solution)/shard_map/ppermute | solution.py:10
  16.8 0.0 collective-permute-done
  16.8 0.3 fusion.6
  17.1 0.0 copy-done.2
  17.1 1.6 fusion.30
  18.8 3.4 %collective-permute-start.2 = (bf16[1,2,64,512]{3,2,0,1:T(8,128)(2,1)S(1)}, bf16[1,2,64,512]{3,2,0,1:T(8,128)(2,1)S(1)}, u32[]{:S(2)}, u32[]{:S(2)}) collective-permute-start(bf16[1,2,64,512]{3,2,0,1:T(8,128)(2,1)S(1)} %slice_bitcast_fusion.15), channel_id=1, source_target_pairs={{0,4},{4,8},{8,12},{12,16},{16,20},{20,24},{24,28},{1,5},{5,9},{9,... | collective-permute-start | bytes 393224 | tf_op jit(solution)/shard_map/ppermute | solution.py:10
  22.2 4.6 %collective-permute-start.3 = (bf16[2,1,64,512]{3,2,0,1:T(8,128)(2,1)S(1)}, bf16[2,1,64,512]{3,2,0,1:T(8,128)(2,1)S(1)}, u32[]{:S(2)}, u32[]{:S(2)}) collective-permute-start(bf16[2,1,64,512]{3,2,0,1:T(8,128)(2,1)S(1)} %slice_bitcast_fusion.14), channel_id=1, source_target_pairs={{0,1},{1,2},{2,3},{4,5},{5,6},{6,7},{8,9},{9,10},{10,11},{12,13},{... | collective-permute-start | bytes 393224 | tf_op jit(solution)/shard_map/ppermute | solution.py:10
  26.8 0.0 collective-permute-done.2
  26.8 3.3 %collective-permute-done.3 = bf16[2,1,64,512]{3,2,0,1:T(8,128)(2,1)S(1)} collective-permute-done((bf16[2,1,64,512]{3,2,0,1:T(8,128)(2,1)S(1)}, bf16[2,1,64,512]{3,2,0,1:T(8,128)(2,1)S(1)}, u32[]{:S(2)}, u32[]{:S(2)}) %collective-permute-start.3) | collective-permute-done | bytes 131104 | tf_op jit(solution)/shard_map/ppermute | solution.py:10
  30.1 0.4 fusion.22
  30.5 0.0 copy-done
  30.5 0.0 copy-start.3
  30.5 1.1 add_convert_fusion
  31.6 0.0 copy-done.3
  31.6 0.4 fusion.35
  32.0 0.5 convolution_bitcast_fusion.1
  32.5 1.3 collective-permute-start.5
  33.8 0.1 slice.159
  33.9 1.3 collective-permute-start.4
  35.2 1.3 copy.25
  36.5 3.6 %collective-permute-done.5 = bf16[2,1,64,512]{3,2,1,0:T(8,128)(2,1)S(1)} collective-permute-done((bf16[2,1,64,512]{3,2,1,0:T(8,128)(2,1)S(1)}, bf16[2,1,64,512]{3,2,1,0:T(8,128)(2,1)S(1)}, u32[]{:S(2)}, u32[]{:S(2)}) %collective-permute-start.5) | collective-permute-done | bytes 131104 | tf_op jit(solution)/shard_map/ppermute | solution.py:10
  40.2 0.0 collective-permute-done.4
  40.2 0.7 multiply_convert_fusion
  40.9 1.4 convolution_bitcast_fusion
  42.3 2.5 %copy.24 = f32[192,4,8,128]{3,1,2,0:T(4,128)} copy(f32[192,4,8,128]{3,2,1,0:T(8,128)S(1)} %convolution_bitcast_fusion) | data formatting | bytes 6291456
  44.8 0.0 all-reduce.9.cloned.1.call-update
  44.9 1.0 fusion.9
  45.9 2.4 %collective-permute-start.6 = (bf16[1,2,64,512]{3,2,1,0:T(8,128)(2,1)S(1)}, bf16[1,2,64,512]{3,2,1,0:T(8,128)(2,1)S(1)}, u32[]{:S(2)}, u32[]{:S(2)}) collective-permute-start(bf16[1,2,64,512]{3,2,1,0:T(8,128)(2,1)S(1)} %slice_bitcast_fusion.13), channel_id=1, source_target_pairs={{0,4},{4,8},{8,12},{12,16},{16,20},{20,24},{24,28},{1,5},{5,9},{9,... | collective-permute-start | bytes 393224 | tf_op jit(solution)/shard_map/ppermute | solution.py:10
  48.3 5.0 %collective-permute-start.7 = (bf16[2,1,64,512]{3,2,1,0:T(8,128)(2,1)S(1)}, bf16[2,1,64,512]{3,2,1,0:T(8,128)(2,1)S(1)}, u32[]{:S(2)}, u32[]{:S(2)}) collective-permute-start(bf16[2,1,64,512]{3,2,1,0:T(8,128)(2,1)S(1)} %slice_bitcast_fusion.12), channel_id=1, source_target_pairs={{0,1},{1,2},{2,3},{4,5},{5,6},{6,7},{8,9},{9,10},{10,11},{12,13},{... | collective-permute-start | bytes 393224 | tf_op jit(solution)/shard_map/ppermute | solution.py:10
  53.5 0.0 collective-permute-done.6
  53.5 6.3 %collective-permute-done.7 = bf16[2,1,64,512]{3,2,1,0:T(8,128)(2,1)S(1)} collective-permute-done((bf16[2,1,64,512]{3,2,1,0:T(8,128)(2,1)S(1)}, bf16[2,1,64,512]{3,2,1,0:T(8,128)(2,1)S(1)}, u32[]{:S(2)}, u32[]{:S(2)}) %collective-permute-start.7) | collective-permute-done | bytes 131104 | tf_op jit(solution)/shard_map/ppermute | solution.py:10
  59.8 1.1 fusion.18
  60.9 129.9 %all-reduce.9.cloned.1.call-done = (f32[786432]{0:T(1024)}, f32[262144]{0:T(1024)}) async-done(((f32[786432]{0:T(1024)}, f32[262144]{0:T(1024)}), (f32[786432]{0:T(1024)}, f32[262144]{0:T(1024)})) %all-reduce.9.cloned.1.call-update) | async-done | bytes 4194320
  190.9 1.5 dynamic-slice
  192.4 1.4 dynamic-slice.1
  (22 shorter events, 0.4 us)
Async XLA Ops:
  7.2 23.3 %copy-start = (bf16[512,512]{1,0:T(8,128)(2,1)S(1)}, bf16[512,512]{1,0:T(8,128)(2,1)}, u32[]{:S(2)}) copy-start(bf16[512,512]{1,0:T(8,128)(2,1)} %param.10) | copy-start | bytes 1572868
  7.2 6.7 %copy-start.1 = (bf16[2,2,64,512]{3,2,1,0:T(8,128)(2,1)S(1)}, bf16[2,2,64,512]{3,2,1,0:T(8,128)(2,1)}, u32[]{:S(2)}) copy-start(bf16[2,2,64,512]{3,2,1,0:T(8,128)(2,1)} %param.6) | copy-start | bytes 786436
  7.2 183.7 %all-reduce.9.cloned.1.call-start = ((), (), s32[]{:S(2)}) async-start(), calls=%async_computation | async-start | bytes 8388608
  8.3 8.4 %collective-permute-start.1 = (bf16[2,1,64,512]{3,2,1,0:T(8,128)(2,1)S(1)}, bf16[2,1,64,512]{3,2,1,0:T(8,128)(2,1)S(1)}, u32[]{:S(2)}, u32[]{:S(2)}) collective-permute-start(bf16[2,1,64,512]{3,2,1,0:T(8,128)(2,1)S(1)} %get-tuple-element.18), channel_id=1, source_target_pairs={{1,0},{2,1},{3,2},{5,4},{6,5},{7,6},{9,8},{10,9},{11,10},{13,12},{... | collective-permute-start | bytes 393224 | tf_op jit(solution)/shard_map/ppermute | solution.py:10
  10.6 6.2 %collective-permute-start = (bf16[1,2,64,512]{3,2,1,0:T(8,128)(2,1)S(1)}, bf16[1,2,64,512]{3,2,1,0:T(8,128)(2,1)S(1)}, u32[]{:S(2)}, u32[]{:S(2)}) collective-permute-start(bf16[1,2,64,512]{3,2,1,0:T(8,128)(2,1)S(1)} %get-tuple-element.16), channel_id=1, source_target_pairs={{4,0},{8,4},{12,8},{16,12},{20,16},{24,20},{28,24},{5,1},{9,5},{13... | collective-permute-start | bytes 393224 | tf_op jit(solution)/shard_map/ppermute | solution.py:10
  13.9 3.2 %copy-start.2 = (bf16[1536,512]{1,0:T(8,128)(2,1)S(1)}, bf16[1536,512]{1,0:T(8,128)(2,1)}, u32[]{:S(2)}) copy-start(bf16[1536,512]{1,0:T(8,128)(2,1)} %param.9) | copy-start | bytes 4718596
  18.8 8.0 %collective-permute-start.2 = (bf16[1,2,64,512]{3,2,0,1:T(8,128)(2,1)S(1)}, bf16[1,2,64,512]{3,2,0,1:T(8,128)(2,1)S(1)}, u32[]{:S(2)}, u32[]{:S(2)}) collective-permute-start(bf16[1,2,64,512]{3,2,0,1:T(8,128)(2,1)S(1)} %slice_bitcast_fusion.15), channel_id=1, source_target_pairs={{0,4},{4,8},{8,12},{12,16},{16,20},{20,24},{24,28},{1,5},{5,9},{9,... | collective-permute-start | bytes 393224 | tf_op jit(solution)/shard_map/ppermute | solution.py:10
  22.2 7.9 %collective-permute-start.3 = (bf16[2,1,64,512]{3,2,0,1:T(8,128)(2,1)S(1)}, bf16[2,1,64,512]{3,2,0,1:T(8,128)(2,1)S(1)}, u32[]{:S(2)}, u32[]{:S(2)}) collective-permute-start(bf16[2,1,64,512]{3,2,0,1:T(8,128)(2,1)S(1)} %slice_bitcast_fusion.14), channel_id=1, source_target_pairs={{0,1},{1,2},{2,3},{4,5},{5,6},{6,7},{8,9},{9,10},{10,11},{12,13},{... | collective-permute-start | bytes 393224 | tf_op jit(solution)/shard_map/ppermute | solution.py:10
  30.5 1.1 copy-start.3
  32.5 7.6 %collective-permute-start.5 = (bf16[2,1,64,512]{3,2,1,0:T(8,128)(2,1)S(1)}, bf16[2,1,64,512]{3,2,1,0:T(8,128)(2,1)S(1)}, u32[]{:S(2)}, u32[]{:S(2)}) collective-permute-start(bf16[2,1,64,512]{3,2,1,0:T(8,128)(2,1)S(1)} %get-tuple-element.14), channel_id=1, source_target_pairs={{1,0},{2,1},{3,2},{5,4},{6,5},{7,6},{9,8},{10,9},{11,10},{13,12},{... | collective-permute-start | bytes 393224 | tf_op jit(solution)/shard_map/ppermute | solution.py:10
  33.9 6.3 %collective-permute-start.4 = (bf16[1,2,64,512]{3,2,1,0:T(8,128)(2,1)S(1)}, bf16[1,2,64,512]{3,2,1,0:T(8,128)(2,1)S(1)}, u32[]{:S(2)}, u32[]{:S(2)}) collective-permute-start(bf16[1,2,64,512]{3,2,1,0:T(8,128)(2,1)S(1)} %get-tuple-element.12), channel_id=1, source_target_pairs={{4,0},{8,4},{12,8},{16,12},{20,16},{24,20},{28,24},{5,1},{9,5},{13... | collective-permute-start | bytes 393224 | tf_op jit(solution)/shard_map/ppermute | solution.py:10
  45.9 7.6 %collective-permute-start.6 = (bf16[1,2,64,512]{3,2,1,0:T(8,128)(2,1)S(1)}, bf16[1,2,64,512]{3,2,1,0:T(8,128)(2,1)S(1)}, u32[]{:S(2)}, u32[]{:S(2)}) collective-permute-start(bf16[1,2,64,512]{3,2,1,0:T(8,128)(2,1)S(1)} %slice_bitcast_fusion.13), channel_id=1, source_target_pairs={{0,4},{4,8},{8,12},{12,16},{16,20},{20,24},{24,28},{1,5},{5,9},{9,... | collective-permute-start | bytes 393224 | tf_op jit(solution)/shard_map/ppermute | solution.py:10
  48.3 11.5 %collective-permute-start.7 = (bf16[2,1,64,512]{3,2,1,0:T(8,128)(2,1)S(1)}, bf16[2,1,64,512]{3,2,1,0:T(8,128)(2,1)S(1)}, u32[]{:S(2)}, u32[]{:S(2)}) collective-permute-start(bf16[2,1,64,512]{3,2,1,0:T(8,128)(2,1)S(1)} %slice_bitcast_fusion.12), channel_id=1, source_target_pairs={{0,1},{1,2},{2,3},{4,5},{5,6},{6,7},{8,9},{9,10},{10,11},{12,13},{... | collective-permute-start | bytes 393224 | tf_op jit(solution)/shard_map/ppermute | solution.py:10
Sparse Core Ops, SparseCore 0:
  45.0 145.8 all-reduce.8
where the time goes:
time: 201 us
  waiting for transfers between devices  146 us (73%)
  starting transfers between devices  20.6 us (10%)
  between operations  14.4 us (7%)
  local copies, waits for them, and re-layouts  10.4 us (5%)
  matrix products  6.01 us (3%)
  other arithmetic  3.38 us (2%)
    unnamed x2, waiting for transfers between devices  130 us
    ppermute x8, starting transfers between devices, passed_along(): lax.ppermute(value, axis, [(source, source + steps) for source in range(f...  20.5 us
    ppermute x8, waiting for transfers between devices, passed_along(): lax.ppermute(value, axis, [(source, source + steps) for source in range(f...  15.9 us
    unnamed x12, local copies, waits for them, and re-layouts  6.76 us
  transfers between devices with their start and end apart: 9, of which 5 were waited for; matrix products, arithmetic and copies ran while one was open for 3% of the time, Pallas kernels for 0%

commit v1 on v0

v1 whole, which is shorter than its diff:
```python
import functools

import jax
import jax.numpy as jnp
from jax import lax
from jax.experimental import pallas as pl
from jax.experimental.pallas import tpu as pltpu
from jax.sharding import PartitionSpec as P

F32 = jnp.float32
BF16 = jnp.bfloat16
PAD = 16


def passed_along(value, axis, steps):
    count = lax.axis_size(axis)
    first, last = (max(0, -steps), min(count, count - steps))
    return lax.ppermute(value, axis, [(source, source + steps) for source in range(first, last)])


def exchanged(value, axis, flip):
    count = lax.axis_size(axis)
    return lax.ppermute(value, axis, [(source, source ^ flip) for source in range(count)])


def dot(left, right):
    return jnp.dot(left, right, preferred_element_type=F32)


def dot_nt(left, right):
    return lax.dot_general(left, right, (((1,), (1,)), ((), ())), preferred_element_type=F32)


def dot_tn(left, right):
    return lax.dot_general(left, right, (((0,), (0,)), ((), ())), preferred_element_type=F32)


def column_of(row):
    size = row.shape[-1]
    spread = jnp.broadcast_to(row, (size, size))
    down = lax.broadcasted_iota(jnp.int32, (size, size), 0)
    across = lax.broadcasted_iota(jnp.int32, (size, size), 1)
    return jnp.sum(jnp.where(down == across, spread, 0.0), axis=1, keepdims=True)


def sigmoid(values):
    return 0.5 * jnp.tanh(0.5 * values) + 0.5


def call(kernel, outs, args, scratch=(), limit=60 << 20, cost=None):
    return pl.pallas_call(
        kernel,
        out_shape=[jax.ShapeDtypeStruct(shape, dtype) for shape, dtype in outs],
        in_specs=[pl.BlockSpec(memory_space=pltpu.VMEM)] * len(args),
        out_specs=[pl.BlockSpec(memory_space=pltpu.VMEM)] * len(outs),
        scratch_shapes=list(scratch),
        compiler_params=pltpu.CompilerParams(vmem_limit_bytes=limit),
        cost_estimate=cost,
    )(*args)


def products_kernel(node_ref, edge_ref, weight_ref, stored_ref, other_ref):
    features = node_ref.shape[-1]
    node = node_ref[...].reshape(-1, features)
    own = dot(node, weight_ref[:features])
    other_ref[...] = dot(node, weight_ref[features : 2 * features])
    for direction in range(3):
        edge = edge_ref[direction].reshape(-1, features)
        stored_ref[direction] = own + dot(edge, weight_ref[2 * features :])


def layer_kernel(
    dims,
    stored_ref, other_ref, weight_ref, node_weight_ref, node_ref, edge_ref, open_ref, cotangent_ref,
    above_first_ref, above_second_ref, below_first_ref, below_second_ref,
    new_ref, low_first_ref, low_second_ref, top_first_ref, top_second_ref,
    own_ref, enter_ref, slope_top_first_ref, slope_top_second_ref, slope_low_first_ref, slope_low_second_ref,
    send_ref, keep_ref,
    summed_ref, update_ref, slope_ref, slope_low_ref, message_ref, message_low_ref,
    grads_ref, total_ref,
):
    ex, ey, nz, features = dims
    at_first, at_second = lax.axis_index("gx"), lax.axis_index("gy")
    inside_first = (at_first < lax.axis_size("gx") - 1).astype(F32)
    inside_second = (at_second < lax.axis_size("gy") - 1).astype(F32)
    self_weight = weight_ref[:features]
    other_weight = weight_ref[features : 2 * features]
    stored_weight = weight_ref[2 * features :]

    def rows(x, y):
        return slice((x * ey + y) * nz, (x * ey + y + 1) * nz)

    def part(index):
        return slice(index * nz, (index + 1) * nz)

    def edge_terms(preact, open_column):
        gate = sigmoid(preact)
        opened = gate * open_column
        message = (preact * opened).astype(BF16).astype(F32)
        return message, opened * (1.0 + preact * (1.0 - gate))

    edge_rows_first, edge_rows_second = ey * nz, ex * nz
    above_first = dot(above_first_ref[...], other_weight)
    above_second = dot(above_second_ref[...], other_weight)
    node_below_first = below_first_ref[:edge_rows_first]
    edge_below_first = below_first_ref[edge_rows_first : 2 * edge_rows_first]
    node_below_second = below_second_ref[:edge_rows_second]
    edge_below_second = below_second_ref[edge_rows_second : 2 * edge_rows_second]
    low_first = dot(node_below_first, self_weight) + dot(edge_below_first, stored_weight)
    low_second = dot(node_below_second, self_weight) + dot(edge_below_second, stored_weight)
    mask_first = below_first_ref[2 * edge_rows_first :].astype(F32)
    mask_second = below_second_ref[2 * edge_rows_second :].astype(F32)
    down = lax.broadcasted_iota(jnp.int32, (nz, 1), 0)
    inside_third = jnp.where(down < nz - 1, 1.0, 0.0)
    opened = open_ref[...].astype(F32)

    for y in range(ey):
        message, slope = edge_terms(low_first[part(y)] + other_ref[rows(0, y)], column_of(mask_first[y : y + 1, :nz]))
        message_low_ref[part(y)] = message
        slope_low_ref[part(y)] = slope
    for x in range(ex):
        at = part(ey + x)
        message, slope = edge_terms(low_second[part(x)] + other_ref[rows(x, 0)], column_of(mask_second[x : x + 1, :nz]))
        message_low_ref[at] = message
        slope_low_ref[at] = slope
    for x in range(ex):
        for y in range(ey):
            here = rows(x, y)
            column = [
                column_of(opened[(direction * ex + x) * ey + y : (direction * ex + x) * ey + y + 1]) for direction in range(3)
            ]
            if x + 1 < ex:
                beyond = other_ref[rows(x + 1, y)]
            else:
                beyond, column[0] = above_first[part(y)], column[0] * inside_first
            message_ref[0, here], slope_ref[0, here] = edge_terms(stored_ref[0, here] + beyond, column[0])
            if y + 1 < ey:
                beyond = other_ref[rows(x, y + 1)]
            else:
                beyond, column[1] = above_second[part(x)], column[1] * inside_second
            message_ref[1, here], slope_ref[1, here] = edge_terms(stored_ref[1, here] + beyond, column[1])
            beyond = pltpu.roll(other_ref[here], nz - 1, 0)
            message_ref[2, here], slope_ref[2, here] = edge_terms(stored_ref[2, here] + beyond, column[2] * inside_third)
    for x in range(ex):
        for y in range(ey):
            here = rows(x, y)
            third = message_ref[2, here]
            total = message_ref[0, here] + message_ref[1, here] + third - pltpu.roll(third, 1, 0)
            total = total - (message_ref[0, rows(x - 1, y)] if x > 0 else message_low_ref[part(y)])
            total = total - (message_ref[1, rows(x, y - 1)] if y > 0 else message_low_ref[part(ey + x)])
            summed_ref[here] = total.astype(BF16)

    node = node_ref[...].reshape(-1, features)
    update = dot(summed_ref[...], node_weight_ref[...])
    gate = sigmoid(update)
    new_ref[...] = (node.astype(F32) + update * gate).astype(BF16).reshape(new_ref.shape)
    cotangent = cotangent_ref[...].reshape(-1, features).astype(F32)
    update_ref[...] = (cotangent * (gate * (1.0 + update * (1.0 - gate)))).astype(BF16)
    grad_summed = dot_nt(update_ref[...], node_weight_ref[...]).astype(BF16)
    for y in range(ey):
        low_first_ref[part(y)] = grad_summed[rows(0, y)]
        top_first_ref[part(y)] = grad_summed[rows(ex - 1, y)]
    for x in range(ex):
        low_second_ref[part(x)] = grad_summed[rows(x, 0)]
        top_second_ref[part(x)] = grad_summed[rows(x, ey - 1)]
    wide = grad_summed.astype(F32)

    count = ex * ey * nz
    for y in range(ey):
        entering = -wide[rows(0, y)] * slope_low_ref[part(y)]
        message_low_ref[part(y)] = entering
        grads_ref[3 * count + y * nz : 3 * count + (y + 1) * nz] = entering.astype(BF16)
    for x in range(ex):
        at = part(ey + x)
        entering = -wide[rows(x, 0)] * slope_low_ref[at]
        message_low_ref[at] = entering
        start = 3 * count + (ey + x) * nz
        grads_ref[start : start + nz] = entering.astype(BF16)
    for x in range(ex):
        for y in range(ey):
            here = rows(x, y)
            mine = wide[here]
            lead = [
                mine - wide[rows(x + 1, y)] if x + 1 < ex else mine,
                mine - wide[rows(x, y + 1)] if y + 1 < ey else mine,
                mine - pltpu.roll(mine, nz - 1, 0),
            ]
            for direction in range(3):
                grad = lead[direction] * slope_ref[direction, here]
                message_ref[direction, here] = grad
                start = direction * count + (x * ey + y) * nz
                grads_ref[start : start + nz] = grad.astype(BF16)
    for x in range(ex):
        for y in range(ey):
            here = rows(x, y)
            third = message_ref[2, here]
            own_ref[here] = message_ref[0, here] + message_ref[1, here] + third
            enter = pltpu.roll(third, 1, 0)
            enter = enter + (message_ref[0, rows(x - 1, y)] if x > 0 else message_low_ref[part(y)])
            enter = enter + (message_ref[1, rows(x, y - 1)] if y > 0 else message_low_ref[part(ey + x)])
            enter_ref[here] = enter
    for y in range(ey):
        slope_top_first_ref[part(y)] = slope_ref[0, rows(ex - 1, y)]
        slope_low_first_ref[part(y)] = slope_low_ref[part(y)]
    for x in range(ex):
        slope_top_second_ref[part(x)] = slope_ref[1, rows(x, ey - 1)]
        slope_low_second_ref[part(x)] = slope_low_ref[part(ey + x)]

    grads_low = grads_ref[3 * count :]
    total_ref[:features] = dot_tn(
        jnp.concatenate([node, node_below_first, node_below_second], axis=0),
        jnp.concatenate([own_ref[...].astype(BF16), grads_low], axis=0),
    )
    tops = [grads_ref[(x * ey + y) * nz : (x * ey + y + 1) * nz] for x in [ex - 1] for y in range(ey)]
    tops += [grads_ref[count + (x * ey + y) * nz : count + (x * ey + y + 1) * nz] for x in range(ex) for y in [ey - 1]]
    total_ref[features : 2 * features] = dot_tn(
        jnp.concatenate([node, above_first_ref[...], above_second_ref[...]], axis=0),
        jnp.concatenate([enter_ref[...].astype(BF16), *tops], axis=0),
    )
    edges = edge_ref[...].reshape(-1, features)
    total_ref[2 * features : 3 * features] = dot_tn(
        jnp.concatenate([edges, edge_below_first, edge_below_second], axis=0), grads_ref[...]
    )
    total_ref[3 * features :] = dot_tn(summed_ref[...], update_ref[...])

    if send_ref is None:
        keep_ref[...] = total_ref[...]
        return
    planes, seconds, chunk = send_ref.shape[0], lax.axis_size("gy"), send_ref.shape[1] // lax.axis_size("gy")
    edge_rows, node_rows = chunk * 3 // 4, chunk // 4
    core, plane = at_first % 2, at_first // 2
    for block in range(planes):
        for second in range(seconds):
            there = (plane ^ block) * 2
            for target, flip in ((keep_ref, core), (send_ref, 1 - core)):
                device = (there + flip) * seconds + (at_second ^ second)
                edge_at = pl.multiple_of(device * edge_rows, 8)
                node_at = pl.multiple_of(3 * features + device * node_rows, 8)
                start = second * chunk
                target[block, start : start + edge_rows] = total_ref[pl.ds(edge_at, edge_rows)].astype(target.dtype)
                target[block, start + edge_rows : start + chunk] = total_ref[pl.ds(node_at, node_rows)].astype(target.dtype)


def node_grad_kernel(
    dims, own_ref, enter_ref, slope_top_first_ref, slope_top_second_ref, slope_low_first_ref, slope_low_second_ref,
    above_first_ref, above_second_ref, below_first_ref, below_second_ref, cotangent_ref, weight_ref, out_ref,
):
    ex, ey, nz, features = dims

    def rows(x, y):
        return slice((x * ey + y) * nz, (x * ey + y + 1) * nz)

    def part(index):
        return slice(index * nz, (index + 1) * nz)

    own, enter = [], []
    for x in range(ex):
        for y in range(ey):
            grad = own_ref[rows(x, y)]
            if x == ex - 1:
                grad = grad - above_first_ref[part(y)].astype(F32) * slope_top_first_ref[part(y)]
            if y == ey - 1:
                grad = grad - above_second_ref[part(x)].astype(F32) * slope_top_second_ref[part(x)]
            own.append(grad.astype(BF16))
            grad = enter_ref[rows(x, y)]
            if x == 0:
                grad = grad + below_first_ref[part(y)].astype(F32) * slope_low_first_ref[part(y)]
            if y == 0:
                grad = grad + below_second_ref[part(x)].astype(F32) * slope_low_second_ref[part(x)]
            enter.append(grad.astype(BF16))
    result = dot_nt(jnp.concatenate(own, axis=0), weight_ref[:features])
    result = result + dot_nt(jnp.concatenate(enter, axis=0), weight_ref[features : 2 * features])
    result = result + cotangent_ref[...].reshape(-1, features).astype(F32)
    out_ref[...] = result.astype(BF16).reshape(out_ref.shape)


def pair_sum_kernel(keep_ref, received_ref, kept_ref, *send_refs):
    kept_ref[...] = keep_ref[0] + received_ref[0].astype(F32)
    for index, send_ref in enumerate(send_refs):
        send_ref[...] = (keep_ref[index + 1] + received_ref[index + 1].astype(F32)).astype(BF16)


def plane_sum_kernel(groups, keep_ref, *refs):
    received, kept_ref, send_refs = refs[: groups[0] - 1], refs[groups[0] - 1], refs[groups[0] :]
    chunk = kept_ref.shape[0]
    for index in range(groups[1]):
        here = slice(index * chunk, (index + 1) * chunk)
        total = keep_ref[here]
        for ref in received:
            total = total + ref[here].astype(F32)
        if index == 0:
            kept_ref[...] = total
        else:
            send_refs[index - 1][...] = total.astype(BF16)


def last_sum_kernel(keep_ref, *refs):
    received, edge_ref, node_ref = refs[:-2], refs[-2], refs[-1]
    total = keep_ref[...]
    for ref in received:
        total = total + ref[...].astype(F32)
    lanes = edge_ref.shape[1]
    pieces = total.shape[1] // lanes
    edge_rows, node_rows = edge_ref.shape[0] // pieces, node_ref.shape[0] // pieces
    for piece in range(pieces):
        across = slice(piece * lanes, (piece + 1) * lanes)
        edge_ref[pl.ds(piece, edge_rows, stride=pieces)] = total[:edge_rows, across]
        node_ref[pl.ds(piece, node_rows, stride=pieces)] = total[edge_rows:, across]


def local(node_features, edge_features, open_faces, edge_weight, node_weight, cotangent):
    dims = ex, ey, nz, features = node_features.shape
    firsts, seconds = lax.axis_size("gx"), lax.axis_size("gy")
    devices = firsts * seconds
    count = ex * ey * nz

    def upward(nodes, edges, mask):
        mask = jnp.pad(mask.astype(BF16), ((0, PAD - mask.shape[0]), (0, features - mask.shape[1])))
        return jnp.concatenate([nodes.reshape(-1, features), edges.reshape(-1, features), mask], axis=0)

    above_first = passed_along(node_features[0].reshape(-1, features), "gx", -1)
    above_second = passed_along(node_features[:, 0].reshape(-1, features), "gy", -1)
    below_first = passed_along(upward(node_features[-1], edge_features[0, -1], open_faces[0, -1]), "gx", 1)
    below_second = passed_along(upward(node_features[:, -1], edge_features[1, :, -1], open_faces[1, :, -1]), "gy", 1)

    stored, other = call(
        products_kernel, [((3, count, features), F32), ((count, features), F32)], [node_features, edge_features, edge_weight]
    )
    total_rows = 4 * features
    chunk = total_rows // devices
    by_hand = (
        total_rows % devices == 0
        and chunk % 64 == 0
        and features % 128 == 0
        and firsts % 2 == 0
        and firsts & (firsts - 1) == 0
        and seconds & (seconds - 1) == 0
    )
    planes = firsts // 2
    face_first, face_second = (ey * nz, features), (ex * nz, features)
    outs = [(node_features.shape, BF16), (face_first, BF16), (face_second, BF16), (face_first, BF16), (face_second, BF16)]
    outs += [((count, features), F32)] * 2 + [(face_first, F32), (face_second, F32)] * 2
    if by_hand:
        outs += [((planes, seconds * chunk, features), BF16), ((planes, seconds * chunk, features), F32)]
        kernel = functools.partial(layer_kernel, dims)
    else:
        outs += [((total_rows, features), F32)]

        def kernel(*refs):
            layer_kernel(dims, *refs[:23], None, *refs[23:])

    low_rows = (ex + ey) * nz
    results = call(
        kernel,
        outs,
        [
            stored, other, edge_weight, node_weight, node_features, edge_features, open_faces.reshape(3 * ex * ey, nz), cotangent,
            above_first, above_second, below_first, below_second,
        ],
        scratch=[
            pltpu.VMEM((count, features), BF16),
            pltpu.VMEM((count, features), BF16),
            pltpu.VMEM((3, count, features), F32),
            pltpu.VMEM((low_rows, features), F32),
            pltpu.VMEM((3, count, features), F32),
            pltpu.VMEM((low_rows, features), F32),
            pltpu.VMEM((3 * count + low_rows, features), BF16),
            pltpu.VMEM((total_rows, features), F32),
        ],
    )
    new_nodes, low_first, low_second, top_first, top_second = results[:5]

    if by_hand:
        send, keep = results[11:]
        received = exchanged(send, "gx", 1)
    grad_above_first = passed_along(low_first, "gx", -1)
    grad_above_second = passed_along(low_second, "gy", -1)
    grad_below_first = passed_along(top_first, "gx", 1)
    grad_below_second = passed_along(top_second, "gy", 1)
    (node_grad,) = call(
        functools.partial(node_grad_kernel, dims),
        [(node_features.shape, BF16)],
        [*results[5:11], grad_above_first, grad_above_second, grad_below_first, grad_below_second, cotangent, edge_weight],
    )
    if not by_hand:
        total = results[11]
        edge_part = lax.psum_scatter(total[: 3 * features].reshape(-1), ("gx", "gy"), scatter_dimension=0, tiled=True)
        node_part = lax.psum_scatter(total[3 * features :].reshape(-1), ("gx", "gy"), scatter_dimension=0, tiled=True)
        return new_nodes, node_grad, edge_part, node_part

    block = (seconds * chunk, features)
    kept, *sends = call(pair_sum_kernel, [(block, F32)] + [(block, BF16)] * (planes - 1), [keep, received])
    arrived = [exchanged(value, "gx", 2 * (index + 1)) for index, value in enumerate(sends)]
    kept, *sends = call(
        functools.partial(plane_sum_kernel, (planes, seconds)),
        [((chunk, features), F32)] + [((chunk, features), BF16)] * (seconds - 1),
        [kept, *arrived],
    )
    arrived = [exchanged(value, "gy", index + 1) for index, value in enumerate(sends)]
    pieces = features // 128
    edge_part, node_part = call(
        last_sum_kernel, [((chunk * 3 // 4 * pieces, 128), F32), ((chunk // 4 * pieces, 128), F32)], [kept, *arrived]
    )
    return new_nodes, node_grad, edge_part.reshape(-1), node_part.reshape(-1)


def solution(mesh):
    placed = (
        P("gx", "gy", None, None),
        P(None, "gx", "gy", None, None),
        P(None, "gx", "gy", None),
        P(),
        P(),
        P("gx", "gy", None, None),
    )
    return jax.shard_map(
        local,
        mesh=mesh,
        in_specs=placed,
        out_specs=(
            P("gx", "gy", None, None),
            P("gx", "gy", None, None),
            P(("gx", "gy")),
            P(("gx", "gy")),
        ),
        check_vma=False,
    )
```

time: 201 us -> 70.5 us (0.35)
  waiting for transfers between devices: 146 us -> 10.8 us
  Pallas kernels: 0 us -> 22.4 us
  between operations: 14.4 us -> 0.9 us
  starting transfers between devices: 20.6 us -> 27.8 us
  matrix products: 6.01 us -> 0 us
  local copies, waits for them, and re-layouts: 10.4 us -> 7.34 us
  other arithmetic: 3.38 us -> 0.79 us
    unnamed x2 -> x0, waiting for transfers between devices: 130 us -> none
    pallas_call x0 -> x6, Pallas kernels: none -> 22.4 us  [call(): pl.pallas_call(kernel, out_shape=[jax.ShapeDtypeStruct(shape, dtype) for...]
    ppermute x8, waiting for transfers between devices: 15.9 us -> 1.21 us  [passed_along(): lax.ppermute(value, axis, [(source, source + steps) for source in range(f...]
    ppermute x0 -> x7, starting transfers between devices: none -> 11.4 us  [exchanged(): lax.ppermute(value, axis, [(source, source ^ flip) for source in range(co...]
    ppermute x0 -> x7, waiting for transfers between devices: none -> 9.61 us  [exchanged(): lax.ppermute(value, axis, [(source, source ^ flip) for source in range(co...]
    dot_general x6 -> x0, matrix products: 6.01 us -> none  [the longest x1 1.6 us: local(): jnp.dot(flat_inputs, edge_weight, preferred_element_type=jnp.float32)]
    ppermute x8, starting transfers between devices: 20.5 us -> 16.3 us  [passed_along(): lax.ppermute(value, axis, [(source, source + steps) for source in range(f...]
    convert_element_type x10 -> x0, other arithmetic: 2.96 us -> none  [the longest x1 1.12 us: local(): return (new_nodes, node_grad.astype(jnp.bfloat16), edge_part, node_part)]
  transfers between devices with their start and end apart: 9 -> 15, of which waited for: 5 -> 5; matrix products, arithmetic and copies ran while one was open for 3% -> 2% of each run, Pallas kernels for 0% -> 13%
where the time goes in v1:
time: 70.5 us; the launch traced here: 70.1 us
  starting transfers between devices  27.8 us (39%)
  Pallas kernels  22.4 us (32%)
  waiting for transfers between devices  10.8 us (15%)
  local copies, waits for them, and re-layouts  7.34 us (10%)
  between operations  0.9 us (1%)
  other arithmetic  0.79 us (1%)
    pallas_call x6, Pallas kernels, call(): pl.pallas_call(kernel, out_shape=[jax.ShapeDtypeStruct(shape, dtype) for...  22.4 us
    ppermute x8, starting transfers between devices, passed_along(): lax.ppermute(value, axis, [(source, source + steps) for source in range(f...  16.3 us
    ppermute x7, starting transfers between devices, exchanged(): lax.ppermute(value, axis, [(source, source ^ flip) for source in range(co...  11.4 us
    ppermute x7, waiting for transfers between devices, exchanged(): lax.ppermute(value, axis, [(source, source ^ flip) for source in range(co...  9.61 us
    unnamed x43, local copies, waits for them, and re-layouts  3.87 us
  transfers between devices with their start and end apart: 15, of which 5 were waited for; matrix products, arithmetic and copies ran while one was open for 2% of the time, Pallas kernels for 13%

profile of v1, /device:TPU:0, one launch (start us, length us, event | category | flops | bytes accessed | tf_op | source)
XLA Modules:
  0.0 70.1 jit_solution(18048979978898434685)
XLA Ops:
  0.6 0.0 copy-start
  0.7 0.7 %convert.4 = bf16[3,2,2,64]{3,2,1,0:T(2,128)(2,1)S(1)} convert(s32[3,2,2,64]{3,2,1,0:T(2,128)} %param.8) | non-fusion elementwise | flops 768 | bytes 4608 | tf_op jit(solution)/shard_map/convert.1
  1.4 0.9 %slice.32 = bf16[1,2,1,64,512]{4,3,2,1,0:T(8,128)(2,1)S(1)} slice(bf16[3,2,2,64,512]{4,3,2,1,0:T(8,128)(2,1)} %edge_ref.3), slice={[1:2], [0:2], [1:2], [0:64], [0:512]} | slice | bytes 262144 | tf_op jit(solution)/shard_map/slice | solution.py:324
  2.3 1.0 %fusion.4 = (bf16[2,1,64,512]{3,2,1,0:T(8,128)(2,1)S(1)}, bf16[2,1,64,512]{3,2,1,0:T(8,128)(2,1)S(1)}) fusion(bf16[2,2,64,512]{3,2,1,0:T(8,128)(2,1)} %node_ref.3), kind=kLoop, calls=%fused_computation.7 | loop fusion | bytes 524288 | tf_op jit(solution)/shard_map/slice | solution.py:324
  3.4 5.0 %collective-permute-start.3 = (bf16[272,512]{1,0:T(8,128)(2,1)S(1)}, bf16[272,512]{1,0:T(8,128)(2,1)S(1)}, u32[]{:S(2)}, u32[]{:S(2)}) collective-permute-start(bf16[272,512]{1,0:T(8,128)(2,1)S(1)} %fusion.3), channel_id=1, source_target_pairs={{0,1},{1,2},{2,3},{4,5},{5,6},{6,7},{8,9},{9,10},{10,11},{12,13},{... | collective-permute-start | bytes 835592 | tf_op jit(solution)/shard_map/ppermute | solution.py:18
  8.4 0.9 %slice.29 = bf16[1,1,2,64,512]{4,3,2,1,0:T(8,128)(2,1)S(1)} slice(bf16[3,2,2,64,512]{4,3,2,1,0:T(8,128)(2,1)} %edge_ref.3), slice={[0:1], [1:2], [0:2], [0:64], [0:512]} | slice | bytes 262144 | tf_op jit(solution)/shard_map/slice | solution.py:323
  9.3 1.5 %collective-permute-start.2 = (bf16[272,512]{1,0:T(8,128)(2,1)S(1)}, bf16[272,512]{1,0:T(8,128)(2,1)S(1)}, u32[]{:S(2)}, u32[]{:S(2)}) collective-permute-start(bf16[272,512]{1,0:T(8,128)(2,1)S(1)} %fusion.2), channel_id=1, source_target_pairs={{0,4},{4,8},{8,12},{12,16},{16,20},{20,24},{24,28},{1,5},{5,9},{9,... | collective-permute-start | bytes 835592 | tf_op jit(solution)/shard_map/ppermute | solution.py:18
  10.8 1.3 %collective-permute-start = (bf16[128,512]{1,0:T(8,128)(2,1)S(1)}, bf16[128,512]{1,0:T(8,128)(2,1)S(1)}, u32[]{:S(2)}, u32[]{:S(2)}) collective-permute-start(bf16[128,512]{1,0:T(8,128)(2,1)S(1)} %bitcast.18), channel_id=1, source_target_pairs={{4,0},{8,4},{12,8},{16,12},{20,16},{24,20},{28,24},{5,1},{9,5},{13... | collective-permute-start | bytes 393224 | tf_op jit(solution)/shard_map/ppermute | solution.py:18
  12.1 1.3 %collective-permute-start.1 = (bf16[128,512]{1,0:T(8,128)(2,1)S(1)}, bf16[128,512]{1,0:T(8,128)(2,1)S(1)}, u32[]{:S(2)}, u32[]{:S(2)}) collective-permute-start(bf16[128,512]{1,0:T(8,128)(2,1)S(1)} %bitcast.17), channel_id=1, source_target_pairs={{1,0},{2,1},{3,2},{5,4},{6,5},{7,6},{9,8},{10,9},{11,10},{13,12},{... | collective-permute-start | bytes 393224 | tf_op jit(solution)/shard_map/ppermute | solution.py:18
  13.4 0.6 reshape.19.open_ref
  14.0 3.7 %shard_map.93 = (f32[3,256,512]{2,1,0:T(8,128)}, f32[256,512]{1,0:T(8,128)}) custom-call(bf16[2,2,64,512]{3,2,1,0:T(8,128)(2,1)} %node_ref.3, bf16[3,2,2,64,512]{4,3,2,1,0:T(8,128)(2,1)} %edge_ref.3, bf16[1536,512]{1,0:T(8,128)(2,1)} %weight_ref.5), custom_call_target="tpu_custom_call" | custom-call | tf_op jit(solution)/shard_map/pallas_call | solution.py:51
  17.8 0.0 collective-permute-done.above_first_ref
  17.8 1.2 %collective-permute-done.1.above_second_ref = bf16[128,512]{1,0:T(8,128)(2,1)S(1)} collective-permute-done((bf16[128,512]{1,0:T(8,128)(2,1)S(1)}, bf16[128,512]{1,0:T(8,128)(2,1)S(1)}, u32[]{:S(2)}, u32[]{:S(2)}) %collective-permute-start.1) | collective-permute-done | bytes 131104 | tf_op jit(solution)/shard_map/ppermute | solution.py:18
  19.0 0.0 collective-permute-done.3.below_second_ref
  19.0 0.0 collective-permute-done.2.below_first_ref
  19.0 0.6 copy-done.12
  19.6 0.1 copy-done.2
  19.8 0.1 copy-done.3
  19.9 8.6 %shard_map.94 = (bf16[2,2,64,512]{3,2,1,0:T(8,128)(2,1)}, bf16[128,512]{1,0:T(8,128)(2,1)}, bf16[128,512]{1,0:T(8,128)(2,1)}, bf16[128,512]{1,0:T(8,128)(2,1)}, ...) custom-call(f32[3,256,512]{2,1,0:T(8,128)} %get-tuple-element.29.sto, ...), custom_call_target="tpu_custom_call" | custom-call | tf_op jit(solution)/shard_map/pallas_call | solution.py:51
  28.4 1.5 %collective-permute-start.8 = (bf16[4,256,512]{2,1,0:T(8,128)(2,1)}, bf16[4,256,512]{2,1,0:T(8,128)(2,1)S(1)}, u32[]{:S(2)}, u32[]{:S(2)}) collective-permute-start(bf16[4,256,512]{2,1,0:T(8,128)(2,1)} %get-tuple-element.43), channel_id=1, source_target_pairs={{0,4},{4,0},{8,12},{12,8},{16,20},{20,16},{24,28},{28,24},{1,5},{5... | collective-permute-start | bytes 3145736 | tf_op jit(solution)/shard_map/ppermute | solution.py:23
  29.9 2.5 %collective-permute-done.8.received_ref = bf16[4,256,512]{2,1,0:T(8,128)(2,1)S(1)} collective-permute-done((bf16[4,256,512]{2,1,0:T(8,128)(2,1)}, bf16[4,256,512]{2,1,0:T(8,128)(2,1)S(1)}, u32[]{:S(2)}, u32[]{:S(2)}) %collective-permute-start.8) | collective-permute-done | bytes 1048608 | tf_op jit(solution)/shard_map/ppermute | solution.py:23
  32.4 1.0 %copy-done.1 = bf16[4,256,512]{2,1,0:T(8,128)(2,1)} copy-done((bf16[4,256,512]{2,1,0:T(8,128)(2,1)}, bf16[4,256,512]{2,1,0:T(8,128)(2,1)S(1)}, u32[]{:S(2)}) %copy-start.1) | copy-done | bytes 1048600
  33.4 3.0 %shard_map.96 = (f32[256,512]{1,0:T(8,128)}, bf16[256,512]{1,0:T(8,128)(2,1)}, bf16[256,512]{1,0:T(8,128)(2,1)}, bf16[256,512]{1,0:T(8,128)(2,1)}) custom-call(f32[4,256,512]{2,1,0:T(8,128)} %get-tuple-element.42.keep_ref, bf16[4,256,512]{2,1,0:T(8,128)(2,1)} %copy-done.1), custom_call_target="tpu_custom_call" | custom-call | tf_op jit(solution)/shard_map/pallas_call | solution.py:51
  36.4 3.5 %collective-permute-start.9 = (bf16[256,512]{1,0:T(8,128)(2,1)}, bf16[256,512]{1,0:T(8,128)(2,1)S(1)}, u32[]{:S(2)}, u32[]{:S(2)}) collective-permute-start(bf16[256,512]{1,0:T(8,128)(2,1)} %get-tuple-element.45), channel_id=1, source_target_pairs={{0,8},{4,12},{8,0},{12,4},{16,24},{20,28},{24,16},{28,20},{1,9},{5... | collective-permute-start | bytes 786440 | tf_op jit(solution)/shard_map/ppermute | solution.py:23
  39.9 1.2 %collective-permute-start.10 = (bf16[256,512]{1,0:T(8,128)(2,1)}, bf16[256,512]{1,0:T(8,128)(2,1)S(1)}, u32[]{:S(2)}, u32[]{:S(2)}) collective-permute-start(bf16[256,512]{1,0:T(8,128)(2,1)} %get-tuple-element.46), channel_id=1, source_target_pairs={{0,16},{4,20},{8,24},{12,28},{16,0},{20,4},{24,8},{28,12},{1,17},{... | collective-permute-start | bytes 786440 | tf_op jit(solution)/shard_map/ppermute | solution.py:23
  41.1 0.9 %collective-permute-start.11 = (bf16[256,512]{1,0:T(8,128)(2,1)}, bf16[256,512]{1,0:T(8,128)(2,1)S(1)}, u32[]{:S(2)}, u32[]{:S(2)}) collective-permute-start(bf16[256,512]{1,0:T(8,128)(2,1)} %get-tuple-element.47), channel_id=1, source_target_pairs={{0,24},{4,28},{8,16},{12,20},{16,8},{20,12},{24,0},{28,4},{1,25},{... | collective-permute-start | bytes 786440 | tf_op jit(solution)/shard_map/ppermute | solution.py:23
  42.0 1.3 %collective-permute-start.4 = (bf16[128,512]{1,0:T(8,128)(2,1)S(1)}, bf16[128,512]{1,0:T(8,128)(2,1)S(1)}, u32[]{:S(2)}, u32[]{:S(2)}) collective-permute-start(bf16[128,512]{1,0:T(8,128)(2,1)S(1)} %copy-done.20), channel_id=1, source_target_pairs={{4,0},{8,4},{12,8},{16,12},{20,16},{24,20},{28,24},{5,1},{9,5},{13... | collective-permute-start | bytes 393224 | tf_op jit(solution)/shard_map/ppermute | solution.py:18
  43.3 1.3 %collective-permute-start.5 = (bf16[128,512]{1,0:T(8,128)(2,1)S(1)}, bf16[128,512]{1,0:T(8,128)(2,1)S(1)}, u32[]{:S(2)}, u32[]{:S(2)}) collective-permute-start(bf16[128,512]{1,0:T(8,128)(2,1)S(1)} %copy-done.19), channel_id=1, source_target_pairs={{1,0},{2,1},{3,2},{5,4},{6,5},{7,6},{9,8},{10,9},{11,10},{13,12},{... | collective-permute-start | bytes 393224 | tf_op jit(solution)/shard_map/ppermute | solution.py:18
  44.6 2.7 %collective-permute-done.9.refs_0_ = bf16[256,512]{1,0:T(8,128)(2,1)S(1)} collective-permute-done((bf16[256,512]{1,0:T(8,128)(2,1)}, bf16[256,512]{1,0:T(8,128)(2,1)S(1)}, u32[]{:S(2)}, u32[]{:S(2)}) %collective-permute-start.9) | collective-permute-done | bytes 262176 | tf_op jit(solution)/shard_map/ppermute | solution.py:23
  47.3 1.3 %collective-permute-start.6 = (bf16[128,512]{1,0:T(8,128)(2,1)S(1)}, bf16[128,512]{1,0:T(8,128)(2,1)S(1)}, u32[]{:S(2)}, u32[]{:S(2)}) collective-permute-start(bf16[128,512]{1,0:T(8,128)(2,1)S(1)} %copy-done.18), channel_id=1, source_target_pairs={{0,4},{4,8},{8,12},{12,16},{16,20},{20,24},{24,28},{1,5},{5,9},{9,... | collective-permute-start | bytes 393224 | tf_op jit(solution)/shard_map/ppermute | solution.py:18
  48.6 4.1 %collective-permute-done.10.refs_1_ = bf16[256,512]{1,0:T(8,128)(2,1)S(1)} collective-permute-done((bf16[256,512]{1,0:T(8,128)(2,1)}, bf16[256,512]{1,0:T(8,128)(2,1)S(1)}, u32[]{:S(2)}, u32[]{:S(2)}) %collective-permute-start.10) | collective-permute-done | bytes 262176 | tf_op jit(solution)/shard_map/ppermute | solution.py:23
  52.7 3.4 %collective-permute-start.7 = (bf16[128,512]{1,0:T(8,128)(2,1)S(1)}, bf16[128,512]{1,0:T(8,128)(2,1)S(1)}, u32[]{:S(2)}, u32[]{:S(2)}) collective-permute-start(bf16[128,512]{1,0:T(8,128)(2,1)S(1)} %copy-done.17), channel_id=1, source_target_pairs={{0,1},{1,2},{2,3},{4,5},{5,6},{6,7},{8,9},{9,10},{10,11},{12,13},{... | collective-permute-start | bytes 393224 | tf_op jit(solution)/shard_map/ppermute | solution.py:18
  56.1 0.7 copy-done.6
  56.8 2.0 %shard_map.97 = (f32[64,512]{1,0:T(8,128)}, bf16[64,512]{1,0:T(8,128)(2,1)}, bf16[64,512]{1,0:T(8,128)(2,1)}, bf16[64,512]{1,0:T(8,128)(2,1)}) custom-call(f32[256,512]{1,0:T(8,128)} %get-tuple-element.44.keep_ref, bf16[256,512]{1,0:T(8,128)(2,1)} %copy-done.4, bf16[256,512]{1,0:T(8,128)(2,1)} %copy-done.5, bf16[256,512]{1,0:T(8,128)(2,1)} %copy-done.6), custom_call_target="tpu_custom_call" | custom-call | tf_op jit(solution)/shard_map/pallas_call | solution.py:51
  58.8 1.6 %collective-permute-start.12 = (bf16[64,512]{1,0:T(8,128)(2,1)}, bf16[64,512]{1,0:T(8,128)(2,1)S(1)}, u32[]{:S(2)}, u32[]{:S(2)}) collective-permute-start(bf16[64,512]{1,0:T(8,128)(2,1)} %get-tuple-element.49), channel_id=1, source_target_pairs={{0,1},{1,0},{2,3},{3,2},{4,5},{5,4},{6,7},{7,6},{8,9},{9,8},{10,11... | collective-permute-start | bytes 196616 | tf_op jit(solution)/shard_map/ppermute | solution.py:23
  60.4 0.0 collective-permute-done.4.above_first_ref
  60.4 1.0 %collective-permute-start.13 = (bf16[64,512]{1,0:T(8,128)(2,1)}, bf16[64,512]{1,0:T(8,128)(2,1)S(1)}, u32[]{:S(2)}, u32[]{:S(2)}) collective-permute-start(bf16[64,512]{1,0:T(8,128)(2,1)} %get-tuple-element.50), channel_id=1, source_target_pairs={{0,2},{1,3},{2,0},{3,1},{4,6},{5,7},{6,4},{7,5},{8,10},{9,11},{10,... | collective-permute-start | bytes 196616 | tf_op jit(solution)/shard_map/ppermute | solution.py:23
  61.4 0.0 collective-permute-done.5.above_second_ref
  61.4 1.8 %collective-permute-start.14 = (bf16[64,512]{1,0:T(8,128)(2,1)}, bf16[64,512]{1,0:T(8,128)(2,1)S(1)}, u32[]{:S(2)}, u32[]{:S(2)}) collective-permute-start(bf16[64,512]{1,0:T(8,128)(2,1)} %get-tuple-element.51), channel_id=1, source_target_pairs={{0,3},{1,2},{2,1},{3,0},{4,7},{5,6},{6,5},{7,4},{8,11},{9,10},{10,... | collective-permute-start | bytes 196616 | tf_op jit(solution)/shard_map/ppermute | solution.py:23
  63.3 0.6 copy-done.9
  63.9 0.1 copy-done.10
  63.9 3.5 %shard_map.95 = bf16[2,2,64,512]{3,2,1,0:T(8,128)(2,1)} custom-call(f32[256,512]{1,0:T(8,128)} %get-tuple-element.32.own_ref, f32[256,512]{1,0:T(8,128)} %get-tuple-element.33.enter_ref, f32[128,512]{1,0:T(8,128)} %get-tuple-element.34.slope_top_first_ref, f32[128,512]{1,0:T(8,128)} %get-tuple-element.35.slope_top_second_ref, ...), custom_call_target="tpu_custom_call" | custom-call | tf_op jit(solution)/shard_map/pallas_call | solution.py:51
  67.4 0.0 collective-permute-done.13.refs_1_
  67.4 0.3 collective-permute-done.14.refs_2_
  67.8 0.3 copy-done.13
  68.1 0.0 copy-done.14
  68.1 0.3 copy-done.15
  68.4 1.6 %shard_map.98 = (f32[192,128]{1,0:T(8,128)}, f32[64,128]{1,0:T(8,128)}) custom-call(f32[64,512]{1,0:T(8,128)} %get-tuple-element.48.keep_ref, bf16[64,512]{1,0:T(8,128)(2,1)} %copy-done.13, bf16[64,512]{1,0:T(8,128)(2,1)} %copy-done.14, bf16[64,512]{1,0:T(8,128)(2,1)} %copy-done.15), custom_call_target="tpu_custom_call" | custom-call | tf_op jit(solution)/shard_map/pallas_call | solution.py:51
  (41 shorter events, 0.1 us)
Async XLA Ops:
  0.6 12.8 %copy-start.16 = (s32[3,2,2,64]{3,2,1,0:T(2,128)S(1)}, s32[3,2,2,64]{3,2,1,0:T(2,128)}, u32[]{:S(2)}) copy-start(s32[3,2,2,64]{3,2,1,0:T(2,128)} %param.8) | copy-start | bytes 9220
  0.6 8.6 %copy-start = (bf16[2,2,64,512]{3,2,1,0:T(8,128)(2,1)S(1)}, bf16[2,2,64,512]{3,2,1,0:T(8,128)(2,1)}, u32[]{:S(2)}) copy-start(bf16[2,2,64,512]{3,2,1,0:T(8,128)(2,1)} %node_ref.3) | copy-start | bytes 786436
  3.4 15.6 %collective-permute-start.3 = (bf16[272,512]{1,0:T(8,128)(2,1)S(1)}, bf16[272,512]{1,0:T(8,128)(2,1)S(1)}, u32[]{:S(2)}, u32[]{:S(2)}) collective-permute-start(bf16[272,512]{1,0:T(8,128)(2,1)S(1)} %fusion.3), channel_id=1, source_target_pairs={{0,1},{1,2},{2,3},{4,5},{5,6},{6,7},{8,9},{9,10},{10,11},{12,13},{... | collective-permute-start | bytes 835592 | tf_op jit(solution)/shard_map/ppermute | solution.py:18
  9.3 9.7 %collective-permute-start.2 = (bf16[272,512]{1,0:T(8,128)(2,1)S(1)}, bf16[272,512]{1,0:T(8,128)(2,1)S(1)}, u32[]{:S(2)}, u32[]{:S(2)}) collective-permute-start(bf16[272,512]{1,0:T(8,128)(2,1)S(1)} %fusion.2), channel_id=1, source_target_pairs={{0,4},{4,8},{8,12},{12,16},{16,20},{20,24},{24,28},{1,5},{5,9},{9,... | collective-permute-start | bytes 835592 | tf_op jit(solution)/shard_map/ppermute | solution.py:18
  10.8 7.0 %collective-permute-start = (bf16[128,512]{1,0:T(8,128)(2,1)S(1)}, bf16[128,512]{1,0:T(8,128)(2,1)S(1)}, u32[]{:S(2)}, u32[]{:S(2)}) collective-permute-start(bf16[128,512]{1,0:T(8,128)(2,1)S(1)} %bitcast.18), channel_id=1, source_target_pairs={{4,0},{8,4},{12,8},{16,12},{20,16},{24,20},{28,24},{5,1},{9,5},{13... | collective-permute-start | bytes 393224 | tf_op jit(solution)/shard_map/ppermute | solution.py:18
  12.1 6.9 %collective-permute-start.1 = (bf16[128,512]{1,0:T(8,128)(2,1)S(1)}, bf16[128,512]{1,0:T(8,128)(2,1)S(1)}, u32[]{:S(2)}, u32[]{:S(2)}) collective-permute-start(bf16[128,512]{1,0:T(8,128)(2,1)S(1)} %bitcast.17), channel_id=1, source_target_pairs={{1,0},{2,1},{3,2},{5,4},{6,5},{7,6},{9,8},{10,9},{11,10},{13,12},{... | collective-permute-start | bytes 393224 | tf_op jit(solution)/shard_map/ppermute | solution.py:18
  17.8 1.2 %copy-start.11 = (bf16[128,512]{1,0:T(8,128)(2,1)}, bf16[128,512]{1,0:T(8,128)(2,1)S(1)}, u32[]{:S(2)}) copy-start(bf16[128,512]{1,0:T(8,128)(2,1)S(1)} %collective-permute-done.above_first_ref) | copy-start | bytes 393220
  19.0 0.7 copy-start.12
  19.0 0.8 %copy-start.2 = (bf16[272,512]{1,0:T(8,128)(2,1)}, bf16[272,512]{1,0:T(8,128)(2,1)S(1)}, u32[]{:S(2)}) copy-start(bf16[272,512]{1,0:T(8,128)(2,1)S(1)} %collective-permute-done.3.below_second_ref) | copy-start | bytes 835588
  19.0 0.9 %copy-start.3 = (bf16[272,512]{1,0:T(8,128)(2,1)}, bf16[272,512]{1,0:T(8,128)(2,1)S(1)}, u32[]{:S(2)}) copy-start(bf16[272,512]{1,0:T(8,128)(2,1)S(1)} %collective-permute-done.2.below_first_ref) | copy-start | bytes 835588
  28.4 4.0 %collective-permute-start.8 = (bf16[4,256,512]{2,1,0:T(8,128)(2,1)}, bf16[4,256,512]{2,1,0:T(8,128)(2,1)S(1)}, u32[]{:S(2)}, u32[]{:S(2)}) collective-permute-start(bf16[4,256,512]{2,1,0:T(8,128)(2,1)} %get-tuple-element.43), channel_id=1, source_target_pairs={{0,4},{4,0},{8,12},{12,8},{16,20},{20,16},{24,28},{28,24},{1,5},{5... | collective-permute-start | bytes 3145736 | tf_op jit(solution)/shard_map/ppermute | solution.py:23
  32.4 1.0 %copy-start.1 = (bf16[4,256,512]{2,1,0:T(8,128)(2,1)}, bf16[4,256,512]{2,1,0:T(8,128)(2,1)S(1)}, u32[]{:S(2)}) copy-start(bf16[4,256,512]{2,1,0:T(8,128)(2,1)S(1)} %collective-permute-done.8.received_ref) | copy-start | bytes 3145732
  33.4 8.6 %copy-start.20 = (bf16[128,512]{1,0:T(8,128)(2,1)S(1)}, bf16[128,512]{1,0:T(8,128)(2,1)}, u32[]{:S(2)}) copy-start(bf16[128,512]{1,0:T(8,128)(2,1)} %get-tuple-element.38) | copy-start | bytes 393220
  33.4 9.9 %copy-start.19 = (bf16[128,512]{1,0:T(8,128)(2,1)S(1)}, bf16[128,512]{1,0:T(8,128)(2,1)}, u32[]{:S(2)}) copy-start(bf16[128,512]{1,0:T(8,128)(2,1)} %get-tuple-element.39) | copy-start | bytes 393220
  33.4 13.9 %copy-start.18 = (bf16[128,512]{1,0:T(8,128)(2,1)S(1)}, bf16[128,512]{1,0:T(8,128)(2,1)}, u32[]{:S(2)}) copy-start(bf16[128,512]{1,0:T(8,128)(2,1)} %get-tuple-element.40) | copy-start | bytes 393220
  33.4 19.2 %copy-start.17 = (bf16[128,512]{1,0:T(8,128)(2,1)S(1)}, bf16[128,512]{1,0:T(8,128)(2,1)}, u32[]{:S(2)}) copy-start(bf16[128,512]{1,0:T(8,128)(2,1)} %get-tuple-element.41) | copy-start | bytes 393220
  36.4 10.8 %collective-permute-start.9 = (bf16[256,512]{1,0:T(8,128)(2,1)}, bf16[256,512]{1,0:T(8,128)(2,1)S(1)}, u32[]{:S(2)}, u32[]{:S(2)}) collective-permute-start(bf16[256,512]{1,0:T(8,128)(2,1)} %get-tuple-element.45), channel_id=1, source_target_pairs={{0,8},{4,12},{8,0},{12,4},{16,24},{20,28},{24,16},{28,20},{1,9},{5... | collective-permute-start | bytes 786440 | tf_op jit(solution)/shard_map/ppermute | solution.py:23
  39.9 12.7 %collective-permute-start.10 = (bf16[256,512]{1,0:T(8,128)(2,1)}, bf16[256,512]{1,0:T(8,128)(2,1)S(1)}, u32[]{:S(2)}, u32[]{:S(2)}) collective-permute-start(bf16[256,512]{1,0:T(8,128)(2,1)} %get-tuple-element.46), channel_id=1, source_target_pairs={{0,16},{4,20},{8,24},{12,28},{16,0},{20,4},{24,8},{28,12},{1,17},{... | collective-permute-start | bytes 786440 | tf_op jit(solution)/shard_map/ppermute | solution.py:23
  41.1 15.0 %collective-permute-start.11 = (bf16[256,512]{1,0:T(8,128)(2,1)}, bf16[256,512]{1,0:T(8,128)(2,1)S(1)}, u32[]{:S(2)}, u32[]{:S(2)}) collective-permute-start(bf16[256,512]{1,0:T(8,128)(2,1)} %get-tuple-element.47), channel_id=1, source_target_pairs={{0,24},{4,28},{8,16},{12,20},{16,8},{20,12},{24,0},{28,4},{1,25},{... | collective-permute-start | bytes 786440 | tf_op jit(solution)/shard_map/ppermute | solution.py:23
  42.0 18.4 %collective-permute-start.4 = (bf16[128,512]{1,0:T(8,128)(2,1)S(1)}, bf16[128,512]{1,0:T(8,128)(2,1)S(1)}, u32[]{:S(2)}, u32[]{:S(2)}) collective-permute-start(bf16[128,512]{1,0:T(8,128)(2,1)S(1)} %copy-done.20), channel_id=1, source_target_pairs={{4,0},{8,4},{12,8},{16,12},{20,16},{24,20},{28,24},{5,1},{9,5},{13... | collective-permute-start | bytes 393224 | tf_op jit(solution)/shard_map/ppermute | solution.py:18
  43.3 18.1 %collective-permute-start.5 = (bf16[128,512]{1,0:T(8,128)(2,1)S(1)}, bf16[128,512]{1,0:T(8,128)(2,1)S(1)}, u32[]{:S(2)}, u32[]{:S(2)}) collective-permute-start(bf16[128,512]{1,0:T(8,128)(2,1)S(1)} %copy-done.19), channel_id=1, source_target_pairs={{1,0},{2,1},{3,2},{5,4},{6,5},{7,6},{9,8},{10,9},{11,10},{13,12},{... | collective-permute-start | bytes 393224 | tf_op jit(solution)/shard_map/ppermute | solution.py:18
  47.3 8.8 %copy-start.4 = (bf16[256,512]{1,0:T(8,128)(2,1)}, bf16[256,512]{1,0:T(8,128)(2,1)S(1)}, u32[]{:S(2)}) copy-start(bf16[256,512]{1,0:T(8,128)(2,1)S(1)} %collective-permute-done.9.refs_0_) | copy-start | bytes 786436
  47.3 15.9 %collective-permute-start.6 = (bf16[128,512]{1,0:T(8,128)(2,1)S(1)}, bf16[128,512]{1,0:T(8,128)(2,1)S(1)}, u32[]{:S(2)}, u32[]{:S(2)}) collective-permute-start(bf16[128,512]{1,0:T(8,128)(2,1)S(1)} %copy-done.18), channel_id=1, source_target_pairs={{0,4},{4,8},{8,12},{12,16},{16,20},{20,24},{24,28},{1,5},{5,9},{9,... | collective-permute-start | bytes 393224 | tf_op jit(solution)/shard_map/ppermute | solution.py:18
  52.6 3.5 %copy-start.5 = (bf16[256,512]{1,0:T(8,128)(2,1)}, bf16[256,512]{1,0:T(8,128)(2,1)S(1)}, u32[]{:S(2)}) copy-start(bf16[256,512]{1,0:T(8,128)(2,1)S(1)} %collective-permute-done.10.refs_1_) | copy-start | bytes 786436
  52.7 10.6 %collective-permute-start.7 = (bf16[128,512]{1,0:T(8,128)(2,1)S(1)}, bf16[128,512]{1,0:T(8,128)(2,1)S(1)}, u32[]{:S(2)}, u32[]{:S(2)}) collective-permute-start(bf16[128,512]{1,0:T(8,128)(2,1)S(1)} %copy-done.17), channel_id=1, source_target_pairs={{0,1},{1,2},{2,3},{4,5},{5,6},{6,7},{8,9},{9,10},{10,11},{12,13},{... | collective-permute-start | bytes 393224 | tf_op jit(solution)/shard_map/ppermute | solution.py:18
  56.1 0.7 copy-start.6
  58.8 8.6 %collective-permute-start.12 = (bf16[64,512]{1,0:T(8,128)(2,1)}, bf16[64,512]{1,0:T(8,128)(2,1)S(1)}, u32[]{:S(2)}, u32[]{:S(2)}) collective-permute-start(bf16[64,512]{1,0:T(8,128)(2,1)} %get-tuple-element.49), channel_id=1, source_target_pairs={{0,1},{1,0},{2,3},{3,2},{4,5},{5,4},{6,7},{7,6},{8,9},{9,8},{10,11... | collective-permute-start | bytes 196616 | tf_op jit(solution)/shard_map/ppermute | solution.py:23
  60.4 2.8 %copy-start.7 = (bf16[128,512]{1,0:T(8,128)(2,1)}, bf16[128,512]{1,0:T(8,128)(2,1)S(1)}, u32[]{:S(2)}) copy-start(bf16[128,512]{1,0:T(8,128)(2,1)S(1)} %collective-permute-done.4.above_first_ref) | copy-start | bytes 393220
  60.4 7.0 %collective-permute-start.13 = (bf16[64,512]{1,0:T(8,128)(2,1)}, bf16[64,512]{1,0:T(8,128)(2,1)S(1)}, u32[]{:S(2)}, u32[]{:S(2)}) collective-permute-start(bf16[64,512]{1,0:T(8,128)(2,1)} %get-tuple-element.50), channel_id=1, source_target_pairs={{0,2},{1,3},{2,0},{3,1},{4,6},{5,7},{6,4},{7,5},{8,10},{9,11},{10,... | collective-permute-start | bytes 196616 | tf_op jit(solution)/shard_map/ppermute | solution.py:23
  61.4 1.8 %copy-start.8 = (bf16[128,512]{1,0:T(8,128)(2,1)}, bf16[128,512]{1,0:T(8,128)(2,1)S(1)}, u32[]{:S(2)}) copy-start(bf16[128,512]{1,0:T(8,128)(2,1)S(1)} %collective-permute-done.5.above_second_ref) | copy-start | bytes 393220
  61.4 6.4 %collective-permute-start.14 = (bf16[64,512]{1,0:T(8,128)(2,1)}, bf16[64,512]{1,0:T(8,128)(2,1)S(1)}, u32[]{:S(2)}, u32[]{:S(2)}) collective-permute-start(bf16[64,512]{1,0:T(8,128)(2,1)} %get-tuple-element.51), channel_id=1, source_target_pairs={{0,3},{1,2},{2,1},{3,0},{4,7},{5,6},{6,5},{7,4},{8,11},{9,10},{10,... | collective-permute-start | bytes 196616 | tf_op jit(solution)/shard_map/ppermute | solution.py:23
  63.2 0.7 copy-start.9
  63.2 0.7 %copy-start.10 = (bf16[128,512]{1,0:T(8,128)(2,1)}, bf16[128,512]{1,0:T(8,128)(2,1)S(1)}, u32[]{:S(2)}) copy-start(bf16[128,512]{1,0:T(8,128)(2,1)S(1)} %collective-permute-done.7.below_second_ref) | copy-start | bytes 393220
  67.4 0.6 copy-start.13
  67.4 0.6 copy-start.14
  67.8 0.6 copy-start.15

commit v2 on v1

--- a/solution.py
+++ b/solution.py
@@ -12,10 +12,10 @@
 PAD = 16
 
 
-def passed_along(value, axis, steps):
+def swapped(value, axis, first):
     count = lax.axis_size(axis)
-    first, last = (max(0, -steps), min(count, count - steps))
-    return lax.ppermute(value, axis, [(source, source + steps) for source in range(first, last)])
+    lower = range(first, count - 1, 2)
+    return lax.ppermute(value, axis, [(at, at + 1) for at in lower] + [(at + 1, at) for at in lower])
 
 
 def exchanged(value, axis, flip):
@@ -47,7 +47,7 @@
     return 0.5 * jnp.tanh(0.5 * values) + 0.5
 
 
-def call(kernel, outs, args, scratch=(), limit=60 << 20, cost=None):
+def call(kernel, outs, args, scratch=(), limit=4 << 20, cost=None):
     return pl.pallas_call(
         kernel,
         out_shape=[jax.ShapeDtypeStruct(shape, dtype) for shape, dtype in outs],
@@ -59,6 +59,48 @@
     )(*args)
 
 
+def spread_rows(rows, count):
+    down = lax.broadcasted_iota(jnp.int32, (count, rows[0].shape[-1]), 0)
+    tile = jnp.zeros((count, rows[0].shape[-1]), F32)
+    for index, row in enumerate(rows):
+        tile = jnp.where(down == index, row, tile)
+    return tile
+
+
+def is_even(axis):
+    return lax.axis_index(axis) % 2 == 0
+
+
+def pack_kernel(dims, node_ref, edge_ref, open_ref, pair_first_ref, odd_first_ref, pair_second_ref, odd_second_ref):
+    ex, ey, nz, features = dims
+
+    def fill_upward(ref, direction, cells):
+        for index, (x, y) in enumerate(cells):
+            ref[index * nz : (index + 1) * nz] = node_ref[x, y]
+            start = (len(cells) + index) * nz
+            ref[start : start + nz] = edge_ref[direction, x, y]
+        mask = spread_rows([open_ref[direction, x, y : y + 1].astype(F32) for x, y in cells], PAD)
+        ref[2 * len(cells) * nz :, :nz] = mask.astype(BF16)
+
+    def fill_downward(ref, cells):
+        for index, (x, y) in enumerate(cells):
+            ref[index * nz : (index + 1) * nz] = node_ref[x, y]
+
+    for direction, axis, pair_ref, odd_ref, top, low in (
+        (1, "gy", pair_second_ref, odd_second_ref, [(x, ey - 1) for x in range(ex)], [(x, 0) for x in range(ex)]),
+        (0, "gx", pair_first_ref, odd_first_ref, [(ex - 1, y) for y in range(ey)], [(0, y) for y in range(ey)]),
+    ):
+        @pl.when(is_even(axis))
+        def _():
+            fill_upward(pair_ref, direction, top)
+            fill_downward(odd_ref, low)
+
+        @pl.when(jnp.logical_not(is_even(axis)))
+        def _():
+            fill_downward(pair_ref, low)
+            fill_upward(odd_ref, direction, top)
+
+
 def products_kernel(node_ref, edge_ref, weight_ref, stored_ref, other_ref):
     features = node_ref.shape[-1]
     node = node_ref[...].reshape(-1, features)
@@ -72,10 +114,10 @@
 def layer_kernel(
     dims,
     stored_ref, other_ref, weight_ref, node_weight_ref, node_ref, edge_ref, open_ref, cotangent_ref,
-    above_first_ref, above_second_ref, below_first_ref, below_second_ref,
-    new_ref, low_first_ref, low_second_ref, top_first_ref, top_second_ref,
+    pair_first_ref, odd_first_ref, pair_second_ref, odd_second_ref,
+    new_ref, grad_odd_first_ref, grad_pair_second_ref, grad_odd_second_ref,
     own_ref, enter_ref, slope_top_first_ref, slope_top_second_ref, slope_low_first_ref, slope_low_second_ref,
-    send_ref, keep_ref,
+    grad_pair_first_ref, send_ref, keep_ref,
     summed_ref, update_ref, slope_ref, slope_low_ref, message_ref, message_low_ref,
     grads_ref, total_ref,
 ):
@@ -100,19 +142,25 @@
         return message, opened * (1.0 + preact * (1.0 - gate))
 
     edge_rows_first, edge_rows_second = ey * nz, ex * nz
-    above_first = dot(above_first_ref[...], other_weight)
-    above_second = dot(above_second_ref[...], other_weight)
-    node_below_first = below_first_ref[:edge_rows_first]
-    edge_below_first = below_first_ref[edge_rows_first : 2 * edge_rows_first]
-    node_below_second = below_second_ref[:edge_rows_second]
-    edge_below_second = below_second_ref[edge_rows_second : 2 * edge_rows_second]
+    even_first, even_second = is_even("gx"), is_even("gy")
+
+    def chosen(even, pair_ref, odd_ref, start, stop):
+        return jnp.where(even, odd_ref[start:stop], pair_ref[start:stop])
+
+    node_above_first = chosen(even_first, odd_first_ref, pair_first_ref, 0, edge_rows_first)
+    node_above_second = chosen(even_second, odd_second_ref, pair_second_ref, 0, edge_rows_second)
+    node_below_first = chosen(even_first, pair_first_ref, odd_first_ref, 0, edge_rows_first)
+    edge_below_first = chosen(even_first, pair_first_ref, odd_first_ref, edge_rows_first, 2 * edge_rows_first)
+    node_below_second = chosen(even_second, pair_second_ref, odd_second_ref, 0, edge_rows_second)
+    edge_below_second = chosen(even_second, pair_second_ref, odd_second_ref, edge_rows_second, 2 * edge_rows_second)
+    above_first = dot(node_above_first, other_weight)
+    above_second = dot(node_above_second, other_weight)
     low_first = dot(node_below_first, self_weight) + dot(edge_below_first, stored_weight)
     low_second = dot(node_below_second, self_weight) + dot(edge_below_second, stored_weight)
-    mask_first = below_first_ref[2 * edge_rows_first :].astype(F32)
-    mask_second = below_second_ref[2 * edge_rows_second :].astype(F32)
+    mask_first = chosen(even_first, pair_first_ref, odd_first_ref, 2 * edge_rows_first, 2 * edge_rows_first + PAD).astype(F32)
+    mask_second = chosen(even_second, pair_second_ref, odd_second_ref, 2 * edge_rows_second, 2 * edge_rows_second + PAD).astype(F32)
     down = lax.broadcasted_iota(jnp.int32, (nz, 1), 0)
     inside_third = jnp.where(down < nz - 1, 1.0, 0.0)
-    opened = open_ref[...].astype(F32)
 
     for y in range(ey):
         message, slope = edge_terms(low_first[part(y)] + other_ref[rows(0, y)], column_of(mask_first[y : y + 1, :nz]))
@@ -127,7 +175,7 @@
         for y in range(ey):
             here = rows(x, y)
             column = [
-                column_of(opened[(direction * ex + x) * ey + y : (direction * ex + x) * ey + y + 1]) for direction in range(3)
+                column_of(open_ref[direction, x, y : y + 1].astype(F32)) for direction in range(3)
             ]
             if x + 1 < ex:
                 beyond = other_ref[rows(x + 1, y)]
@@ -157,12 +205,15 @@
     cotangent = cotangent_ref[...].reshape(-1, features).astype(F32)
     update_ref[...] = (cotangent * (gate * (1.0 + update * (1.0 - gate)))).astype(BF16)
     grad_summed = dot_nt(update_ref[...], node_weight_ref[...]).astype(BF16)
+    extra = 0 if send_ref is None else send_ref.shape[0] - edge_rows_first
     for y in range(ey):
-        low_first_ref[part(y)] = grad_summed[rows(0, y)]
-        top_first_ref[part(y)] = grad_summed[rows(ex - 1, y)]
-    for x in range(ex):
-        low_second_ref[part(x)] = grad_summed[rows(x, 0)]
-        top_second_ref[part(x)] = grad_summed[rows(x, ey - 1)]
+        low, top = grad_summed[rows(0, y)], grad_summed[rows(ex - 1, y)]
+        (grad_pair_first_ref if send_ref is None else send_ref)[extra + y * nz : extra + (y + 1) * nz] = jnp.where(even_first, top, low)
+        grad_odd_first_ref[part(y)] = jnp.where(even_first, low, top)
+    for x in range(ex):
+        low, top = grad_summed[rows(x, 0)], grad_summed[rows(x, ey - 1)]
+        grad_pair_second_ref[part(x)] = jnp.where(even_second, top, low)
+        grad_odd_second_ref[part(x)] = jnp.where(even_second, low, top)
     wide = grad_summed.astype(F32)
 
     count = ex * ey * nz
@@ -214,7 +265,7 @@
     tops = [grads_ref[(x * ey + y) * nz : (x * ey + y + 1) * nz] for x in [ex - 1] for y in range(ey)]
     tops += [grads_ref[count + (x * ey + y) * nz : count + (x * ey + y + 1) * nz] for x in range(ex) for y in [ey - 1]]
     total_ref[features : 2 * features] = dot_tn(
-        jnp.concatenate([node, above_first_ref[...], above_second_ref[...]], axis=0),
+        jnp.concatenate([node, node_above_first, node_above_second], axis=0),
         jnp.concatenate([enter_ref[...].astype(BF16), *tops], axis=0),
     )
     edges = edge_ref[...].reshape(-1, features)
@@ -226,26 +277,34 @@
     if send_ref is None:
         keep_ref[...] = total_ref[...]
         return
-    planes, seconds, chunk = send_ref.shape[0], lax.axis_size("gy"), send_ref.shape[1] // lax.axis_size("gy")
+    planes = keep_ref.shape[0]
+    seconds, chunk = lax.axis_size("gy"), keep_ref.shape[1] // lax.axis_size("gy")
     edge_rows, node_rows = chunk * 3 // 4, chunk // 4
     core, plane = at_first % 2, at_first // 2
     for block in range(planes):
         for second in range(seconds):
             there = (plane ^ block) * 2
-            for target, flip in ((keep_ref, core), (send_ref, 1 - core)):
+            start = second * chunk
+            for flip in (core, 1 - core):
                 device = (there + flip) * seconds + (at_second ^ second)
-                edge_at = pl.multiple_of(device * edge_rows, 8)
-                node_at = pl.multiple_of(3 * features + device * node_rows, 8)
-                start = second * chunk
-                target[block, start : start + edge_rows] = total_ref[pl.ds(edge_at, edge_rows)].astype(target.dtype)
-                target[block, start + edge_rows : start + chunk] = total_ref[pl.ds(node_at, node_rows)].astype(target.dtype)
+                edge = total_ref[pl.ds(pl.multiple_of(device * edge_rows, 8), edge_rows)]
+                node = total_ref[pl.ds(pl.multiple_of(3 * features + device * node_rows, 8), node_rows)]
+                if flip is core:
+                    keep_ref[block, start : start + edge_rows] = edge
+                    keep_ref[block, start + edge_rows : start + chunk] = node
+                else:
+                    send_at = block * seconds * chunk + start
+                    send_ref[send_at : send_at + edge_rows] = edge.astype(BF16)
+                    send_ref[send_at + edge_rows : send_at + chunk] = node.astype(BF16)
 
 
 def node_grad_kernel(
     dims, own_ref, enter_ref, slope_top_first_ref, slope_top_second_ref, slope_low_first_ref, slope_low_second_ref,
-    above_first_ref, above_second_ref, below_first_ref, below_second_ref, cotangent_ref, weight_ref, out_ref,
+    pair_first_ref, odd_first_ref, pair_second_ref, odd_second_ref, cotangent_ref, weight_ref, out_ref,
 ):
     ex, ey, nz, features = dims
+    even_first, even_second = is_even("gx"), is_even("gy")
+    extra = pair_first_ref.shape[0] - ey * nz
 
     def rows(x, y):
         return slice((x * ey + y) * nz, (x * ey + y + 1) * nz)
@@ -257,16 +316,19 @@
     for x in range(ex):
         for y in range(ey):
             grad = own_ref[rows(x, y)]
+            pair_first = pair_first_ref[extra + y * nz : extra + (y + 1) * nz].astype(F32)
+            odd_first = odd_first_ref[part(y)].astype(F32)
+            pair_second, odd_second = pair_second_ref[part(x)].astype(F32), odd_second_ref[part(x)].astype(F32)
             if x == ex - 1:
-                grad = grad - above_first_ref[part(y)].astype(F32) * slope_top_first_ref[part(y)]
+                grad = grad - jnp.where(even_first, pair_first, odd_first) * slope_top_first_ref[part(y)]
             if y == ey - 1:
-                grad = grad - above_second_ref[part(x)].astype(F32) * slope_top_second_ref[part(x)]
+                grad = grad - jnp.where(even_second, pair_second, odd_second) * slope_top_second_ref[part(x)]
             own.append(grad.astype(BF16))
             grad = enter_ref[rows(x, y)]
             if x == 0:
-                grad = grad + below_first_ref[part(y)].astype(F32) * slope_low_first_ref[part(y)]
+                grad = grad + jnp.where(even_first, odd_first, pair_first) * slope_low_first_ref[part(y)]
             if y == 0:
-                grad = grad + below_second_ref[part(x)].astype(F32) * slope_low_second_ref[part(x)]
+                grad = grad + jnp.where(even_second, odd_second, pair_second) * slope_low_second_ref[part(x)]
             enter.append(grad.astype(BF16))
     result = dot_nt(jnp.concatenate(own, axis=0), weight_ref[:features])
     result = result + dot_nt(jnp.concatenate(enter, axis=0), weight_ref[features : 2 * features])
@@ -275,9 +337,10 @@
 
 
 def pair_sum_kernel(keep_ref, received_ref, kept_ref, *send_refs):
-    kept_ref[...] = keep_ref[0] + received_ref[0].astype(F32)
-    for index, send_ref in enumerate(send_refs):
-        send_ref[...] = (keep_ref[index + 1] + received_ref[index + 1].astype(F32)).astype(BF16)
+    rows = kept_ref.shape[0]
+    kept_ref[...] = keep_ref[0] + received_ref[:rows].astype(F32)
+    for index, send_ref in enumerate(send_refs, 1):
+        send_ref[...] = (keep_ref[index] + received_ref[index * rows : (index + 1) * rows].astype(F32)).astype(BF16)
 
 
 def plane_sum_kernel(groups, keep_ref, *refs):
@@ -314,14 +377,15 @@
     devices = firsts * seconds
     count = ex * ey * nz
 
-    def upward(nodes, edges, mask):
-        mask = jnp.pad(mask.astype(BF16), ((0, PAD - mask.shape[0]), (0, features - mask.shape[1])))
-        return jnp.concatenate([nodes.reshape(-1, features), edges.reshape(-1, features), mask], axis=0)
-
-    above_first = passed_along(node_features[0].reshape(-1, features), "gx", -1)
-    above_second = passed_along(node_features[:, 0].reshape(-1, features), "gy", -1)
-    below_first = passed_along(upward(node_features[-1], edge_features[0, -1], open_faces[0, -1]), "gx", 1)
-    below_second = passed_along(upward(node_features[:, -1], edge_features[1, :, -1], open_faces[1, :, -1]), "gy", 1)
+    face_first, face_second = (ey * nz, features), (ex * nz, features)
+    packed_first, packed_second = (2 * ey * nz + PAD, features), (2 * ex * nz + PAD, features)
+    pair_first, odd_first, pair_second, odd_second = call(
+        functools.partial(pack_kernel, dims),
+        [(packed_first, BF16)] * 2 + [(packed_second, BF16)] * 2,
+        [node_features, edge_features, open_faces],
+    )
+    pair_second, odd_second = swapped(pair_second, "gy", 0), swapped(odd_second, "gy", 1)
+    odd_first, pair_first = swapped(odd_first, "gx", 1), swapped(pair_first, "gx", 0)
 
     stored, other = call(
         products_kernel, [((3, count, features), F32), ((count, features), F32)], [node_features, edge_features, edge_weight]
@@ -337,14 +401,16 @@
         and seconds & (seconds - 1) == 0
     )
     planes = firsts // 2
-    face_first, face_second = (ey * nz, features), (ex * nz, features)
-    outs = [(node_features.shape, BF16), (face_first, BF16), (face_second, BF16), (face_first, BF16), (face_second, BF16)]
+    outs = [(node_features.shape, BF16), (face_first, BF16), (face_second, BF16), (face_second, BF16)]
     outs += [((count, features), F32)] * 2 + [(face_first, F32), (face_second, F32)] * 2
     if by_hand:
-        outs += [((planes, seconds * chunk, features), BF16), ((planes, seconds * chunk, features), F32)]
-        kernel = functools.partial(layer_kernel, dims)
+        outs += [((planes * seconds * chunk + ey * nz, features), BF16), ((planes, seconds * chunk, features), F32)]
+
+        def kernel(*refs):
+            layer_kernel(dims, *refs[:22], None, *refs[22:])
+
     else:
-        outs += [((total_rows, features), F32)]
+        outs += [(face_first, BF16), ((total_rows, features), F32)]
 
         def kernel(*refs):
             layer_kernel(dims, *refs[:23], None, *refs[23:])
@@ -354,9 +420,10 @@
         kernel,
         outs,
         [
-            stored, other, edge_weight, node_weight, node_features, edge_features, open_faces.reshape(3 * ex * ey, nz), cotangent,
-            above_first, above_second, below_first, below_second,
+            stored, other, edge_weight, node_weight, node_features, edge_features, open_faces, cotangent,
+            pair_first, odd_first, pair_second, odd_second,
         ],
+        limit=16 << 20,
         scratch=[
             pltpu.VMEM((count, features), BF16),
             pltpu.VMEM((count, features), BF16),
@@ -368,22 +435,18 @@
             pltpu.VMEM((total_rows, features), F32),
         ],
     )
-    new_nodes, low_first, low_second, top_first, top_second = results[:5]
-
-    if by_hand:
-        send, keep = results[11:]
-        received = exchanged(send, "gx", 1)
-    grad_above_first = passed_along(low_first, "gx", -1)
-    grad_above_second = passed_along(low_second, "gy", -1)
-    grad_below_first = passed_along(top_first, "gx", 1)
-    grad_below_second = passed_along(top_second, "gy", 1)
+    new_nodes, odd_first, pair_second, odd_second = results[:4]
+    received = swapped(results[10], "gx", 0)
+    keep = results[11]
+    odd_first = swapped(odd_first, "gx", 1)
+    pair_second, odd_second = swapped(pair_second, "gy", 0), swapped(odd_second, "gy", 1)
     (node_grad,) = call(
         functools.partial(node_grad_kernel, dims),
         [(node_features.shape, BF16)],
-        [*results[5:11], grad_above_first, grad_above_second, grad_below_first, grad_below_second, cotangent, edge_weight],
+        [*results[4:10], received, odd_first, pair_second, odd_second, cotangent, edge_weight],
     )
     if not by_hand:
-        total = results[11]
+        total = keep
         edge_part = lax.psum_scatter(total[: 3 * features].reshape(-1), ("gx", "gy"), scatter_dimension=0, tiled=True)
         node_part = lax.psum_scatter(total[3 * features :].reshape(-1), ("gx", "gy"), scatter_dimension=0, tiled=True)
         return new_nodes, node_grad, edge_part, node_part

time: 70.5 us -> 53.5 us (0.76)
  Pallas kernels: 22.4 us -> 7.79 us
  waiting for transfers between devices: 10.8 us -> 14.1 us
  local copies, waits for them, and re-layouts: 7.34 us -> 4.19 us
  starting transfers between devices: 27.8 us -> 26.2 us
  other arithmetic: 0.79 us -> 0 us
    pallas_call x6 -> x7, Pallas kernels: 22.4 us -> 7.79 us  [call(): pl.pallas_call(kernel, out_shape=[jax.ShapeDtypeStruct(shape, dtype) for...]
    ppermute x8, waiting for transfers between devices: 1.21 us -> 4.72 us  [swapped(): lax.ppermute(value, axis, [(at, at + 1) for at in lower] + [(at + 1, at)...]
    ppermute x8, starting transfers between devices: 16.3 us -> 12.9 us  [swapped(): lax.ppermute(value, axis, [(at, at + 1) for at in lower] + [(at + 1, at)...]
    slice x5 -> x0, local copies, waits for them, and re-layouts: 2.86 us -> none  [the longest x1 0.99 us: local(): node_features[:, -1]]
    ppermute x7 -> x6, starting transfers between devices: 11.4 us -> 13.3 us  [exchanged(): lax.ppermute(value, axis, [(source, source ^ flip) for source in range(co...]
    another operation x1 -> x0, other arithmetic: 0.75 us -> none
    unnamed x43 -> x20, local copies, waits for them, and re-layouts: 3.87 us -> 4.19 us
    ppermute x7 -> x6, waiting for transfers between devices: 9.61 us -> 9.41 us  [exchanged(): lax.ppermute(value, axis, [(source, source ^ flip) for source in range(co...]
  transfers between devices with their start and end apart: 15 -> 14, of which waited for: 5 -> 6; matrix products, arithmetic and copies ran while one was open for 2% -> 0% of each run, Pallas kernels for 13% -> 4%
where the time goes in v2:
time: 53.5 us; the launch traced here: 53.1 us
  starting transfers between devices  26.2 us (49%)
  waiting for transfers between devices  14.1 us (26%)
  Pallas kernels  7.79 us (15%)
  local copies, waits for them, and re-layouts  4.19 us (8%)
  between operations  0.78 us (1%)
    ppermute x6, starting transfers between devices, exchanged(): lax.ppermute(value, axis, [(source, source ^ flip) for source in range(co...  13.3 us
    ppermute x8, starting transfers between devices, swapped(): lax.ppermute(value, axis, [(at, at + 1) for at in lower] + [(at + 1, at)...  12.9 us
    ppermute x6, waiting for transfers between devices, exchanged(): lax.ppermute(value, axis, [(source, source ^ flip) for source in range(co...  9.41 us
    pallas_call x7, Pallas kernels, call(): pl.pallas_call(kernel, out_shape=[jax.ShapeDtypeStruct(shape, dtype) for...  7.79 us
    ppermute x8, waiting for transfers between devices, swapped(): lax.ppermute(value, axis, [(at, at + 1) for at in lower] + [(at + 1, at)...  4.72 us
    unnamed x20, local copies, waits for them, and re-layouts  4.19 us
  transfers between devices with their start and end apart: 14, of which 6 were waited for; matrix products, arithmetic and copies ran while one was open for 0% of the time, Pallas kernels for 4%

profile of v2, /device:TPU:0, one launch (start us, length us, event | category | flops | bytes accessed | tf_op | source)
XLA Modules:
  0.0 53.1 jit_solution(12327286135186534628)
XLA Ops:
  0.6 0.0 copy-start.2
  0.6 1.1 %copy-done.2 = bf16[3,2,2,64,512]{4,3,2,1,0:T(8,128)(2,1)S(1)} copy-done((bf16[3,2,2,64,512]{4,3,2,1,0:T(8,128)(2,1)S(1)}, bf16[3,2,2,64,512]{4,3,2,1,0:T(8,128)(2,1)}, u32[]{:S(2)}) %copy-start.2) | copy-done | bytes 786456
  1.8 0.9 %copy-done.4 = bf16[2,2,64,512]{3,2,1,0:T(8,128)(2,1)S(1)} copy-done((bf16[2,2,64,512]{3,2,1,0:T(8,128)(2,1)S(1)}, bf16[2,2,64,512]{3,2,1,0:T(8,128)(2,1)}, u32[]{:S(2)}) %copy-start.4) | copy-done | bytes 262168
  2.7 0.7 %copy-done.8 = s32[3,2,2,64]{3,2,1,0:T(2,128)S(1)} copy-done((s32[3,2,2,64]{3,2,1,0:T(2,128)S(1)}, s32[3,2,2,64]{3,2,1,0:T(2,128)}, u32[]{:S(2)}) %copy-start.8) | copy-done | bytes 3096
  3.4 0.1 shard_map.94
  3.5 0.0 copy-start.9
  3.5 0.6 %collective-permute-start = (bf16[272,512]{1,0:T(8,128)(2,1)S(1)}, bf16[272,512]{1,0:T(8,128)(2,1)S(1)}, u32[]{:S(2)}, u32[]{:S(2)}) collective-permute-start(bf16[272,512]{1,0:T(8,128)(2,1)S(1)} %get-tuple-element.34), channel_id=1, source_target_pairs={{0,4},{8,12},{16,20},{24,28},{4,0},{12,8},{20,16},{28,24},{1,5},{9... | collective-permute-start | bytes 835592 | tf_op jit(solution)/shard_map/ppermute | solution.py:18
  4.1 0.7 %collective-permute-start.1 = (bf16[272,512]{1,0:T(8,128)(2,1)S(1)}, bf16[272,512]{1,0:T(8,128)(2,1)S(1)}, u32[]{:S(2)}, u32[]{:S(2)}) collective-permute-start(bf16[272,512]{1,0:T(8,128)(2,1)S(1)} %get-tuple-element.35), channel_id=1, source_target_pairs={{4,8},{12,16},{20,24},{8,4},{16,12},{24,20},{5,9},{13,17},{21,25},... | collective-permute-start | bytes 835592 | tf_op jit(solution)/shard_map/ppermute | solution.py:18
  4.7 2.8 %collective-permute-start.2 = (bf16[272,512]{1,0:T(8,128)(2,1)S(1)}, bf16[272,512]{1,0:T(8,128)(2,1)S(1)}, u32[]{:S(2)}, u32[]{:S(2)}) collective-permute-start(bf16[272,512]{1,0:T(8,128)(2,1)S(1)} %get-tuple-element.36), channel_id=1, source_target_pairs={{0,1},{2,3},{1,0},{3,2},{4,5},{6,7},{5,4},{7,6},{8,9},{10,11},{9,8... | collective-permute-start | bytes 835592 | tf_op jit(solution)/shard_map/ppermute | solution.py:18
  7.5 0.7 %collective-permute-start.3 = (bf16[272,512]{1,0:T(8,128)(2,1)S(1)}, bf16[272,512]{1,0:T(8,128)(2,1)S(1)}, u32[]{:S(2)}, u32[]{:S(2)}) collective-permute-start(bf16[272,512]{1,0:T(8,128)(2,1)S(1)} %get-tuple-element.37), channel_id=1, source_target_pairs={{1,2},{2,1},{5,6},{6,5},{9,10},{10,9},{13,14},{14,13},{17,18},{18,... | collective-permute-start | bytes 835592 | tf_op jit(solution)/shard_map/ppermute | solution.py:18
  8.2 0.0 copy-start
  8.2 1.4 %copy-done = bf16[1536,512]{1,0:T(8,128)(2,1)S(1)} copy-done((bf16[1536,512]{1,0:T(8,128)(2,1)S(1)}, bf16[1536,512]{1,0:T(8,128)(2,1)}, u32[]{:S(2)}) %copy-start) | copy-done | bytes 1572888
  9.6 0.8 %shard_map.93 = (f32[3,256,512]{2,1,0:T(8,128)S(1)}, f32[256,512]{1,0:T(8,128)S(1)}) custom-call(bf16[2,2,64,512]{3,2,1,0:T(8,128)(2,1)S(1)} %copy-done.4, bf16[3,2,2,64,512]{4,3,2,1,0:T(8,128)(2,1)S(1)} %copy-done.2, bf16[1536,512]{1,0:T(8,128)(2,1)S(1)} %copy-done), custom_call_target="tpu_custom_call" | custom-call | tf_op jit(solution)/shard_map/pallas_call | solution.py:51
  10.5 0.0 collective-permute-done.refs_8_
  10.5 0.0 collective-permute-done.1.refs_9_
  10.5 2.2 %collective-permute-done.2.refs_10_ = bf16[272,512]{1,0:T(8,128)(2,1)S(1)} collective-permute-done((bf16[272,512]{1,0:T(8,128)(2,1)S(1)}, bf16[272,512]{1,0:T(8,128)(2,1)S(1)}, u32[]{:S(2)}, u32[]{:S(2)}) %collective-permute-start.2) | collective-permute-done | bytes 278560 | tf_op jit(solution)/shard_map/ppermute | solution.py:18
  12.7 0.0 collective-permute-done.3.refs_11_
  12.7 0.0 copy-done.3
  12.7 0.0 copy-done.5
  12.7 0.0 copy-done.9
  12.7 0.0 copy-done.1
  12.7 0.0 copy-done.6
  12.8 0.0 copy-done.7
  12.8 4.7 %shard_map.95 = (bf16[2,2,64,512]{3,2,1,0:T(8,128)(2,1)}, bf16[128,512]{1,0:T(8,128)(2,1)S(1)}, bf16[128,512]{1,0:T(8,128)(2,1)S(1)}, bf16[128,512]{1,0:T(8,128)...) custom-call(f32[3,256,512]{2,1,0:T(8,128)S(1)} %get-tuple-element.32, ...), custom_call_target="tpu_custom_call" | custom-call | tf_op jit(solution)/shard_map/pallas_call | solution.py:51
  17.4 2.3 %collective-permute-start.4 = (bf16[1152,512]{1,0:T(8,128)(2,1)S(1)}, bf16[1152,512]{1,0:T(8,128)(2,1)S(1)}, u32[]{:S(2)}, u32[]{:S(2)}) collective-permute-start(bf16[1152,512]{1,0:T(8,128)(2,1)S(1)} %get-tuple-element.45), channel_id=1, source_target_pairs={{0,4},{8,12},{16,20},{24,28},{4,0},{12,8},{20,16},{28,24},{1,5},{9... | collective-permute-start | bytes 3538952 | tf_op jit(solution)/shard_map/ppermute | solution.py:18
  19.7 2.5 %collective-permute-done.4.pair_first_ref.received_ref = bf16[1152,512]{1,0:T(8,128)(2,1)S(1)} collective-permute-done((bf16[1152,512]{1,0:T(8,128)(2,1)S(1)}, bf16[1152,512]{1,0:T(8,128)(2,1)S(1)}, u32[]{:S(2)}, u32[]{:S(2)}) %collective-permute-start.4) | collective-permute-done | bytes 1179680 | tf_op jit(solution)/shard_map/ppermute | solution.py:18
  22.2 0.2 shard_map.97
  22.4 3.4 %collective-permute-start.8 = (bf16[256,512]{1,0:T(8,128)(2,1)S(1)}, bf16[256,512]{1,0:T(8,128)(2,1)S(1)}, u32[]{:S(2)}, u32[]{:S(2)}) collective-permute-start(bf16[256,512]{1,0:T(8,128)(2,1)S(1)} %get-tuple-element.51), channel_id=1, source_target_pairs={{0,8},{4,12},{8,0},{12,4},{16,24},{20,28},{24,16},{28,20},{1,9},{5... | collective-permute-start | bytes 786440 | tf_op jit(solution)/shard_map/ppermute | solution.py:23
  25.8 1.0 %collective-permute-start.9 = (bf16[256,512]{1,0:T(8,128)(2,1)S(1)}, bf16[256,512]{1,0:T(8,128)(2,1)S(1)}, u32[]{:S(2)}, u32[]{:S(2)}) collective-permute-start(bf16[256,512]{1,0:T(8,128)(2,1)S(1)} %get-tuple-element.52), channel_id=1, source_target_pairs={{0,16},{4,20},{8,24},{12,28},{16,0},{20,4},{24,8},{28,12},{1,17},{... | collective-permute-start | bytes 786440 | tf_op jit(solution)/shard_map/ppermute | solution.py:23
  26.8 1.4 %collective-permute-start.10 = (bf16[256,512]{1,0:T(8,128)(2,1)S(1)}, bf16[256,512]{1,0:T(8,128)(2,1)S(1)}, u32[]{:S(2)}, u32[]{:S(2)}) collective-permute-start(bf16[256,512]{1,0:T(8,128)(2,1)S(1)} %get-tuple-element.53), channel_id=1, source_target_pairs={{0,24},{4,28},{8,16},{12,20},{16,8},{20,12},{24,0},{28,4},{1,25},{... | collective-permute-start | bytes 786440 | tf_op jit(solution)/shard_map/ppermute | solution.py:23
  28.2 0.7 %collective-permute-start.5 = (bf16[128,512]{1,0:T(8,128)(2,1)S(1)}, bf16[128,512]{1,0:T(8,128)(2,1)S(1)}, u32[]{:S(2)}, u32[]{:S(2)}) collective-permute-start(bf16[128,512]{1,0:T(8,128)(2,1)S(1)} %get-tuple-element.46), channel_id=1, source_target_pairs={{4,8},{12,16},{20,24},{8,4},{16,12},{24,20},{5,9},{13,17},{21,25},... | collective-permute-start | bytes 393224 | tf_op jit(solution)/shard_map/ppermute | solution.py:18
  28.8 4.7 %collective-permute-start.6 = (bf16[128,512]{1,0:T(8,128)(2,1)S(1)}, bf16[128,512]{1,0:T(8,128)(2,1)S(1)}, u32[]{:S(2)}, u32[]{:S(2)}) collective-permute-start(bf16[128,512]{1,0:T(8,128)(2,1)S(1)} %get-tuple-element.47), channel_id=1, source_target_pairs={{0,1},{2,3},{1,0},{3,2},{4,5},{6,7},{5,4},{7,6},{8,9},{10,11},{9,8... | collective-permute-start | bytes 393224 | tf_op jit(solution)/shard_map/ppermute | solution.py:18
  33.5 0.0 collective-permute-done.8.refs_0_
  33.5 0.7 %collective-permute-start.7 = (bf16[128,512]{1,0:T(8,128)(2,1)S(1)}, bf16[128,512]{1,0:T(8,128)(2,1)S(1)}, u32[]{:S(2)}, u32[]{:S(2)}) collective-permute-start(bf16[128,512]{1,0:T(8,128)(2,1)S(1)} %get-tuple-element.48), channel_id=1, source_target_pairs={{1,2},{2,1},{5,6},{6,5},{9,10},{10,9},{13,14},{14,13},{17,18},{18,... | collective-permute-start | bytes 393224 | tf_op jit(solution)/shard_map/ppermute | solution.py:18
  34.2 5.3 %collective-permute-done.9.refs_1_ = bf16[256,512]{1,0:T(8,128)(2,1)S(1)} collective-permute-done((bf16[256,512]{1,0:T(8,128)(2,1)S(1)}, bf16[256,512]{1,0:T(8,128)(2,1)S(1)}, u32[]{:S(2)}, u32[]{:S(2)}) %collective-permute-start.9) | collective-permute-done | bytes 262176 | tf_op jit(solution)/shard_map/ppermute | solution.py:23
  39.4 0.7 %collective-permute-done.10.refs_2_ = bf16[256,512]{1,0:T(8,128)(2,1)S(1)} collective-permute-done((bf16[256,512]{1,0:T(8,128)(2,1)S(1)}, bf16[256,512]{1,0:T(8,128)(2,1)S(1)}, u32[]{:S(2)}, u32[]{:S(2)}) %collective-permute-start.10) | collective-permute-done | bytes 262176 | tf_op jit(solution)/shard_map/ppermute | solution.py:23
  40.1 0.1 shard_map.98
  40.2 4.7 %collective-permute-start.11 = (bf16[64,512]{1,0:T(8,128)(2,1)S(1)}, bf16[64,512]{1,0:T(8,128)(2,1)S(1)}, u32[]{:S(2)}, u32[]{:S(2)}) collective-permute-start(bf16[64,512]{1,0:T(8,128)(2,1)S(1)} %get-tuple-element.55), channel_id=1, source_target_pairs={{0,1},{1,0},{2,3},{3,2},{4,5},{5,4},{6,7},{7,6},{8,9},{9,8},{10,11... | collective-permute-start | bytes 196616 | tf_op jit(solution)/shard_map/ppermute | solution.py:23
  44.9 1.5 %collective-permute-start.12 = (bf16[64,512]{1,0:T(8,128)(2,1)S(1)}, bf16[64,512]{1,0:T(8,128)(2,1)S(1)}, u32[]{:S(2)}, u32[]{:S(2)}) collective-permute-start(bf16[64,512]{1,0:T(8,128)(2,1)S(1)} %get-tuple-element.56), channel_id=1, source_target_pairs={{0,2},{1,3},{2,0},{3,1},{4,6},{5,7},{6,4},{7,5},{8,10},{9,11},{10,... | collective-permute-start | bytes 196616 | tf_op jit(solution)/shard_map/ppermute | solution.py:23
  46.4 0.0 collective-permute-done.5.odd_first_ref
  46.4 1.4 %collective-permute-start.13 = (bf16[64,512]{1,0:T(8,128)(2,1)S(1)}, bf16[64,512]{1,0:T(8,128)(2,1)S(1)}, u32[]{:S(2)}, u32[]{:S(2)}) collective-permute-start(bf16[64,512]{1,0:T(8,128)(2,1)S(1)} %get-tuple-element.57), channel_id=1, source_target_pairs={{0,3},{1,2},{2,1},{3,0},{4,7},{5,6},{6,5},{7,4},{8,11},{9,10},{10,... | collective-permute-start | bytes 196616 | tf_op jit(solution)/shard_map/ppermute | solution.py:23
  47.8 0.0 collective-permute-done.6.pair_second_ref
  47.8 0.0 collective-permute-done.7.odd_second_ref
  47.8 1.2 %shard_map.96 = bf16[2,2,64,512]{3,2,1,0:T(8,128)(2,1)} custom-call(f32[256,512]{1,0:T(8,128)S(1)} %get-tuple-element.39.own_ref, f32[256,512]{1,0:T(8,128)S(1)} %get-tuple-element.40.enter_ref, f32[128,512]{1,0:T(8,128)S(1)} %get-tuple-element.41.slope_top_first_ref, f32[128,512]{1,0:T(8,128)S(1)} %get-tuple-element.42.slope_top_second_ref, ...), custom_call_target="tpu_custom_call" | custom-call | tf_op jit(solution)/shard_map/pallas_call | solution.py:51
  49.0 0.0 collective-permute-done.11.refs_0_
  49.0 2.7 %collective-permute-done.12.refs_1_ = bf16[64,512]{1,0:T(8,128)(2,1)S(1)} collective-permute-done((bf16[64,512]{1,0:T(8,128)(2,1)S(1)}, bf16[64,512]{1,0:T(8,128)(2,1)S(1)}, u32[]{:S(2)}, u32[]{:S(2)}) %collective-permute-start.12) | collective-permute-done | bytes 65568 | tf_op jit(solution)/shard_map/ppermute | solution.py:23
  51.7 0.8 %collective-permute-done.13.refs_2_ = bf16[64,512]{1,0:T(8,128)(2,1)S(1)} collective-permute-done((bf16[64,512]{1,0:T(8,128)(2,1)S(1)}, bf16[64,512]{1,0:T(8,128)(2,1)S(1)}, u32[]{:S(2)}, u32[]{:S(2)}) %collective-permute-start.13) | collective-permute-done | bytes 65568 | tf_op jit(solution)/shard_map/ppermute | solution.py:23
  52.5 0.7 %shard_map.99 = (f32[192,128]{1,0:T(8,128)}, f32[64,128]{1,0:T(8,128)}) custom-call(f32[64,512]{1,0:T(8,128)S(1)} %get-tuple-element.54.keep_ref, bf16[64,512]{1,0:T(8,128)(2,1)S(1)} %collective-permute-done.11.refs_0_, bf16[64,512]{1,0:T(8,128)(2,1)S(1)} %collective-permute-done.12.refs_1_, bf16[64,512]{1,0:T(8,128)(2,1)S(1)} %collective-permute-done.13.refs_2_), custom_call_target="tpu_custom_call" | custom-call | tf_op jit(solution)/shard_map/pallas_call | solution.py:51
  (7 shorter events, 0.0 us)
Async XLA Ops:
  0.6 1.1 %copy-start.2 = (bf16[3,2,2,64,512]{4,3,2,1,0:T(8,128)(2,1)S(1)}, bf16[3,2,2,64,512]{4,3,2,1,0:T(8,128)(2,1)}, u32[]{:S(2)}) copy-start(bf16[3,2,2,64,512]{4,3,2,1,0:T(8,128)(2,1)} %refs_5_.1) | copy-start | bytes 2359300
  1.8 0.9 %copy-start.4 = (bf16[2,2,64,512]{3,2,1,0:T(8,128)(2,1)S(1)}, bf16[2,2,64,512]{3,2,1,0:T(8,128)(2,1)}, u32[]{:S(2)}) copy-start(bf16[2,2,64,512]{3,2,1,0:T(8,128)(2,1)} %refs_4_.1) | copy-start | bytes 786436
  2.7 0.7 %copy-start.8 = (s32[3,2,2,64]{3,2,1,0:T(2,128)S(1)}, s32[3,2,2,64]{3,2,1,0:T(2,128)}, u32[]{:S(2)}) copy-start(s32[3,2,2,64]{3,2,1,0:T(2,128)} %refs_6_.1) | copy-start | bytes 9220
  3.4 9.3 %copy-start.3 = (bf16[3,2,2,64,512]{4,3,2,1,0:T(8,128)(2,1)S(1)}, bf16[3,2,2,64,512]{4,3,2,1,0:T(8,128)(2,1)}, u32[]{:S(2)}) copy-start(bf16[3,2,2,64,512]{4,3,2,1,0:T(8,128)(2,1)} %refs_5_.1) | copy-start | bytes 2359300
  3.4 9.3 %copy-start.5 = (bf16[2,2,64,512]{3,2,1,0:T(8,128)(2,1)S(1)}, bf16[2,2,64,512]{3,2,1,0:T(8,128)(2,1)}, u32[]{:S(2)}) copy-start(bf16[2,2,64,512]{3,2,1,0:T(8,128)(2,1)} %refs_4_.1) | copy-start | bytes 786436
  3.5 9.2 %copy-start.9 = (s32[3,2,2,64]{3,2,1,0:T(2,128)S(1)}, s32[3,2,2,64]{3,2,1,0:T(2,128)}, u32[]{:S(2)}) copy-start(s32[3,2,2,64]{3,2,1,0:T(2,128)} %refs_6_.1) | copy-start | bytes 9220
  3.5 7.0 %collective-permute-start = (bf16[272,512]{1,0:T(8,128)(2,1)S(1)}, bf16[272,512]{1,0:T(8,128)(2,1)S(1)}, u32[]{:S(2)}, u32[]{:S(2)}) collective-permute-start(bf16[272,512]{1,0:T(8,128)(2,1)S(1)} %get-tuple-element.34), channel_id=1, source_target_pairs={{0,4},{8,12},{16,20},{24,28},{4,0},{12,8},{20,16},{28,24},{1,5},{9... | collective-permute-start | bytes 835592 | tf_op jit(solution)/shard_map/ppermute | solution.py:18
  4.1 6.4 %collective-permute-start.1 = (bf16[272,512]{1,0:T(8,128)(2,1)S(1)}, bf16[272,512]{1,0:T(8,128)(2,1)S(1)}, u32[]{:S(2)}, u32[]{:S(2)}) collective-permute-start(bf16[272,512]{1,0:T(8,128)(2,1)S(1)} %get-tuple-element.35), channel_id=1, source_target_pairs={{4,8},{12,16},{20,24},{8,4},{16,12},{24,20},{5,9},{13,17},{21,25},... | collective-permute-start | bytes 835592 | tf_op jit(solution)/shard_map/ppermute | solution.py:18
  4.7 8.0 %collective-permute-start.2 = (bf16[272,512]{1,0:T(8,128)(2,1)S(1)}, bf16[272,512]{1,0:T(8,128)(2,1)S(1)}, u32[]{:S(2)}, u32[]{:S(2)}) collective-permute-start(bf16[272,512]{1,0:T(8,128)(2,1)S(1)} %get-tuple-element.36), channel_id=1, source_target_pairs={{0,1},{2,3},{1,0},{3,2},{4,5},{6,7},{5,4},{7,6},{8,9},{10,11},{9,8... | collective-permute-start | bytes 835592 | tf_op jit(solution)/shard_map/ppermute | solution.py:18
  7.5 5.2 %collective-permute-start.3 = (bf16[272,512]{1,0:T(8,128)(2,1)S(1)}, bf16[272,512]{1,0:T(8,128)(2,1)S(1)}, u32[]{:S(2)}, u32[]{:S(2)}) collective-permute-start(bf16[272,512]{1,0:T(8,128)(2,1)S(1)} %get-tuple-element.37), channel_id=1, source_target_pairs={{1,2},{2,1},{5,6},{6,5},{9,10},{10,9},{13,14},{14,13},{17,18},{18,... | collective-permute-start | bytes 835592 | tf_op jit(solution)/shard_map/ppermute | solution.py:18
  8.2 1.4 %copy-start = (bf16[1536,512]{1,0:T(8,128)(2,1)S(1)}, bf16[1536,512]{1,0:T(8,128)(2,1)}, u32[]{:S(2)}) copy-start(bf16[1536,512]{1,0:T(8,128)(2,1)} %weight_ref.3) | copy-start | bytes 4718596
  9.6 3.1 %copy-start.1 = (bf16[1536,512]{1,0:T(8,128)(2,1)S(1)}, bf16[1536,512]{1,0:T(8,128)(2,1)}, u32[]{:S(2)}) copy-start(bf16[1536,512]{1,0:T(8,128)(2,1)} %weight_ref.3) | copy-start | bytes 4718596
  9.6 3.1 %copy-start.6 = (bf16[2,2,64,512]{3,2,1,0:T(8,128)(2,1)S(1)}, bf16[2,2,64,512]{3,2,1,0:T(8,128)(2,1)}, u32[]{:S(2)}) copy-start(bf16[2,2,64,512]{3,2,1,0:T(8,128)(2,1)} %cotangent_ref.1) | copy-start | bytes 786436
  9.6 3.2 %copy-start.7 = (bf16[512,512]{1,0:T(8,128)(2,1)S(1)}, bf16[512,512]{1,0:T(8,128)(2,1)}, u32[]{:S(2)}) copy-start(bf16[512,512]{1,0:T(8,128)(2,1)} %refs_3_.1) | copy-start | bytes 1572868
  17.4 4.8 %collective-permute-start.4 = (bf16[1152,512]{1,0:T(8,128)(2,1)S(1)}, bf16[1152,512]{1,0:T(8,128)(2,1)S(1)}, u32[]{:S(2)}, u32[]{:S(2)}) collective-permute-start(bf16[1152,512]{1,0:T(8,128)(2,1)S(1)} %get-tuple-element.45), channel_id=1, source_target_pairs={{0,4},{8,12},{16,20},{24,28},{4,0},{12,8},{20,16},{28,24},{1,5},{9... | collective-permute-start | bytes 3538952 | tf_op jit(solution)/shard_map/ppermute | solution.py:18
  22.4 11.1 %collective-permute-start.8 = (bf16[256,512]{1,0:T(8,128)(2,1)S(1)}, bf16[256,512]{1,0:T(8,128)(2,1)S(1)}, u32[]{:S(2)}, u32[]{:S(2)}) collective-permute-start(bf16[256,512]{1,0:T(8,128)(2,1)S(1)} %get-tuple-element.51), channel_id=1, source_target_pairs={{0,8},{4,12},{8,0},{12,4},{16,24},{20,28},{24,16},{28,20},{1,9},{5... | collective-permute-start | bytes 786440 | tf_op jit(solution)/shard_map/ppermute | solution.py:23
  25.8 13.6 %collective-permute-start.9 = (bf16[256,512]{1,0:T(8,128)(2,1)S(1)}, bf16[256,512]{1,0:T(8,128)(2,1)S(1)}, u32[]{:S(2)}, u32[]{:S(2)}) collective-permute-start(bf16[256,512]{1,0:T(8,128)(2,1)S(1)} %get-tuple-element.52), channel_id=1, source_target_pairs={{0,16},{4,20},{8,24},{12,28},{16,0},{20,4},{24,8},{28,12},{1,17},{... | collective-permute-start | bytes 786440 | tf_op jit(solution)/shard_map/ppermute | solution.py:23
  26.8 13.3 %collective-permute-start.10 = (bf16[256,512]{1,0:T(8,128)(2,1)S(1)}, bf16[256,512]{1,0:T(8,128)(2,1)S(1)}, u32[]{:S(2)}, u32[]{:S(2)}) collective-permute-start(bf16[256,512]{1,0:T(8,128)(2,1)S(1)} %get-tuple-element.53), channel_id=1, source_target_pairs={{0,24},{4,28},{8,16},{12,20},{16,8},{20,12},{24,0},{28,4},{1,25},{... | collective-permute-start | bytes 786440 | tf_op jit(solution)/shard_map/ppermute | solution.py:23
  28.2 18.2 %collective-permute-start.5 = (bf16[128,512]{1,0:T(8,128)(2,1)S(1)}, bf16[128,512]{1,0:T(8,128)(2,1)S(1)}, u32[]{:S(2)}, u32[]{:S(2)}) collective-permute-start(bf16[128,512]{1,0:T(8,128)(2,1)S(1)} %get-tuple-element.46), channel_id=1, source_target_pairs={{4,8},{12,16},{20,24},{8,4},{16,12},{24,20},{5,9},{13,17},{21,25},... | collective-permute-start | bytes 393224 | tf_op jit(solution)/shard_map/ppermute | solution.py:18
  28.8 18.9 %collective-permute-start.6 = (bf16[128,512]{1,0:T(8,128)(2,1)S(1)}, bf16[128,512]{1,0:T(8,128)(2,1)S(1)}, u32[]{:S(2)}, u32[]{:S(2)}) collective-permute-start(bf16[128,512]{1,0:T(8,128)(2,1)S(1)} %get-tuple-element.47), channel_id=1, source_target_pairs={{0,1},{2,3},{1,0},{3,2},{4,5},{6,7},{5,4},{7,6},{8,9},{10,11},{9,8... | collective-permute-start | bytes 393224 | tf_op jit(solution)/shard_map/ppermute | solution.py:18
  33.5 14.3 %collective-permute-start.7 = (bf16[128,512]{1,0:T(8,128)(2,1)S(1)}, bf16[128,512]{1,0:T(8,128)(2,1)S(1)}, u32[]{:S(2)}, u32[]{:S(2)}) collective-permute-start(bf16[128,512]{1,0:T(8,128)(2,1)S(1)} %get-tuple-element.48), channel_id=1, source_target_pairs={{1,2},{2,1},{5,6},{6,5},{9,10},{10,9},{13,14},{14,13},{17,18},{18,... | collective-permute-start | bytes 393224 | tf_op jit(solution)/shard_map/ppermute | solution.py:18
  40.2 8.8 %collective-permute-start.11 = (bf16[64,512]{1,0:T(8,128)(2,1)S(1)}, bf16[64,512]{1,0:T(8,128)(2,1)S(1)}, u32[]{:S(2)}, u32[]{:S(2)}) collective-permute-start(bf16[64,512]{1,0:T(8,128)(2,1)S(1)} %get-tuple-element.55), channel_id=1, source_target_pairs={{0,1},{1,0},{2,3},{3,2},{4,5},{5,4},{6,7},{7,6},{8,9},{9,8},{10,11... | collective-permute-start | bytes 196616 | tf_op jit(solution)/shard_map/ppermute | solution.py:23
  44.9 6.8 %collective-permute-start.12 = (bf16[64,512]{1,0:T(8,128)(2,1)S(1)}, bf16[64,512]{1,0:T(8,128)(2,1)S(1)}, u32[]{:S(2)}, u32[]{:S(2)}) collective-permute-start(bf16[64,512]{1,0:T(8,128)(2,1)S(1)} %get-tuple-element.56), channel_id=1, source_target_pairs={{0,2},{1,3},{2,0},{3,1},{4,6},{5,7},{6,4},{7,5},{8,10},{9,11},{10,... | collective-permute-start | bytes 196616 | tf_op jit(solution)/shard_map/ppermute | solution.py:23
  46.4 6.1 %collective-permute-start.13 = (bf16[64,512]{1,0:T(8,128)(2,1)S(1)}, bf16[64,512]{1,0:T(8,128)(2,1)S(1)}, u32[]{:S(2)}, u32[]{:S(2)}) collective-permute-start(bf16[64,512]{1,0:T(8,128)(2,1)S(1)} %get-tuple-element.57), channel_id=1, source_target_pairs={{0,3},{1,2},{2,1},{3,0},{4,7},{5,6},{6,5},{7,4},{8,11},{9,10},{10,... | collective-permute-start | bytes 196616 | tf_op jit(solution)/shard_map/ppermute | solution.py:23

commit v3 on v2

v3 whole, which is shorter than its diff:
```python
import functools

import jax
import jax.numpy as jnp
from jax import lax
from jax.experimental import pallas as pl
from jax.experimental.pallas import tpu as pltpu
from jax.sharding import PartitionSpec as P

F32 = jnp.float32
BF16 = jnp.bfloat16
PAD = 16


def swapped(value, axis, first):
    count = lax.axis_size(axis)
    lower = range(first, count - 1, 2)
    return lax.ppermute(value, axis, [(at, at + 1) for at in lower] + [(at + 1, at) for at in lower])


def exchanged(value, axis, flip):
    count = lax.axis_size(axis)
    return lax.ppermute(value, axis, [(source, source ^ flip) for source in range(count)])


def dot(left, right):
    return jnp.dot(left, right, preferred_element_type=F32)


def dot_nt(left, right):
    return lax.dot_general(left, right, (((1,), (1,)), ((), ())), preferred_element_type=F32)


def dot_tn(left, right):
    return lax.dot_general(left, right, (((0,), (0,)), ((), ())), preferred_element_type=F32)


def column_of(row):
    size = row.shape[-1]
    spread = jnp.broadcast_to(row, (size, size))
    down = lax.broadcasted_iota(jnp.int32, (size, size), 0)
    across = lax.broadcasted_iota(jnp.int32, (size, size), 1)
    return jnp.sum(jnp.where(down == across, spread, 0.0), axis=1, keepdims=True)


def sigmoid(values):
    return 0.5 * jnp.tanh(0.5 * values) + 0.5


def call(kernel, outs, args, scratch=(), limit=4 << 20, cost=None, far=0):
    return pl.pallas_call(
        kernel,
        out_shape=[jax.ShapeDtypeStruct(shape, dtype) for shape, dtype in outs],
        in_specs=[pl.BlockSpec(memory_space=pl.ANY)] * far + [pl.BlockSpec(memory_space=pltpu.VMEM)] * (len(args) - far),
        out_specs=[pl.BlockSpec(memory_space=pltpu.VMEM)] * len(outs),
        scratch_shapes=list(scratch),
        compiler_params=pltpu.CompilerParams(vmem_limit_bytes=limit),
        cost_estimate=cost,
    )(*args)


def spread_rows(rows, count):
    down = lax.broadcasted_iota(jnp.int32, (count, rows[0].shape[-1]), 0)
    tile = jnp.zeros((count, rows[0].shape[-1]), F32)
    for index, row in enumerate(rows):
        tile = jnp.where(down == index, row, tile)
    return tile


def is_even(axis):
    return lax.axis_index(axis) % 2 == 0


def pack_kernel(
    dims, node_ref, edge_ref, open_ref, pair_first_ref, odd_first_ref, pair_second_ref, odd_second_ref, sems
):
    ex, ey, nz, _ = dims

    def upward(ref, direction, cells):
        pairs = []
        for index, (x, y) in enumerate(cells):
            pairs.append((node_ref.at[x, y], ref.at[pl.ds(index * nz, nz)]))
            pairs.append((edge_ref.at[direction, x, y], ref.at[pl.ds((len(cells) + index) * nz, nz)]))
        return pairs

    def downward(ref, cells):
        return [(node_ref.at[x, y], ref.at[pl.ds(index * nz, nz)]) for index, (x, y) in enumerate(cells)]

    plans, used = [], 0
    for direction, axis, pair_ref, odd_ref, top, low in (
        (1, "gy", pair_second_ref, odd_second_ref, [(x, ey - 1) for x in range(ex)], [(x, 0) for x in range(ex)]),
        (0, "gx", pair_first_ref, odd_first_ref, [(ex - 1, y) for y in range(ey)], [(0, y) for y in range(ey)]),
    ):
        choices = [upward(up, direction, top) + downward(down, low) for up, down in ((pair_ref, odd_ref), (odd_ref, pair_ref))]
        copies = [
            [pltpu.make_async_copy(source, target, sems.at[used + index]) for index, (source, target) in enumerate(pairs)]
            for pairs in choices
        ]
        used += len(copies[0])
        mask = spread_rows([open_ref[direction, x, y : y + 1].astype(F32) for x, y in top], PAD).astype(BF16)
        plans.append((is_even(axis), copies, (pair_ref, odd_ref), 2 * len(top) * nz, mask))
    for even, copies, refs, start, mask in plans:
        for wanted, group in ((even, copies[0]), (jnp.logical_not(even), copies[1])):
            @pl.when(wanted)
            def _():
                for copy in group:
                    copy.start()
    for even, copies, refs, start, mask in plans:
        for ref in refs:
            ref[start:, :nz] = mask
        for wanted, group in ((even, copies[0]), (jnp.logical_not(even), copies[1])):
            @pl.when(wanted)
            def _():
                for copy in group:
                    copy.wait()


def edge_terms(preact, open_column):
    gate = sigmoid(preact)
    opened = gate * open_column
    message = (preact * opened).astype(BF16).astype(F32)
    return message, opened * (1.0 + preact * (1.0 - gate))


def halves(even, pair_ref, odd_ref, rows):
    def pick(first, second, start, stop):
        return jnp.where(even, first[start:stop], second[start:stop])

    return (
        pick(pair_ref, odd_ref, 0, rows),
        pick(odd_ref, pair_ref, 0, rows),
        pick(odd_ref, pair_ref, rows, 2 * rows),
        pick(odd_ref, pair_ref, 2 * rows, 2 * rows + PAD).astype(F32),
    )


def before_kernel(
    dims, node_ref, edge_ref, open_ref, weight_ref,
    sum_ref, slope_ref, stored_top_first_ref, other_low_first_ref, stored_top_second_ref, other_low_second_ref,
    other_ref, stored_ref, message_ref,
):
    ex, ey, nz, features = dims

    def rows(x, y):
        return slice((x * ey + y) * nz, (x * ey + y + 1) * nz)

    def part(index):
        return slice(index * nz, (index + 1) * nz)

    node = node_ref[...].reshape(-1, features)
    own = dot(node, weight_ref[:features])
    other_ref[...] = dot(node, weight_ref[features : 2 * features])
    for direction in range(3):
        stored_ref[direction] = own + dot(edge_ref[direction].reshape(-1, features), weight_ref[2 * features :])
    inside_third = jnp.where(lax.broadcasted_iota(jnp.int32, (nz, 1), 0) < nz - 1, 1.0, 0.0)
    for y in range(ey):
        stored_top_first_ref[part(y)] = stored_ref[0, rows(ex - 1, y)]
        other_low_first_ref[part(y)] = other_ref[rows(0, y)]
    for x in range(ex):
        stored_top_second_ref[part(x)] = stored_ref[1, rows(x, ey - 1)]
        other_low_second_ref[part(x)] = other_ref[rows(x, 0)]
        for y in range(ey):
            here = rows(x, y)
            column = [column_of(open_ref[direction, x, y : y + 1].astype(F32)) for direction in range(3)]
            if x + 1 < ex:
                beyond = other_ref[rows(x + 1, y)]
                message_ref[0, here], slope_ref[0, here] = edge_terms(stored_ref[0, here] + beyond, column[0])
            if y + 1 < ey:
                beyond = other_ref[rows(x, y + 1)]
                message_ref[1, here], slope_ref[1, here] = edge_terms(stored_ref[1, here] + beyond, column[1])
            beyond = pltpu.roll(other_ref[here], nz - 1, 0)
            message_ref[2, here], slope_ref[2, here] = edge_terms(stored_ref[2, here] + beyond, column[2] * inside_third)
    for x in range(ex):
        for y in range(ey):
            here = rows(x, y)
            third = message_ref[2, here]
            total = third - pltpu.roll(third, 1, 0)
            if x + 1 < ex:
                total = total + message_ref[0, here]
            if x > 0:
                total = total - message_ref[0, rows(x - 1, y)]
            if y + 1 < ey:
                total = total + message_ref[1, here]
            if y > 0:
                total = total - message_ref[1, rows(x, y - 1)]
            sum_ref[here] = total


def layer_kernel(
    dims,
    sum_ref, slope_ref, stored_top_first_ref, other_low_first_ref, stored_top_second_ref, other_low_second_ref,
    weight_ref, node_weight_ref, node_ref, edge_ref, open_ref, cotangent_ref,
    pair_first_ref, odd_first_ref, pair_second_ref, odd_second_ref,
    new_ref, grad_odd_first_ref, grad_pair_second_ref, grad_odd_second_ref,
    own_ref, enter_ref, slope_top_first_ref, slope_low_first_ref, slope_top_second_ref, slope_low_second_ref,
    grad_pair_first_ref, send_ref, keep_ref,
    summed_ref, update_ref, grad_ref, grad_low_ref, grads_ref, total_ref,
):
    ex, ey, nz, features = dims
    at_first, at_second = lax.axis_index("gx"), lax.axis_index("gy")
    inside_first = (at_first < lax.axis_size("gx") - 1).astype(F32)
    inside_second = (at_second < lax.axis_size("gy") - 1).astype(F32)
    even_first, even_second = is_even("gx"), is_even("gy")

    def rows(x, y):
        return slice((x * ey + y) * nz, (x * ey + y + 1) * nz)

    def part(index):
        return slice(index * nz, (index + 1) * nz)

    rows_first, rows_second = ey * nz, ex * nz
    node_above_first, node_below_first, edge_below_first, mask_first = halves(
        even_first, pair_first_ref, odd_first_ref, rows_first
    )
    node_above_second, node_below_second, edge_below_second, mask_second = halves(
        even_second, pair_second_ref, odd_second_ref, rows_second
    )
    other_weight = weight_ref[features : 2 * features]
    above_first, above_second = dot(node_above_first, other_weight), dot(node_above_second, other_weight)
    entering_first = dot(node_below_first, weight_ref[:features]) + dot(edge_below_first, weight_ref[2 * features :])
    entering_second = dot(node_below_second, weight_ref[:features]) + dot(edge_below_second, weight_ref[2 * features :])
    totals = [[sum_ref[rows(x, y)] for y in range(ey)] for x in range(ex)]
    for y in range(ey):
        here = part(y)
        column = column_of(open_ref[0, ex - 1, y : y + 1].astype(F32)) * inside_first
        message, slope_top_first_ref[here] = edge_terms(stored_top_first_ref[here] + above_first[here], column)
        totals[ex - 1][y] = totals[ex - 1][y] + message
        column = column_of(mask_first[y : y + 1, :nz])
        message, slope_low_first_ref[here] = edge_terms(entering_first[here] + other_low_first_ref[here], column)
        totals[0][y] = totals[0][y] - message
    for x in range(ex):
        here = part(x)
        column = column_of(open_ref[1, x, ey - 1 : ey].astype(F32)) * inside_second
        message, slope_top_second_ref[here] = edge_terms(stored_top_second_ref[here] + above_second[here], column)
        totals[x][ey - 1] = totals[x][ey - 1] + message
        column = column_of(mask_second[x : x + 1, :nz])
        message, slope_low_second_ref[here] = edge_terms(entering_second[here] + other_low_second_ref[here], column)
        totals[x][0] = totals[x][0] - message
    for x in range(ex):
        for y in range(ey):
            summed_ref[rows(x, y)] = totals[x][y].astype(BF16)

    node = node_ref[...].reshape(-1, features)
    update = dot(summed_ref[...], node_weight_ref[...])
    gate = sigmoid(update)
    new_ref[...] = (node.astype(F32) + update * gate).astype(BF16).reshape(new_ref.shape)
    cotangent = cotangent_ref[...].reshape(-1, features).astype(F32)
    update_ref[...] = (cotangent * (gate * (1.0 + update * (1.0 - gate)))).astype(BF16)
    grad_summed = dot_nt(update_ref[...], node_weight_ref[...]).astype(BF16)
    pair_target, extra = (grad_pair_first_ref, 0) if send_ref is None else (send_ref, send_ref.shape[0] - rows_first)
    for y in range(ey):
        low, top = grad_summed[rows(0, y)], grad_summed[rows(ex - 1, y)]
        pair_target[extra + y * nz : extra + (y + 1) * nz] = jnp.where(even_first, top, low)
        grad_odd_first_ref[part(y)] = jnp.where(even_first, low, top)
    for x in range(ex):
        low, top = grad_summed[rows(x, 0)], grad_summed[rows(x, ey - 1)]
        grad_pair_second_ref[part(x)] = jnp.where(even_second, top, low)
        grad_odd_second_ref[part(x)] = jnp.where(even_second, low, top)
    wide = grad_summed.astype(F32)

    count = ex * ey * nz
    for index in range(ey + ex):
        cell = rows(0, index) if index < ey else rows(index - ey, 0)
        slope = slope_low_first_ref[part(index)] if index < ey else slope_low_second_ref[part(index - ey)]
        grad = -wide[cell] * slope
        grad_low_ref[part(index)] = grad
        grads_ref[3 * count + index * nz : 3 * count + (index + 1) * nz] = grad.astype(BF16)
    for x in range(ex):
        for y in range(ey):
            here = rows(x, y)
            mine = wide[here]
            lead = [
                mine - wide[rows(x + 1, y)] if x + 1 < ex else mine,
                mine - wide[rows(x, y + 1)] if y + 1 < ey else mine,
                mine - pltpu.roll(mine, nz - 1, 0),
            ]
            for direction in range(3):
                if direction == 0 and x == ex - 1:
                    slope = slope_top_first_ref[part(y)]
                elif direction == 1 and y == ey - 1:
                    slope = slope_top_second_ref[part(x)]
                else:
                    slope = slope_ref[direction, here]
                grad = lead[direction] * slope
                grad_ref[direction, here] = grad
                start = direction * count + (x * ey + y) * nz
                grads_ref[start : start + nz] = grad.astype(BF16)
    for x in range(ex):
        for y in range(ey):
            here = rows(x, y)
            third = grad_ref[2, here]
            own_ref[here] = grad_ref[0, here] + grad_ref[1, here] + third
            enter = pltpu.roll(third, 1, 0)
            enter = enter + (grad_ref[0, rows(x - 1, y)] if x > 0 else grad_low_ref[part(y)])
            enter = enter + (grad_ref[1, rows(x, y - 1)] if y > 0 else grad_low_ref[part(ey + x)])
            enter_ref[here] = enter

    grads_low = grads_ref[3 * count :]
    total_ref[:features] = dot_tn(
        jnp.concatenate([node, node_below_first, node_below_second], axis=0),
        jnp.concatenate([own_ref[...].astype(BF16), grads_low], axis=0),
    )
    tops = [grads_ref[((ex - 1) * ey + y) * nz : ((ex - 1) * ey + y + 1) * nz] for y in range(ey)]
    tops += [grads_ref[count + (x * ey + ey - 1) * nz : count + (x * ey + ey) * nz] for x in range(ex)]
    total_ref[features : 2 * features] = dot_tn(
        jnp.concatenate([node, node_above_first, node_above_second], axis=0),
        jnp.concatenate([enter_ref[...].astype(BF16), *tops], axis=0),
    )
    edges = edge_ref[...].reshape(-1, features)
    total_ref[2 * features : 3 * features] = dot_tn(
        jnp.concatenate([edges, edge_below_first, edge_below_second], axis=0), grads_ref[...]
    )
    total_ref[3 * features :] = dot_tn(summed_ref[...], update_ref[...])

    if send_ref is None:
        keep_ref[...] = total_ref[...]
        return
    planes = keep_ref.shape[0]
    seconds, chunk = lax.axis_size("gy"), keep_ref.shape[1] // lax.axis_size("gy")
    edge_rows, node_rows = chunk * 3 // 4, chunk // 4
    core, plane = at_first % 2, at_first // 2
    for block in range(planes):
        for second in range(seconds):
            there = (plane ^ block) * 2
            start = second * chunk
            for flip in (core, 1 - core):
                device = (there + flip) * seconds + (at_second ^ second)
                edge = total_ref[pl.ds(pl.multiple_of(device * edge_rows, 8), edge_rows)]
                node = total_ref[pl.ds(pl.multiple_of(3 * features + device * node_rows, 8), node_rows)]
                if flip is core:
                    keep_ref[block, start : start + edge_rows] = edge
                    keep_ref[block, start + edge_rows : start + chunk] = node
                else:
                    send_at = block * seconds * chunk + start
                    send_ref[send_at : send_at + edge_rows] = edge.astype(BF16)
                    send_ref[send_at + edge_rows : send_at + chunk] = node.astype(BF16)


def node_grad_kernel(
    dims, own_ref, enter_ref, slope_top_first_ref, slope_low_first_ref, slope_top_second_ref, slope_low_second_ref,
    pair_first_ref, odd_first_ref, pair_second_ref, odd_second_ref, cotangent_ref, weight_ref, out_ref,
):
    ex, ey, nz, features = dims
    even_first, even_second = is_even("gx"), is_even("gy")
    extra = pair_first_ref.shape[0] - ey * nz

    def rows(x, y):
        return slice((x * ey + y) * nz, (x * ey + y + 1) * nz)

    def part(index):
        return slice(index * nz, (index + 1) * nz)

    own, enter = [], []
    for x in range(ex):
        for y in range(ey):
            grad = own_ref[rows(x, y)]
            pair_first = pair_first_ref[extra + y * nz : extra + (y + 1) * nz].astype(F32)
            odd_first = odd_first_ref[part(y)].astype(F32)
            pair_second, odd_second = pair_second_ref[part(x)].astype(F32), odd_second_ref[part(x)].astype(F32)
            if x == ex - 1:
                grad = grad - jnp.where(even_first, pair_first, odd_first) * slope_top_first_ref[part(y)]
            if y == ey - 1:
                grad = grad - jnp.where(even_second, pair_second, odd_second) * slope_top_second_ref[part(x)]
            own.append(grad.astype(BF16))
            grad = enter_ref[rows(x, y)]
            if x == 0:
                grad = grad + jnp.where(even_first, odd_first, pair_first) * slope_low_first_ref[part(y)]
            if y == 0:
                grad = grad + jnp.where(even_second, odd_second, pair_second) * slope_low_second_ref[part(x)]
            enter.append(grad.astype(BF16))
    result = dot_nt(jnp.concatenate(own, axis=0), weight_ref[:features])
    result = result + dot_nt(jnp.concatenate(enter, axis=0), weight_ref[features : 2 * features])
    result = result + cotangent_ref[...].reshape(-1, features).astype(F32)
    out_ref[...] = result.astype(BF16).reshape(out_ref.shape)


def pair_sum_kernel(keep_ref, received_ref, kept_ref, *send_refs):
    rows = kept_ref.shape[0]
    kept_ref[...] = keep_ref[0] + received_ref[:rows].astype(F32)
    for index, send_ref in enumerate(send_refs, 1):
        send_ref[...] = (keep_ref[index] + received_ref[index * rows : (index + 1) * rows].astype(F32)).astype(BF16)


def plane_sum_kernel(groups, keep_ref, *refs):
    received, kept_ref, send_refs = refs[: groups[0] - 1], refs[groups[0] - 1], refs[groups[0] :]
    chunk = kept_ref.shape[0]
    for index in range(groups[1]):
        here = slice(index * chunk, (index + 1) * chunk)
        total = keep_ref[here]
        for ref in received:
            total = total + ref[here].astype(F32)
        if index == 0:
            kept_ref[...] = total
        else:
            send_refs[index - 1][...] = total.astype(BF16)


def last_sum_kernel(keep_ref, *refs):
    received, edge_ref, node_ref = refs[:-2], refs[-2], refs[-1]
    total = keep_ref[...]
    for ref in received:
        total = total + ref[...].astype(F32)
    lanes = edge_ref.shape[1]
    pieces = total.shape[1] // lanes
    edge_rows, node_rows = edge_ref.shape[0] // pieces, node_ref.shape[0] // pieces
    for piece in range(pieces):
        across = slice(piece * lanes, (piece + 1) * lanes)
        edge_ref[pl.ds(piece, edge_rows, stride=pieces)] = total[:edge_rows, across]
        node_ref[pl.ds(piece, node_rows, stride=pieces)] = total[edge_rows:, across]


def local(node_features, edge_features, open_faces, edge_weight, node_weight, cotangent):
    dims = ex, ey, nz, features = node_features.shape
    firsts, seconds = lax.axis_size("gx"), lax.axis_size("gy")
    devices = firsts * seconds
    count = ex * ey * nz

    face_first, face_second = (ey * nz, features), (ex * nz, features)
    packed_first, packed_second = (2 * ey * nz + PAD, features), (2 * ex * nz + PAD, features)
    copies = 3 * (ex + ey)
    pair_first, odd_first, pair_second, odd_second = call(
        functools.partial(pack_kernel, dims),
        [(packed_first, BF16)] * 2 + [(packed_second, BF16)] * 2,
        [node_features, edge_features, open_faces],
        scratch=[pltpu.SemaphoreType.DMA((copies,))],
        far=2,
    )
    pair_second = swapped(pair_second, "gy", 0)
    odd_second = swapped(odd_second, "gy", 1)
    odd_first = swapped(odd_first, "gx", 1)
    pair_first = swapped(pair_first, "gx", 0)
    before = [((count, features), F32), ((3, count, features), F32)] + [(face_first, F32)] * 2 + [(face_second, F32)] * 2
    before = call(
        functools.partial(before_kernel, dims),
        before,
        [node_features, edge_features, open_faces, edge_weight],
        scratch=[
            pltpu.VMEM((count, features), F32),
            pltpu.VMEM((3, count, features), F32),
            pltpu.VMEM((3, count, features), F32),
        ],
        limit=12 << 20,
    )
    total_rows = 4 * features
    chunk = total_rows // devices
    by_hand = (
        total_rows % devices == 0
        and chunk % 64 == 0
        and features % 128 == 0
        and firsts % 2 == 0
        and firsts & (firsts - 1) == 0
        and seconds & (seconds - 1) == 0
    )
    planes = firsts // 2
    outs = [(node_features.shape, BF16), (face_first, BF16), (face_second, BF16), (face_second, BF16)]
    outs += [((count, features), F32)] * 2 + [(face_first, F32)] * 2 + [(face_second, F32)] * 2
    if by_hand:
        outs += [((planes * seconds * chunk + ey * nz, features), BF16), ((planes, seconds * chunk, features), F32)]

        def kernel(*refs):
            layer_kernel(dims, *refs[:26], None, *refs[26:])

    else:
        outs += [(face_first, BF16), ((total_rows, features), F32)]

        def kernel(*refs):
            layer_kernel(dims, *refs[:27], None, *refs[27:])

    low_rows = (ex + ey) * nz
    results = call(
        kernel,
        outs,
        [
            *before, edge_weight, node_weight, node_features, edge_features, open_faces, cotangent,
            pair_first, odd_first, pair_second, odd_second,
        ],
        scratch=[
            pltpu.VMEM((count, features), BF16),
            pltpu.VMEM((count, features), BF16),
            pltpu.VMEM((3, count, features), F32),
            pltpu.VMEM((low_rows, features), F32),
            pltpu.VMEM((3 * count + low_rows, features), BF16),
            pltpu.VMEM((total_rows, features), F32),
        ],
        limit=14 << 20,
    )
    new_nodes, odd_first, pair_second, odd_second = results[:4]
    received, keep = results[10:]
    received = swapped(received, "gx", 0)
    pair_second = swapped(pair_second, "gy", 0)
    odd_second = swapped(odd_second, "gy", 1)
    odd_first = swapped(odd_first, "gx", 1)
    (node_grad,) = call(
        functools.partial(node_grad_kernel, dims),
        [(node_features.shape, BF16)],
        [
            *results[4:10], received, odd_first, pair_second, odd_second, cotangent, edge_weight,
        ],
    )
    if not by_hand:
        total = keep
        edge_part = lax.psum_scatter(total[: 3 * features].reshape(-1), ("gx", "gy"), scatter_dimension=0, tiled=True)
        node_part = lax.psum_scatter(total[3 * features :].reshape(-1), ("gx", "gy"), scatter_dimension=0, tiled=True)
        return new_nodes, node_grad, edge_part, node_part

    block = (seconds * chunk, features)
    kept, *sends = call(pair_sum_kernel, [(block, F32)] + [(block, BF16)] * (planes - 1), [keep, received])
    arrived = []
    for index, value in enumerate(sends):
        arrived.append(exchanged(value, "gx", 2 * (index + 1)))
    kept, *sends = call(
        functools.partial(plane_sum_kernel, (planes, seconds)),
        [((chunk, features), F32)] + [((chunk, features), BF16)] * (seconds - 1),
        [kept, *arrived],
    )
    arrived = []
    for index, value in enumerate(sends):
        arrived.append(exchanged(value, "gy", index + 1))
    pieces = features // 128
    edge_part, node_part = call(
        last_sum_kernel, [((chunk * 3 // 4 * pieces, 128), F32), ((chunk // 4 * pieces, 128), F32)], [kept, *arrived]
    )
    return new_nodes, node_grad, edge_part.reshape(-1), node_part.reshape(-1)


def solution(mesh):
    placed = (
        P("gx", "gy", None, None),
        P(None, "gx", "gy", None, None),
        P(None, "gx", "gy", None),
        P(),
        P(),
        P("gx", "gy", None, None),
    )
    return jax.shard_map(
        local,
        mesh=mesh,
        in_specs=placed,
        out_specs=(
            P("gx", "gy", None, None),
            P("gx", "gy", None, None),
            P(("gx", "gy")),
            P(("gx", "gy")),
        ),
        check_vma=False,
    )
```

time: 53.5 us -> 54 us (level)
  waiting for transfers between devices: 14.1 us -> 12.1 us
  local copies, waits for them, and re-layouts: 4.19 us -> 5.94 us
  Pallas kernels: 7.79 us -> 8.76 us
    ppermute x8, waiting for transfers between devices: 4.72 us -> 2.73 us  [swapped(): lax.ppermute(value, axis, [(at, at + 1) for at in lower] + [(at + 1, at)...]
    unnamed x20 -> x22, local copies, waits for them, and re-layouts: 4.19 us -> 5.94 us
    pallas_call x7, Pallas kernels: 7.79 us -> 8.76 us  [call(): pl.pallas_call(kernel, out_shape=[jax.ShapeDtypeStruct(shape, dtype) for...]
  transfers between devices with their start and end apart: 14 -> 14, of which waited for: 6 -> 6; matrix products, arithmetic and copies ran while one was open for 0% -> 0% of each run, Pallas kernels for 4% -> 5%
where the time goes in v3:
time: 54 us; the launch traced here: 53.6 us
  starting transfers between devices  26 us (48%)
  waiting for transfers between devices  12.1 us (22%)
  Pallas kernels  8.76 us (16%)
  local copies, waits for them, and re-layouts  5.94 us (11%)
  between operations  0.75 us (1%)
    ppermute x8, starting transfers between devices, swapped(): lax.ppermute(value, axis, [(at, at + 1) for at in lower] + [(at + 1, at)...  13.1 us
    ppermute x6, starting transfers between devices, exchanged(): lax.ppermute(value, axis, [(source, source ^ flip) for source in range(co...  13 us
    ppermute x6, waiting for transfers between devices, exchanged(): lax.ppermute(value, axis, [(source, source ^ flip) for source in range(co...  9.4 us
    pallas_call x7, Pallas kernels, call(): pl.pallas_call(kernel, out_shape=[jax.ShapeDtypeStruct(shape, dtype) for...  8.76 us
    unnamed x22, local copies, waits for them, and re-layouts  5.94 us
    ppermute x8, waiting for transfers between devices, swapped(): lax.ppermute(value, axis, [(at, at + 1) for at in lower] + [(at + 1, at)...  2.73 us
  transfers between devices with their start and end apart: 14, of which 6 were waited for; matrix products, arithmetic and copies ran while one was open for 0% of the time, Pallas kernels for 5%

profile of v3, /device:TPU:0, one launch (start us, length us, event | category | flops | bytes accessed | tf_op | source)
XLA Modules:
  0.0 53.6 jit_solution(5136885791802304978)
XLA Ops:
  0.6 0.0 copy-start.2
  0.6 1.1 %copy-done.2 = bf16[3,2,2,64,512]{4,3,2,1,0:T(8,128)(2,1)S(1)} copy-done((bf16[3,2,2,64,512]{4,3,2,1,0:T(8,128)(2,1)S(1)}, bf16[3,2,2,64,512]{4,3,2,1,0:T(8,128)(2,1)}, u32[]{:S(2)}) %copy-start.2) | copy-done | bytes 786456
  1.8 0.9 %copy-done.4 = bf16[2,2,64,512]{3,2,1,0:T(8,128)(2,1)S(1)} copy-done((bf16[2,2,64,512]{3,2,1,0:T(8,128)(2,1)S(1)}, bf16[2,2,64,512]{3,2,1,0:T(8,128)(2,1)}, u32[]{:S(2)}) %copy-start.4) | copy-done | bytes 262168
  2.7 0.7 %copy-done.9 = s32[3,2,2,64]{3,2,1,0:T(2,128)S(1)} copy-done((s32[3,2,2,64]{3,2,1,0:T(2,128)S(1)}, s32[3,2,2,64]{3,2,1,0:T(2,128)}, u32[]{:S(2)}) %copy-start.9) | copy-done | bytes 3096
  3.4 1.2 %shard_map.94 = (bf16[272,512]{1,0:T(8,128)(2,1)S(1)}, bf16[272,512]{1,0:T(8,128)(2,1)S(1)}, bf16[272,512]{1,0:T(8,128)(2,1)S(1)}, bf16[272,512]{1,0:T(8,128)(2,1)S(1)}) custom-call(bf16[2,2,64,512]{3,2,1,0:T(8,128)(2,1)S(1)} %copy-done.4, bf16[3,2,2,64,512]{4,3,2,1,0:T(8,128)(2,1)S(1)} %copy-done.2, s32[3,2,2,64]{3,2,1,0:T(2,128)S(1)} %copy-done.9), custom_call_target="tpu_custom_call" | custom-call | tf_op jit(solution)/shard_map/pallas_call | solution.py:51
  4.6 0.6 %collective-permute-start = (bf16[272,512]{1,0:T(8,128)(2,1)S(1)}, bf16[272,512]{1,0:T(8,128)(2,1)S(1)}, u32[]{:S(2)}, u32[]{:S(2)}) collective-permute-start(bf16[272,512]{1,0:T(8,128)(2,1)S(1)} %get-tuple-element.42), channel_id=1, source_target_pairs={{0,4},{8,12},{16,20},{24,28},{4,0},{12,8},{20,16},{28,24},{1,5},{9... | collective-permute-start | bytes 835592 | tf_op jit(solution)/shard_map/ppermute | solution.py:18
  5.2 0.7 %collective-permute-start.1 = (bf16[272,512]{1,0:T(8,128)(2,1)S(1)}, bf16[272,512]{1,0:T(8,128)(2,1)S(1)}, u32[]{:S(2)}, u32[]{:S(2)}) collective-permute-start(bf16[272,512]{1,0:T(8,128)(2,1)S(1)} %get-tuple-element.43), channel_id=1, source_target_pairs={{4,8},{12,16},{20,24},{8,4},{16,12},{24,20},{5,9},{13,17},{21,25},... | collective-permute-start | bytes 835592 | tf_op jit(solution)/shard_map/ppermute | solution.py:18
  5.8 2.6 %collective-permute-start.2 = (bf16[272,512]{1,0:T(8,128)(2,1)S(1)}, bf16[272,512]{1,0:T(8,128)(2,1)S(1)}, u32[]{:S(2)}, u32[]{:S(2)}) collective-permute-start(bf16[272,512]{1,0:T(8,128)(2,1)S(1)} %get-tuple-element.44), channel_id=1, source_target_pairs={{0,1},{2,3},{1,0},{3,2},{4,5},{6,7},{5,4},{7,6},{8,9},{10,11},{9,8... | collective-permute-start | bytes 835592 | tf_op jit(solution)/shard_map/ppermute | solution.py:18
  8.5 0.7 %collective-permute-start.3 = (bf16[272,512]{1,0:T(8,128)(2,1)S(1)}, bf16[272,512]{1,0:T(8,128)(2,1)S(1)}, u32[]{:S(2)}, u32[]{:S(2)}) collective-permute-start(bf16[272,512]{1,0:T(8,128)(2,1)S(1)} %get-tuple-element.45), channel_id=1, source_target_pairs={{1,2},{2,1},{5,6},{6,5},{9,10},{10,9},{13,14},{14,13},{17,18},{18,... | collective-permute-start | bytes 835592 | tf_op jit(solution)/shard_map/ppermute | solution.py:18
  9.1 0.0 copy-done.3
  9.2 0.0 copy-start
  9.2 1.4 %copy-done = bf16[1536,512]{1,0:T(8,128)(2,1)S(1)} copy-done((bf16[1536,512]{1,0:T(8,128)(2,1)S(1)}, bf16[1536,512]{1,0:T(8,128)(2,1)}, u32[]{:S(2)}) %copy-start) | copy-done | bytes 1572888
  10.6 0.9 %copy-done.5 = bf16[2,2,64,512]{3,2,1,0:T(8,128)(2,1)S(1)} copy-done((bf16[2,2,64,512]{3,2,1,0:T(8,128)(2,1)S(1)}, bf16[2,2,64,512]{3,2,1,0:T(8,128)(2,1)}, u32[]{:S(2)}) %copy-start.5) | copy-done | bytes 262168
  11.5 0.7 %copy-done.10 = s32[3,2,2,64]{3,2,1,0:T(2,128)S(1)} copy-done((s32[3,2,2,64]{3,2,1,0:T(2,128)S(1)}, s32[3,2,2,64]{3,2,1,0:T(2,128)}, u32[]{:S(2)}) %copy-start.10) | copy-done | bytes 3096
  12.2 1.2 %shard_map.93 = (f32[256,512]{1,0:T(8,128)S(1)}, f32[3,256,512]{2,1,0:T(8,128)S(1)}, f32[128,512]{1,0:T(8,128)S(1)}, f32[128,512]{1,0:T(8,128)S(1)}, f32[128,512]{1,0:T(8,128)S(1)}, /*index=5*/f32[128,512]{1,0:T(8,128)S(1)}) custom-call(bf16[2,2,64,512]{3,2,1,0:T(8,128)(2,1)S(1)} %copy-done.5, bf16[3,2,2,64,512]{4,3,2,1,0:T(8,128)(2,1)S(1)} %copy-done.3, ...), custom_call_target="tpu_custom_call" | custom-call | tf_op jit(solution)/shard_map/pallas_call | solution.py:51
  13.4 0.0 collective-permute-done.refs_12_
  13.4 0.0 collective-permute-done.1.refs_13_
  13.4 0.2 collective-permute-done.2.refs_14_
  13.7 0.0 collective-permute-done.3.refs_15_
  13.7 0.0 copy-done.6
  13.7 0.0 copy-done.1
  13.7 0.0 copy-done.7
  13.7 0.1 copy-done.8
  13.8 4.2 %shard_map.95 = (bf16[2,2,64,512]{3,2,1,0:T(8,128)(2,1)}, bf16[128,512]{1,0:T(8,128)(2,1)S(1)}, bf16[128,512]{1,0:T(8,128)(2,1)S(1)}, bf16[128,512]{1,0:T(8,128)...) custom-call(f32[256,512]{1,0:T(8,128)S(1)} %get-tuple-element.36.ref, ...), custom_call_target="tpu_custom_call" | custom-call | tf_op jit(solution)/shard_map/pallas_call | solution.py:51
  18.0 2.6 %collective-permute-start.4 = (bf16[1152,512]{1,0:T(8,128)(2,1)S(1)}, bf16[1152,512]{1,0:T(8,128)(2,1)S(1)}, u32[]{:S(2)}, u32[]{:S(2)}) collective-permute-start(bf16[1152,512]{1,0:T(8,128)(2,1)S(1)} %get-tuple-element.53), channel_id=1, source_target_pairs={{0,4},{8,12},{16,20},{24,28},{4,0},{12,8},{20,16},{28,24},{1,5},{9... | collective-permute-start | bytes 3538952 | tf_op jit(solution)/shard_map/ppermute | solution.py:18
  20.5 2.5 %collective-permute-done.4.pair_first_ref.received_ref = bf16[1152,512]{1,0:T(8,128)(2,1)S(1)} collective-permute-done((bf16[1152,512]{1,0:T(8,128)(2,1)S(1)}, bf16[1152,512]{1,0:T(8,128)(2,1)S(1)}, u32[]{:S(2)}, u32[]{:S(2)}) %collective-permute-start.4) | collective-permute-done | bytes 1179680 | tf_op jit(solution)/shard_map/ppermute | solution.py:18
  23.0 0.2 shard_map.97
  23.2 3.0 %collective-permute-start.8 = (bf16[256,512]{1,0:T(8,128)(2,1)S(1)}, bf16[256,512]{1,0:T(8,128)(2,1)S(1)}, u32[]{:S(2)}, u32[]{:S(2)}) collective-permute-start(bf16[256,512]{1,0:T(8,128)(2,1)S(1)} %get-tuple-element.59), channel_id=1, source_target_pairs={{0,8},{4,12},{8,0},{12,4},{16,24},{20,28},{24,16},{28,20},{1,9},{5... | collective-permute-start | bytes 786440 | tf_op jit(solution)/shard_map/ppermute | solution.py:23
  26.3 1.0 %collective-permute-start.9 = (bf16[256,512]{1,0:T(8,128)(2,1)S(1)}, bf16[256,512]{1,0:T(8,128)(2,1)S(1)}, u32[]{:S(2)}, u32[]{:S(2)}) collective-permute-start(bf16[256,512]{1,0:T(8,128)(2,1)S(1)} %get-tuple-element.60), channel_id=1, source_target_pairs={{0,16},{4,20},{8,24},{12,28},{16,0},{20,4},{24,8},{28,12},{1,17},{... | collective-permute-start | bytes 786440 | tf_op jit(solution)/shard_map/ppermute | solution.py:23
  27.3 1.4 %collective-permute-start.10 = (bf16[256,512]{1,0:T(8,128)(2,1)S(1)}, bf16[256,512]{1,0:T(8,128)(2,1)S(1)}, u32[]{:S(2)}, u32[]{:S(2)}) collective-permute-start(bf16[256,512]{1,0:T(8,128)(2,1)S(1)} %get-tuple-element.61), channel_id=1, source_target_pairs={{0,24},{4,28},{8,16},{12,20},{16,8},{20,12},{24,0},{28,4},{1,25},{... | collective-permute-start | bytes 786440 | tf_op jit(solution)/shard_map/ppermute | solution.py:23
  28.7 0.7 %collective-permute-start.5 = (bf16[128,512]{1,0:T(8,128)(2,1)S(1)}, bf16[128,512]{1,0:T(8,128)(2,1)S(1)}, u32[]{:S(2)}, u32[]{:S(2)}) collective-permute-start(bf16[128,512]{1,0:T(8,128)(2,1)S(1)} %get-tuple-element.54), channel_id=1, source_target_pairs={{4,8},{12,16},{20,24},{8,4},{16,12},{24,20},{5,9},{13,17},{21,25},... | collective-permute-start | bytes 393224 | tf_op jit(solution)/shard_map/ppermute | solution.py:18
  29.3 4.7 %collective-permute-start.6 = (bf16[128,512]{1,0:T(8,128)(2,1)S(1)}, bf16[128,512]{1,0:T(8,128)(2,1)S(1)}, u32[]{:S(2)}, u32[]{:S(2)}) collective-permute-start(bf16[128,512]{1,0:T(8,128)(2,1)S(1)} %get-tuple-element.55), channel_id=1, source_target_pairs={{0,1},{2,3},{1,0},{3,2},{4,5},{6,7},{5,4},{7,6},{8,9},{10,11},{9,8... | collective-permute-start | bytes 393224 | tf_op jit(solution)/shard_map/ppermute | solution.py:18
  34.0 0.0 collective-permute-done.8.refs_0_
  34.0 0.7 %collective-permute-start.7 = (bf16[128,512]{1,0:T(8,128)(2,1)S(1)}, bf16[128,512]{1,0:T(8,128)(2,1)S(1)}, u32[]{:S(2)}, u32[]{:S(2)}) collective-permute-start(bf16[128,512]{1,0:T(8,128)(2,1)S(1)} %get-tuple-element.56), channel_id=1, source_target_pairs={{1,2},{2,1},{5,6},{6,5},{9,10},{10,9},{13,14},{14,13},{17,18},{18,... | collective-permute-start | bytes 393224 | tf_op jit(solution)/shard_map/ppermute | solution.py:18
  34.7 5.3 %collective-permute-done.9.refs_1_ = bf16[256,512]{1,0:T(8,128)(2,1)S(1)} collective-permute-done((bf16[256,512]{1,0:T(8,128)(2,1)S(1)}, bf16[256,512]{1,0:T(8,128)(2,1)S(1)}, u32[]{:S(2)}, u32[]{:S(2)}) %collective-permute-start.9) | collective-permute-done | bytes 262176 | tf_op jit(solution)/shard_map/ppermute | solution.py:23
  39.9 0.7 %collective-permute-done.10.refs_2_ = bf16[256,512]{1,0:T(8,128)(2,1)S(1)} collective-permute-done((bf16[256,512]{1,0:T(8,128)(2,1)S(1)}, bf16[256,512]{1,0:T(8,128)(2,1)S(1)}, u32[]{:S(2)}, u32[]{:S(2)}) %collective-permute-start.10) | collective-permute-done | bytes 262176 | tf_op jit(solution)/shard_map/ppermute | solution.py:23
  40.6 0.1 shard_map.98
  40.7 4.9 %collective-permute-start.11 = (bf16[64,512]{1,0:T(8,128)(2,1)S(1)}, bf16[64,512]{1,0:T(8,128)(2,1)S(1)}, u32[]{:S(2)}, u32[]{:S(2)}) collective-permute-start(bf16[64,512]{1,0:T(8,128)(2,1)S(1)} %get-tuple-element.63), channel_id=1, source_target_pairs={{0,1},{1,0},{2,3},{3,2},{4,5},{5,4},{6,7},{7,6},{8,9},{9,8},{10,11... | collective-permute-start | bytes 196616 | tf_op jit(solution)/shard_map/ppermute | solution.py:23
  45.6 1.3 %collective-permute-start.12 = (bf16[64,512]{1,0:T(8,128)(2,1)S(1)}, bf16[64,512]{1,0:T(8,128)(2,1)S(1)}, u32[]{:S(2)}, u32[]{:S(2)}) collective-permute-start(bf16[64,512]{1,0:T(8,128)(2,1)S(1)} %get-tuple-element.64), channel_id=1, source_target_pairs={{0,2},{1,3},{2,0},{3,1},{4,6},{5,7},{6,4},{7,5},{8,10},{9,11},{10,... | collective-permute-start | bytes 196616 | tf_op jit(solution)/shard_map/ppermute | solution.py:23
  46.9 0.0 collective-permute-done.5.odd_first_ref
  46.9 1.4 %collective-permute-start.13 = (bf16[64,512]{1,0:T(8,128)(2,1)S(1)}, bf16[64,512]{1,0:T(8,128)(2,1)S(1)}, u32[]{:S(2)}, u32[]{:S(2)}) collective-permute-start(bf16[64,512]{1,0:T(8,128)(2,1)S(1)} %get-tuple-element.65), channel_id=1, source_target_pairs={{0,3},{1,2},{2,1},{3,0},{4,7},{5,6},{6,5},{7,4},{8,11},{9,10},{10,... | collective-permute-start | bytes 196616 | tf_op jit(solution)/shard_map/ppermute | solution.py:23
  48.3 0.0 collective-permute-done.6.pair_second_ref
  48.3 0.0 collective-permute-done.7.odd_second_ref
  48.3 1.2 %shard_map.96 = bf16[2,2,64,512]{3,2,1,0:T(8,128)(2,1)} custom-call(f32[256,512]{1,0:T(8,128)S(1)} %get-tuple-element.47.own_ref, f32[256,512]{1,0:T(8,128)S(1)} %get-tuple-element.48.enter_ref, f32[128,512]{1,0:T(8,128)S(1)} %get-tuple-element.49.slope_top_first_ref, f32[128,512]{1,0:T(8,128)S(1)} %get-tuple-element.50.slope_low_first_ref, ...), custom_call_target="tpu_custom_call" | custom-call | tf_op jit(solution)/shard_map/pallas_call | solution.py:51
  49.5 0.0 collective-permute-done.11.refs_0_
  49.5 2.7 %collective-permute-done.12.refs_1_ = bf16[64,512]{1,0:T(8,128)(2,1)S(1)} collective-permute-done((bf16[64,512]{1,0:T(8,128)(2,1)S(1)}, bf16[64,512]{1,0:T(8,128)(2,1)S(1)}, u32[]{:S(2)}, u32[]{:S(2)}) %collective-permute-start.12) | collective-permute-done | bytes 65568 | tf_op jit(solution)/shard_map/ppermute | solution.py:23
  52.2 0.8 %collective-permute-done.13.refs_2_ = bf16[64,512]{1,0:T(8,128)(2,1)S(1)} collective-permute-done((bf16[64,512]{1,0:T(8,128)(2,1)S(1)}, bf16[64,512]{1,0:T(8,128)(2,1)S(1)}, u32[]{:S(2)}, u32[]{:S(2)}) %collective-permute-start.13) | collective-permute-done | bytes 65568 | tf_op jit(solution)/shard_map/ppermute | solution.py:23
  52.9 0.7 %shard_map.99 = (f32[192,128]{1,0:T(8,128)}, f32[64,128]{1,0:T(8,128)}) custom-call(f32[64,512]{1,0:T(8,128)S(1)} %get-tuple-element.62.keep_ref, bf16[64,512]{1,0:T(8,128)(2,1)S(1)} %collective-permute-done.11.refs_0_, bf16[64,512]{1,0:T(8,128)(2,1)S(1)} %collective-permute-done.12.refs_1_, bf16[64,512]{1,0:T(8,128)(2,1)S(1)} %collective-permute-done.13.refs_2_), custom_call_target="tpu_custom_call" | custom-call | tf_op jit(solution)/shard_map/pallas_call | solution.py:51
  (9 shorter events, 0.0 us)
Async XLA Ops:
  0.6 1.1 %copy-start.2 = (bf16[3,2,2,64,512]{4,3,2,1,0:T(8,128)(2,1)S(1)}, bf16[3,2,2,64,512]{4,3,2,1,0:T(8,128)(2,1)}, u32[]{:S(2)}) copy-start(bf16[3,2,2,64,512]{4,3,2,1,0:T(8,128)(2,1)} %refs_9_.1) | copy-start | bytes 2359300
  1.8 0.9 %copy-start.4 = (bf16[2,2,64,512]{3,2,1,0:T(8,128)(2,1)S(1)}, bf16[2,2,64,512]{3,2,1,0:T(8,128)(2,1)}, u32[]{:S(2)}) copy-start(bf16[2,2,64,512]{3,2,1,0:T(8,128)(2,1)} %refs_8_.1) | copy-start | bytes 786436
  2.7 0.7 %copy-start.9 = (s32[3,2,2,64]{3,2,1,0:T(2,128)S(1)}, s32[3,2,2,64]{3,2,1,0:T(2,128)}, u32[]{:S(2)}) copy-start(s32[3,2,2,64]{3,2,1,0:T(2,128)} %refs_10_.1) | copy-start | bytes 9220
  3.4 5.7 %copy-start.3 = (bf16[3,2,2,64,512]{4,3,2,1,0:T(8,128)(2,1)S(1)}, bf16[3,2,2,64,512]{4,3,2,1,0:T(8,128)(2,1)}, u32[]{:S(2)}) copy-start(bf16[3,2,2,64,512]{4,3,2,1,0:T(8,128)(2,1)} %refs_9_.1) | copy-start | bytes 2359300
  3.4 10.3 %copy-start.6 = (bf16[2,2,64,512]{3,2,1,0:T(8,128)(2,1)S(1)}, bf16[2,2,64,512]{3,2,1,0:T(8,128)(2,1)}, u32[]{:S(2)}) copy-start(bf16[2,2,64,512]{3,2,1,0:T(8,128)(2,1)} %refs_8_.1) | copy-start | bytes 786436
  4.6 8.8 %collective-permute-start = (bf16[272,512]{1,0:T(8,128)(2,1)S(1)}, bf16[272,512]{1,0:T(8,128)(2,1)S(1)}, u32[]{:S(2)}, u32[]{:S(2)}) collective-permute-start(bf16[272,512]{1,0:T(8,128)(2,1)S(1)} %get-tuple-element.42), channel_id=1, source_target_pairs={{0,4},{8,12},{16,20},{24,28},{4,0},{12,8},{20,16},{28,24},{1,5},{9... | collective-permute-start | bytes 835592 | tf_op jit(solution)/shard_map/ppermute | solution.py:18
  5.2 8.3 %collective-permute-start.1 = (bf16[272,512]{1,0:T(8,128)(2,1)S(1)}, bf16[272,512]{1,0:T(8,128)(2,1)S(1)}, u32[]{:S(2)}, u32[]{:S(2)}) collective-permute-start(bf16[272,512]{1,0:T(8,128)(2,1)S(1)} %get-tuple-element.43), channel_id=1, source_target_pairs={{4,8},{12,16},{20,24},{8,4},{16,12},{24,20},{5,9},{13,17},{21,25},... | collective-permute-start | bytes 835592 | tf_op jit(solution)/shard_map/ppermute | solution.py:18
  5.8 7.8 %collective-permute-start.2 = (bf16[272,512]{1,0:T(8,128)(2,1)S(1)}, bf16[272,512]{1,0:T(8,128)(2,1)S(1)}, u32[]{:S(2)}, u32[]{:S(2)}) collective-permute-start(bf16[272,512]{1,0:T(8,128)(2,1)S(1)} %get-tuple-element.44), channel_id=1, source_target_pairs={{0,1},{2,3},{1,0},{3,2},{4,5},{6,7},{5,4},{7,6},{8,9},{10,11},{9,8... | collective-permute-start | bytes 835592 | tf_op jit(solution)/shard_map/ppermute | solution.py:18
  8.5 5.2 %collective-permute-start.3 = (bf16[272,512]{1,0:T(8,128)(2,1)S(1)}, bf16[272,512]{1,0:T(8,128)(2,1)S(1)}, u32[]{:S(2)}, u32[]{:S(2)}) collective-permute-start(bf16[272,512]{1,0:T(8,128)(2,1)S(1)} %get-tuple-element.45), channel_id=1, source_target_pairs={{1,2},{2,1},{5,6},{6,5},{9,10},{10,9},{13,14},{14,13},{17,18},{18,... | collective-permute-start | bytes 835592 | tf_op jit(solution)/shard_map/ppermute | solution.py:18
  9.2 1.4 %copy-start = (bf16[1536,512]{1,0:T(8,128)(2,1)S(1)}, bf16[1536,512]{1,0:T(8,128)(2,1)}, u32[]{:S(2)}) copy-start(bf16[1536,512]{1,0:T(8,128)(2,1)} %weight_ref.3) | copy-start | bytes 4718596
  10.6 0.9 %copy-start.5 = (bf16[2,2,64,512]{3,2,1,0:T(8,128)(2,1)S(1)}, bf16[2,2,64,512]{3,2,1,0:T(8,128)(2,1)}, u32[]{:S(2)}) copy-start(bf16[2,2,64,512]{3,2,1,0:T(8,128)(2,1)} %refs_8_.1) | copy-start | bytes 786436
  11.5 0.7 %copy-start.10 = (s32[3,2,2,64]{3,2,1,0:T(2,128)S(1)}, s32[3,2,2,64]{3,2,1,0:T(2,128)}, u32[]{:S(2)}) copy-start(s32[3,2,2,64]{3,2,1,0:T(2,128)} %refs_10_.1) | copy-start | bytes 9220
  12.2 1.5 %copy-start.1 = (bf16[1536,512]{1,0:T(8,128)(2,1)S(1)}, bf16[1536,512]{1,0:T(8,128)(2,1)}, u32[]{:S(2)}) copy-start(bf16[1536,512]{1,0:T(8,128)(2,1)} %weight_ref.3) | copy-start | bytes 4718596
  12.2 1.5 %copy-start.7 = (bf16[2,2,64,512]{3,2,1,0:T(8,128)(2,1)S(1)}, bf16[2,2,64,512]{3,2,1,0:T(8,128)(2,1)}, u32[]{:S(2)}) copy-start(bf16[2,2,64,512]{3,2,1,0:T(8,128)(2,1)} %cotangent_ref.1) | copy-start | bytes 786436
  12.2 1.6 %copy-start.8 = (bf16[512,512]{1,0:T(8,128)(2,1)S(1)}, bf16[512,512]{1,0:T(8,128)(2,1)}, u32[]{:S(2)}) copy-start(bf16[512,512]{1,0:T(8,128)(2,1)} %refs_7_.1) | copy-start | bytes 1572868
  18.0 5.0 %collective-permute-start.4 = (bf16[1152,512]{1,0:T(8,128)(2,1)S(1)}, bf16[1152,512]{1,0:T(8,128)(2,1)S(1)}, u32[]{:S(2)}, u32[]{:S(2)}) collective-permute-start(bf16[1152,512]{1,0:T(8,128)(2,1)S(1)} %get-tuple-element.53), channel_id=1, source_target_pairs={{0,4},{8,12},{16,20},{24,28},{4,0},{12,8},{20,16},{28,24},{1,5},{9... | collective-permute-start | bytes 3538952 | tf_op jit(solution)/shard_map/ppermute | solution.py:18
  23.2 10.7 %collective-permute-start.8 = (bf16[256,512]{1,0:T(8,128)(2,1)S(1)}, bf16[256,512]{1,0:T(8,128)(2,1)S(1)}, u32[]{:S(2)}, u32[]{:S(2)}) collective-permute-start(bf16[256,512]{1,0:T(8,128)(2,1)S(1)} %get-tuple-element.59), channel_id=1, source_target_pairs={{0,8},{4,12},{8,0},{12,4},{16,24},{20,28},{24,16},{28,20},{1,9},{5... | collective-permute-start | bytes 786440 | tf_op jit(solution)/shard_map/ppermute | solution.py:23
  26.3 13.6 %collective-permute-start.9 = (bf16[256,512]{1,0:T(8,128)(2,1)S(1)}, bf16[256,512]{1,0:T(8,128)(2,1)S(1)}, u32[]{:S(2)}, u32[]{:S(2)}) collective-permute-start(bf16[256,512]{1,0:T(8,128)(2,1)S(1)} %get-tuple-element.60), channel_id=1, source_target_pairs={{0,16},{4,20},{8,24},{12,28},{16,0},{20,4},{24,8},{28,12},{1,17},{... | collective-permute-start | bytes 786440 | tf_op jit(solution)/shard_map/ppermute | solution.py:23
  27.3 13.3 %collective-permute-start.10 = (bf16[256,512]{1,0:T(8,128)(2,1)S(1)}, bf16[256,512]{1,0:T(8,128)(2,1)S(1)}, u32[]{:S(2)}, u32[]{:S(2)}) collective-permute-start(bf16[256,512]{1,0:T(8,128)(2,1)S(1)} %get-tuple-element.61), channel_id=1, source_target_pairs={{0,24},{4,28},{8,16},{12,20},{16,8},{20,12},{24,0},{28,4},{1,25},{... | collective-permute-start | bytes 786440 | tf_op jit(solution)/shard_map/ppermute | solution.py:23
  28.7 18.2 %collective-permute-start.5 = (bf16[128,512]{1,0:T(8,128)(2,1)S(1)}, bf16[128,512]{1,0:T(8,128)(2,1)S(1)}, u32[]{:S(2)}, u32[]{:S(2)}) collective-permute-start(bf16[128,512]{1,0:T(8,128)(2,1)S(1)} %get-tuple-element.54), channel_id=1, source_target_pairs={{4,8},{12,16},{20,24},{8,4},{16,12},{24,20},{5,9},{13,17},{21,25},... | collective-permute-start | bytes 393224 | tf_op jit(solution)/shard_map/ppermute | solution.py:18
  29.3 18.9 %collective-permute-start.6 = (bf16[128,512]{1,0:T(8,128)(2,1)S(1)}, bf16[128,512]{1,0:T(8,128)(2,1)S(1)}, u32[]{:S(2)}, u32[]{:S(2)}) collective-permute-start(bf16[128,512]{1,0:T(8,128)(2,1)S(1)} %get-tuple-element.55), channel_id=1, source_target_pairs={{0,1},{2,3},{1,0},{3,2},{4,5},{6,7},{5,4},{7,6},{8,9},{10,11},{9,8... | collective-permute-start | bytes 393224 | tf_op jit(solution)/shard_map/ppermute | solution.py:18
  34.0 14.3 %collective-permute-start.7 = (bf16[128,512]{1,0:T(8,128)(2,1)S(1)}, bf16[128,512]{1,0:T(8,128)(2,1)S(1)}, u32[]{:S(2)}, u32[]{:S(2)}) collective-permute-start(bf16[128,512]{1,0:T(8,128)(2,1)S(1)} %get-tuple-element.56), channel_id=1, source_target_pairs={{1,2},{2,1},{5,6},{6,5},{9,10},{10,9},{13,14},{14,13},{17,18},{18,... | collective-permute-start | bytes 393224 | tf_op jit(solution)/shard_map/ppermute | solution.py:18
  40.7 8.8 %collective-permute-start.11 = (bf16[64,512]{1,0:T(8,128)(2,1)S(1)}, bf16[64,512]{1,0:T(8,128)(2,1)S(1)}, u32[]{:S(2)}, u32[]{:S(2)}) collective-permute-start(bf16[64,512]{1,0:T(8,128)(2,1)S(1)} %get-tuple-element.63), channel_id=1, source_target_pairs={{0,1},{1,0},{2,3},{3,2},{4,5},{5,4},{6,7},{7,6},{8,9},{9,8},{10,11... | collective-permute-start | bytes 196616 | tf_op jit(solution)/shard_map/ppermute | solution.py:23
  45.6 6.6 %collective-permute-start.12 = (bf16[64,512]{1,0:T(8,128)(2,1)S(1)}, bf16[64,512]{1,0:T(8,128)(2,1)S(1)}, u32[]{:S(2)}, u32[]{:S(2)}) collective-permute-start(bf16[64,512]{1,0:T(8,128)(2,1)S(1)} %get-tuple-element.64), channel_id=1, source_target_pairs={{0,2},{1,3},{2,0},{3,1},{4,6},{5,7},{6,4},{7,5},{8,10},{9,11},{10,... | collective-permute-start | bytes 196616 | tf_op jit(solution)/shard_map/ppermute | solution.py:23
  46.9 6.1 %collective-permute-start.13 = (bf16[64,512]{1,0:T(8,128)(2,1)S(1)}, bf16[64,512]{1,0:T(8,128)(2,1)S(1)}, u32[]{:S(2)}, u32[]{:S(2)}) collective-permute-start(bf16[64,512]{1,0:T(8,128)(2,1)S(1)} %get-tuple-element.65), channel_id=1, source_target_pairs={{0,3},{1,2},{2,1},{3,0},{4,7},{5,6},{6,5},{7,4},{8,11},{9,10},{10,... | collective-permute-start | bytes 196616 | tf_op jit(solution)/shard_map/ppermute | solution.py:23

commit v4 on v3

--- a/solution.py
+++ b/solution.py
@@ -48,10 +48,11 @@
 
 
 def call(kernel, outs, args, scratch=(), limit=4 << 20, cost=None, far=0):
+    args = [pltpu.with_memory_space_constraint(arg, pltpu.HBM) for arg in args[:far]] + list(args[far:])
     return pl.pallas_call(
         kernel,
         out_shape=[jax.ShapeDtypeStruct(shape, dtype) for shape, dtype in outs],
-        in_specs=[pl.BlockSpec(memory_space=pl.ANY)] * far + [pl.BlockSpec(memory_space=pltpu.VMEM)] * (len(args) - far),
+        in_specs=[pl.BlockSpec(memory_space=pltpu.HBM)] * far + [pl.BlockSpec(memory_space=pltpu.VMEM)] * (len(args) - far),
         out_specs=[pl.BlockSpec(memory_space=pltpu.VMEM)] * len(outs),
         scratch_shapes=list(scratch),
         compiler_params=pltpu.CompilerParams(vmem_limit_bytes=limit),
@@ -72,9 +73,11 @@
 
 
 def pack_kernel(
-    dims, node_ref, edge_ref, open_ref, pair_first_ref, odd_first_ref, pair_second_ref, odd_second_ref, sems
+    dims, node_ref, edge_ref, faces_ref, pair_first_ref, odd_first_ref, pair_second_ref, odd_second_ref, open_ref, sems
 ):
     ex, ey, nz, _ = dims
+    faces_copy = pltpu.make_async_copy(faces_ref, open_ref, sems.at[0])
+    faces_copy.start()
 
     def upward(ref, direction, cells):
         pairs = []
@@ -86,7 +89,7 @@
     def downward(ref, cells):
         return [(node_ref.at[x, y], ref.at[pl.ds(index * nz, nz)]) for index, (x, y) in enumerate(cells)]
 
-    plans, used = [], 0
+    plans, used = [], 1
     for direction, axis, pair_ref, odd_ref, top, low in (
         (1, "gy", pair_second_ref, odd_second_ref, [(x, ey - 1) for x in range(ex)], [(x, 0) for x in range(ex)]),
         (0, "gx", pair_first_ref, odd_first_ref, [(ex - 1, y) for y in range(ey)], [(0, y) for y in range(ey)]),
@@ -97,15 +100,16 @@
             for pairs in choices
         ]
         used += len(copies[0])
-        mask = spread_rows([open_ref[direction, x, y : y + 1].astype(F32) for x, y in top], PAD).astype(BF16)
-        plans.append((is_even(axis), copies, (pair_ref, odd_ref), 2 * len(top) * nz, mask))
-    for even, copies, refs, start, mask in plans:
+        plans.append((is_even(axis), copies, (pair_ref, odd_ref), 2 * len(top) * nz, (direction, top)))
+    for even, copies, _, _, _ in plans:
         for wanted, group in ((even, copies[0]), (jnp.logical_not(even), copies[1])):
             @pl.when(wanted)
             def _():
                 for copy in group:
                     copy.start()
-    for even, copies, refs, start, mask in plans:
+    faces_copy.wait()
+    for even, copies, refs, start, (direction, top) in plans:
+        mask = spread_rows([open_ref[direction, x, y : y + 1].astype(F32) for x, y in top], PAD).astype(BF16)
         for ref in refs:
             ref[start:, :nz] = mask
         for wanted, group in ((even, copies[0]), (jnp.logical_not(even), copies[1])):
@@ -135,11 +139,19 @@
 
 
 def before_kernel(
-    dims, node_ref, edge_ref, open_ref, weight_ref,
+    dims, node_ref, edge_ref, weight_ref, faces_ref,
     sum_ref, slope_ref, stored_top_first_ref, other_low_first_ref, stored_top_second_ref, other_low_second_ref,
-    other_ref, stored_ref, message_ref,
+    other_ref, stored_ref, message_ref, node_here, edge_here, weight_here, open_ref, sems,
 ):
     ex, ey, nz, features = dims
+    copies = [
+        pltpu.make_async_copy(node_ref, node_here, sems.at[0]),
+        pltpu.make_async_copy(weight_ref, weight_here, sems.at[1]),
+        pltpu.make_async_copy(edge_ref, edge_here, sems.at[2]),
+        pltpu.make_async_copy(faces_ref, open_ref, sems.at[3]),
+    ]
+    for copy in copies:
+        copy.start()
 
     def rows(x, y):
         return slice((x * ey + y) * nz, (x * ey + y + 1) * nz)
@@ -147,11 +159,15 @@
     def part(index):
         return slice(index * nz, (index + 1) * nz)
 
-    node = node_ref[...].reshape(-1, features)
-    own = dot(node, weight_ref[:features])
-    other_ref[...] = dot(node, weight_ref[features : 2 * features])
+    copies[0].wait()
+    copies[1].wait()
+    node = node_here[...].reshape(-1, features)
+    own = dot(node, weight_here[:features])
+    other_ref[...] = dot(node, weight_here[features : 2 * features])
+    copies[2].wait()
+    copies[3].wait()
     for direction in range(3):
-        stored_ref[direction] = own + dot(edge_ref[direction].reshape(-1, features), weight_ref[2 * features :])
+        stored_ref[direction] = own + dot(edge_here[direction].reshape(-1, features), weight_here[2 * features :])
     inside_third = jnp.where(lax.broadcasted_iota(jnp.int32, (nz, 1), 0) < nz - 1, 1.0, 0.0)
     for y in range(ey):
         stored_top_first_ref[part(y)] = stored_ref[0, rows(ex - 1, y)]
@@ -417,13 +433,13 @@
 
     face_first, face_second = (ey * nz, features), (ex * nz, features)
     packed_first, packed_second = (2 * ey * nz + PAD, features), (2 * ex * nz + PAD, features)
-    copies = 3 * (ex + ey)
+    copies = 3 * (ex + ey) + 1
     pair_first, odd_first, pair_second, odd_second = call(
         functools.partial(pack_kernel, dims),
         [(packed_first, BF16)] * 2 + [(packed_second, BF16)] * 2,
         [node_features, edge_features, open_faces],
-        scratch=[pltpu.SemaphoreType.DMA((copies,))],
-        far=2,
+        scratch=[pltpu.VMEM(open_faces.shape, jnp.int32), pltpu.SemaphoreType.DMA((copies,))],
+        far=3,
     )
     pair_second = swapped(pair_second, "gy", 0)
     odd_second = swapped(odd_second, "gy", 1)
@@ -433,13 +449,19 @@
     before = call(
         functools.partial(before_kernel, dims),
         before,
-        [node_features, edge_features, open_faces, edge_weight],
+        [node_features, edge_features, edge_weight, open_faces],
         scratch=[
             pltpu.VMEM((count, features), F32),
             pltpu.VMEM((3, count, features), F32),
             pltpu.VMEM((3, count, features), F32),
+            pltpu.VMEM(node_features.shape, BF16),
+            pltpu.VMEM(edge_features.shape, BF16),
+            pltpu.VMEM(edge_weight.shape, BF16),
+            pltpu.VMEM(open_faces.shape, jnp.int32),
+            pltpu.SemaphoreType.DMA((4,)),
         ],
         limit=12 << 20,
+        far=4,
     )
     total_rows = 4 * features
     chunk = total_rows // devices

time: 54 us -> 51.4 us (0.952)
  local copies, waits for them, and re-layouts: 5.94 us -> 0.03 us
  Pallas kernels: 8.76 us -> 10.7 us
  waiting for transfers between devices: 12.1 us -> 13.4 us
    unnamed x22 -> x12, local copies, waits for them, and re-layouts: 5.94 us -> 0.03 us
    pallas_call x7, Pallas kernels: 8.76 us -> 10.7 us  [call(): pl.pallas_call(kernel, out_shape=[jax.ShapeDtypeStruct(shape, dtype) for...]
    ppermute x8, waiting for transfers between devices: 2.73 us -> 4.04 us  [swapped(): lax.ppermute(value, axis, [(at, at + 1) for at in lower] + [(at + 1, at)...]
  transfers between devices with their start and end apart: 14 -> 14, of which waited for: 6 -> 6; matrix products, arithmetic and copies ran while one was open for 0% -> 0% of each run, Pallas kernels for 5% -> 8%
where the time goes in v4:
time: 51.4 us; the launch traced here: 51.2 us
  starting transfers between devices  26.3 us (51%)
  waiting for transfers between devices  13.4 us (26%)
  Pallas kernels  10.7 us (21%)
  between operations  0.8 us (2%)
    ppermute x6, starting transfers between devices, exchanged(): lax.ppermute(value, axis, [(source, source ^ flip) for source in range(co...  13.3 us
    ppermute x8, starting transfers between devices, swapped(): lax.ppermute(value, axis, [(at, at + 1) for at in lower] + [(at + 1, at)...  13 us
    pallas_call x7, Pallas kernels, call(): pl.pallas_call(kernel, out_shape=[jax.ShapeDtypeStruct(shape, dtype) for...  10.7 us
    ppermute x6, waiting for transfers between devices, exchanged(): lax.ppermute(value, axis, [(source, source ^ flip) for source in range(co...  9.38 us
    ppermute x8, waiting for transfers between devices, swapped(): lax.ppermute(value, axis, [(at, at + 1) for at in lower] + [(at + 1, at)...  4.04 us
  transfers between devices with their start and end apart: 14, of which 6 were waited for; matrix products, arithmetic and copies ran while one was open for 0% of the time, Pallas kernels for 8%

profile of v4, /device:TPU:0, one launch (start us, length us, event | category | flops | bytes accessed | tf_op | source)
XLA Modules:
  0.0 51.2 jit_solution(7906818529221475707)
XLA Ops:
  0.6 0.0 copy-start.3
  0.6 0.0 copy-start.4
  0.7 1.4 %shard_map.94 = (bf16[272,512]{1,0:T(8,128)(2,1)S(1)}, bf16[272,512]{1,0:T(8,128)(2,1)S(1)}, bf16[272,512]{1,0:T(8,128)(2,1)S(1)}, bf16[272,512]{1,0:T(8,128)(2,1)S(1)}) custom-call(bf16[2,2,64,512]{3,2,1,0:T(8,128)(2,1)} %refs_8_.1, bf16[3,2,2,64,512]{4,3,2,1,0:T(8,128)(2,1)} %refs_9_.1, s32[3,2,2,64]{3,2,1,0:T(2,128)} %refs_10_.1), custom_call_target="tpu_custom_call" | custom-call | tf_op jit(solution)/shard_map/pallas_call | solution.py:52
  2.0 0.0 copy-start
  2.0 0.0 copy-start.1
  2.0 0.0 copy-start.2
  2.0 0.0 copy-start.5
  2.1 0.6 %collective-permute-start = (bf16[272,512]{1,0:T(8,128)(2,1)S(1)}, bf16[272,512]{1,0:T(8,128)(2,1)S(1)}, u32[]{:S(2)}, u32[]{:S(2)}) collective-permute-start(bf16[272,512]{1,0:T(8,128)(2,1)S(1)} %get-tuple-element.42), channel_id=1, source_target_pairs={{0,4},{8,12},{16,20},{24,28},{4,0},{12,8},{20,16},{28,24},{1,5},{9... | collective-permute-start | bytes 835592 | tf_op jit(solution)/shard_map/ppermute | solution.py:18
  2.6 0.8 %collective-permute-start.1 = (bf16[272,512]{1,0:T(8,128)(2,1)S(1)}, bf16[272,512]{1,0:T(8,128)(2,1)S(1)}, u32[]{:S(2)}, u32[]{:S(2)}) collective-permute-start(bf16[272,512]{1,0:T(8,128)(2,1)S(1)} %get-tuple-element.43), channel_id=1, source_target_pairs={{4,8},{12,16},{20,24},{8,4},{16,12},{24,20},{5,9},{13,17},{21,25},... | collective-permute-start | bytes 835592 | tf_op jit(solution)/shard_map/ppermute | solution.py:18
  3.4 2.6 %collective-permute-start.2 = (bf16[272,512]{1,0:T(8,128)(2,1)S(1)}, bf16[272,512]{1,0:T(8,128)(2,1)S(1)}, u32[]{:S(2)}, u32[]{:S(2)}) collective-permute-start(bf16[272,512]{1,0:T(8,128)(2,1)S(1)} %get-tuple-element.44), channel_id=1, source_target_pairs={{0,1},{2,3},{1,0},{3,2},{4,5},{6,7},{5,4},{7,6},{8,9},{10,11},{9,8... | collective-permute-start | bytes 835592 | tf_op jit(solution)/shard_map/ppermute | solution.py:18
  6.1 0.7 %collective-permute-start.3 = (bf16[272,512]{1,0:T(8,128)(2,1)S(1)}, bf16[272,512]{1,0:T(8,128)(2,1)S(1)}, u32[]{:S(2)}, u32[]{:S(2)}) collective-permute-start(bf16[272,512]{1,0:T(8,128)(2,1)S(1)} %get-tuple-element.45), channel_id=1, source_target_pairs={{1,2},{2,1},{5,6},{6,5},{9,10},{10,9},{13,14},{14,13},{17,18},{18,... | collective-permute-start | bytes 835592 | tf_op jit(solution)/shard_map/ppermute | solution.py:18
  6.7 2.9 %shard_map.93 = (f32[256,512]{1,0:T(8,128)S(1)}, f32[3,256,512]{2,1,0:T(8,128)S(1)}, f32[128,512]{1,0:T(8,128)S(1)}, f32[128,512]{1,0:T(8,128)S(1)}, f32[128,512]{1,0:T(8,128)S(1)}, /*index=5*/f32[128,512]{1,0:T(8,128)S(1)}) custom-call(bf16[2,2,64,512]{3,2,1,0:T(8,128)(2,1)} %refs_8_.1, bf16[3,2,2,64,512]{4,3,2,1,0:T(8,128)(2,1)} %refs_9_.1, ...), custom_call_target="tpu_custom_call" | custom-call | tf_op jit(solution)/shard_map/pallas_call | solution.py:52
  9.7 0.0 collective-permute-done.refs_12_
  9.7 0.0 collective-permute-done.1.refs_13_
  9.7 1.5 %collective-permute-done.2.refs_14_ = bf16[272,512]{1,0:T(8,128)(2,1)S(1)} collective-permute-done((bf16[272,512]{1,0:T(8,128)(2,1)S(1)}, bf16[272,512]{1,0:T(8,128)(2,1)S(1)}, u32[]{:S(2)}, u32[]{:S(2)}) %collective-permute-start.2) | collective-permute-done | bytes 278560 | tf_op jit(solution)/shard_map/ppermute | solution.py:18
  11.3 0.0 collective-permute-done.3.refs_15_
  11.3 0.0 copy-done.3
  11.3 0.0 copy-done.4
  11.3 0.0 copy-done
  11.3 0.0 copy-done.1
  11.3 0.0 copy-done.2
  11.3 0.0 copy-done.5
  11.3 4.1 %shard_map.95 = (bf16[2,2,64,512]{3,2,1,0:T(8,128)(2,1)}, bf16[128,512]{1,0:T(8,128)(2,1)S(1)}, bf16[128,512]{1,0:T(8,128)(2,1)S(1)}, bf16[128,512]{1,0:T(8,128)...) custom-call(f32[256,512]{1,0:T(8,128)S(1)} %get-tuple-element.36.ref, ...), custom_call_target="tpu_custom_call" | custom-call | tf_op jit(solution)/shard_map/pallas_call | solution.py:52
  15.5 2.3 %collective-permute-start.4 = (bf16[1152,512]{1,0:T(8,128)(2,1)S(1)}, bf16[1152,512]{1,0:T(8,128)(2,1)S(1)}, u32[]{:S(2)}, u32[]{:S(2)}) collective-permute-start(bf16[1152,512]{1,0:T(8,128)(2,1)S(1)} %get-tuple-element.53), channel_id=1, source_target_pairs={{0,4},{8,12},{16,20},{24,28},{4,0},{12,8},{20,16},{28,24},{1,5},{9... | collective-permute-start | bytes 3538952 | tf_op jit(solution)/shard_map/ppermute | solution.py:18
  17.8 2.5 %collective-permute-done.4.pair_first_ref.received_ref = bf16[1152,512]{1,0:T(8,128)(2,1)S(1)} collective-permute-done((bf16[1152,512]{1,0:T(8,128)(2,1)S(1)}, bf16[1152,512]{1,0:T(8,128)(2,1)S(1)}, u32[]{:S(2)}, u32[]{:S(2)}) %collective-permute-start.4) | collective-permute-done | bytes 1179680 | tf_op jit(solution)/shard_map/ppermute | solution.py:18
  20.3 0.2 shard_map.97
  20.5 3.4 %collective-permute-start.8 = (bf16[256,512]{1,0:T(8,128)(2,1)S(1)}, bf16[256,512]{1,0:T(8,128)(2,1)S(1)}, u32[]{:S(2)}, u32[]{:S(2)}) collective-permute-start(bf16[256,512]{1,0:T(8,128)(2,1)S(1)} %get-tuple-element.59), channel_id=1, source_target_pairs={{0,8},{4,12},{8,0},{12,4},{16,24},{20,28},{24,16},{28,20},{1,9},{5... | collective-permute-start | bytes 786440 | tf_op jit(solution)/shard_map/ppermute | solution.py:23
  23.8 1.0 %collective-permute-start.9 = (bf16[256,512]{1,0:T(8,128)(2,1)S(1)}, bf16[256,512]{1,0:T(8,128)(2,1)S(1)}, u32[]{:S(2)}, u32[]{:S(2)}) collective-permute-start(bf16[256,512]{1,0:T(8,128)(2,1)S(1)} %get-tuple-element.60), channel_id=1, source_target_pairs={{0,16},{4,20},{8,24},{12,28},{16,0},{20,4},{24,8},{28,12},{1,17},{... | collective-permute-start | bytes 786440 | tf_op jit(solution)/shard_map/ppermute | solution.py:23
  24.8 1.4 %collective-permute-start.10 = (bf16[256,512]{1,0:T(8,128)(2,1)S(1)}, bf16[256,512]{1,0:T(8,128)(2,1)S(1)}, u32[]{:S(2)}, u32[]{:S(2)}) collective-permute-start(bf16[256,512]{1,0:T(8,128)(2,1)S(1)} %get-tuple-element.61), channel_id=1, source_target_pairs={{0,24},{4,28},{8,16},{12,20},{16,8},{20,12},{24,0},{28,4},{1,25},{... | collective-permute-start | bytes 786440 | tf_op jit(solution)/shard_map/ppermute | solution.py:23
  26.2 0.7 %collective-permute-start.5 = (bf16[128,512]{1,0:T(8,128)(2,1)S(1)}, bf16[128,512]{1,0:T(8,128)(2,1)S(1)}, u32[]{:S(2)}, u32[]{:S(2)}) collective-permute-start(bf16[128,512]{1,0:T(8,128)(2,1)S(1)} %get-tuple-element.54), channel_id=1, source_target_pairs={{4,8},{12,16},{20,24},{8,4},{16,12},{24,20},{5,9},{13,17},{21,25},... | collective-permute-start | bytes 393224 | tf_op jit(solution)/shard_map/ppermute | solution.py:18
  26.9 4.7 %collective-permute-start.6 = (bf16[128,512]{1,0:T(8,128)(2,1)S(1)}, bf16[128,512]{1,0:T(8,128)(2,1)S(1)}, u32[]{:S(2)}, u32[]{:S(2)}) collective-permute-start(bf16[128,512]{1,0:T(8,128)(2,1)S(1)} %get-tuple-element.55), channel_id=1, source_target_pairs={{0,1},{2,3},{1,0},{3,2},{4,5},{6,7},{5,4},{7,6},{8,9},{10,11},{9,8... | collective-permute-start | bytes 393224 | tf_op jit(solution)/shard_map/ppermute | solution.py:18
  31.6 0.0 collective-permute-done.8.refs_0_
  31.6 0.7 %collective-permute-start.7 = (bf16[128,512]{1,0:T(8,128)(2,1)S(1)}, bf16[128,512]{1,0:T(8,128)(2,1)S(1)}, u32[]{:S(2)}, u32[]{:S(2)}) collective-permute-start(bf16[128,512]{1,0:T(8,128)(2,1)S(1)} %get-tuple-element.56), channel_id=1, source_target_pairs={{1,2},{2,1},{5,6},{6,5},{9,10},{10,9},{13,14},{14,13},{17,18},{18,... | collective-permute-start | bytes 393224 | tf_op jit(solution)/shard_map/ppermute | solution.py:18
  32.2 5.2 %collective-permute-done.9.refs_1_ = bf16[256,512]{1,0:T(8,128)(2,1)S(1)} collective-permute-done((bf16[256,512]{1,0:T(8,128)(2,1)S(1)}, bf16[256,512]{1,0:T(8,128)(2,1)S(1)}, u32[]{:S(2)}, u32[]{:S(2)}) %collective-permute-start.9) | collective-permute-done | bytes 262176 | tf_op jit(solution)/shard_map/ppermute | solution.py:23
  37.5 0.7 %collective-permute-done.10.refs_2_ = bf16[256,512]{1,0:T(8,128)(2,1)S(1)} collective-permute-done((bf16[256,512]{1,0:T(8,128)(2,1)S(1)}, bf16[256,512]{1,0:T(8,128)(2,1)S(1)}, u32[]{:S(2)}, u32[]{:S(2)}) %collective-permute-start.10) | collective-permute-done | bytes 262176 | tf_op jit(solution)/shard_map/ppermute | solution.py:23
  38.2 0.1 shard_map.98
  38.3 4.9 %collective-permute-start.11 = (bf16[64,512]{1,0:T(8,128)(2,1)S(1)}, bf16[64,512]{1,0:T(8,128)(2,1)S(1)}, u32[]{:S(2)}, u32[]{:S(2)}) collective-permute-start(bf16[64,512]{1,0:T(8,128)(2,1)S(1)} %get-tuple-element.63), channel_id=1, source_target_pairs={{0,1},{1,0},{2,3},{3,2},{4,5},{5,4},{6,7},{7,6},{8,9},{9,8},{10,11... | collective-permute-start | bytes 196616 | tf_op jit(solution)/shard_map/ppermute | solution.py:23
  43.2 1.3 %collective-permute-start.12 = (bf16[64,512]{1,0:T(8,128)(2,1)S(1)}, bf16[64,512]{1,0:T(8,128)(2,1)S(1)}, u32[]{:S(2)}, u32[]{:S(2)}) collective-permute-start(bf16[64,512]{1,0:T(8,128)(2,1)S(1)} %get-tuple-element.64), channel_id=1, source_target_pairs={{0,2},{1,3},{2,0},{3,1},{4,6},{5,7},{6,4},{7,5},{8,10},{9,11},{10,... | collective-permute-start | bytes 196616 | tf_op jit(solution)/shard_map/ppermute | solution.py:23
  44.5 0.0 collective-permute-done.5.odd_first_ref
  44.5 1.4 %collective-permute-start.13 = (bf16[64,512]{1,0:T(8,128)(2,1)S(1)}, bf16[64,512]{1,0:T(8,128)(2,1)S(1)}, u32[]{:S(2)}, u32[]{:S(2)}) collective-permute-start(bf16[64,512]{1,0:T(8,128)(2,1)S(1)} %get-tuple-element.65), channel_id=1, source_target_pairs={{0,3},{1,2},{2,1},{3,0},{4,7},{5,6},{6,5},{7,4},{8,11},{9,10},{10,... | collective-permute-start | bytes 196616 | tf_op jit(solution)/shard_map/ppermute | solution.py:23
  45.8 0.0 collective-permute-done.6.pair_second_ref
  45.8 0.0 collective-permute-done.7.odd_second_ref
  45.8 1.2 %shard_map.96 = bf16[2,2,64,512]{3,2,1,0:T(8,128)(2,1)} custom-call(f32[256,512]{1,0:T(8,128)S(1)} %get-tuple-element.47.own_ref, f32[256,512]{1,0:T(8,128)S(1)} %get-tuple-element.48.enter_ref, f32[128,512]{1,0:T(8,128)S(1)} %get-tuple-element.49.slope_top_first_ref, f32[128,512]{1,0:T(8,128)S(1)} %get-tuple-element.50.slope_low_first_ref, ...), custom_call_target="tpu_custom_call" | custom-call | tf_op jit(solution)/shard_map/pallas_call | solution.py:52
  47.1 0.0 collective-permute-done.11.refs_0_
  47.1 2.7 %collective-permute-done.12.refs_1_ = bf16[64,512]{1,0:T(8,128)(2,1)S(1)} collective-permute-done((bf16[64,512]{1,0:T(8,128)(2,1)S(1)}, bf16[64,512]{1,0:T(8,128)(2,1)S(1)}, u32[]{:S(2)}, u32[]{:S(2)}) %collective-permute-start.12) | collective-permute-done | bytes 65568 | tf_op jit(solution)/shard_map/ppermute | solution.py:23
  49.7 0.8 %collective-permute-done.13.refs_2_ = bf16[64,512]{1,0:T(8,128)(2,1)S(1)} collective-permute-done((bf16[64,512]{1,0:T(8,128)(2,1)S(1)}, bf16[64,512]{1,0:T(8,128)(2,1)S(1)}, u32[]{:S(2)}, u32[]{:S(2)}) %collective-permute-start.13) | collective-permute-done | bytes 65568 | tf_op jit(solution)/shard_map/ppermute | solution.py:23
  50.5 0.7 %shard_map.99 = (f32[192,128]{1,0:T(8,128)}, f32[64,128]{1,0:T(8,128)}) custom-call(f32[64,512]{1,0:T(8,128)S(1)} %get-tuple-element.62.keep_ref, bf16[64,512]{1,0:T(8,128)(2,1)S(1)} %collective-permute-done.11.refs_0_, bf16[64,512]{1,0:T(8,128)(2,1)S(1)} %collective-permute-done.12.refs_1_, bf16[64,512]{1,0:T(8,128)(2,1)S(1)} %collective-permute-done.13.refs_2_), custom_call_target="tpu_custom_call" | custom-call | tf_op jit(solution)/shard_map/pallas_call | solution.py:52
Async XLA Ops:
  0.6 10.6 %copy-start.3 = (bf16[2,2,64,512]{3,2,1,0:T(8,128)(2,1)S(1)}, bf16[2,2,64,512]{3,2,1,0:T(8,128)(2,1)}, u32[]{:S(2)}) copy-start(bf16[2,2,64,512]{3,2,1,0:T(8,128)(2,1)} %cotangent_ref.1) | copy-start | bytes 786436
  0.6 10.6 %copy-start.4 = (bf16[512,512]{1,0:T(8,128)(2,1)S(1)}, bf16[512,512]{1,0:T(8,128)(2,1)}, u32[]{:S(2)}) copy-start(bf16[512,512]{1,0:T(8,128)(2,1)} %refs_7_.1) | copy-start | bytes 1572868
  2.0 9.3 %copy-start = (bf16[1536,512]{1,0:T(8,128)(2,1)S(1)}, bf16[1536,512]{1,0:T(8,128)(2,1)}, u32[]{:S(2)}) copy-start(bf16[1536,512]{1,0:T(8,128)(2,1)} %weight_ref.3) | copy-start | bytes 4718596
  2.0 9.3 %copy-start.1 = (bf16[3,2,2,64,512]{4,3,2,1,0:T(8,128)(2,1)S(1)}, bf16[3,2,2,64,512]{4,3,2,1,0:T(8,128)(2,1)}, u32[]{:S(2)}) copy-start(bf16[3,2,2,64,512]{4,3,2,1,0:T(8,128)(2,1)} %refs_9_.1) | copy-start | bytes 2359300
  2.0 9.3 %copy-start.2 = (bf16[2,2,64,512]{3,2,1,0:T(8,128)(2,1)S(1)}, bf16[2,2,64,512]{3,2,1,0:T(8,128)(2,1)}, u32[]{:S(2)}) copy-start(bf16[2,2,64,512]{3,2,1,0:T(8,128)(2,1)} %refs_8_.1) | copy-start | bytes 786436
  2.0 9.3 %copy-start.5 = (s32[3,2,2,64]{3,2,1,0:T(2,128)S(1)}, s32[3,2,2,64]{3,2,1,0:T(2,128)}, u32[]{:S(2)}) copy-start(s32[3,2,2,64]{3,2,1,0:T(2,128)} %refs_10_.1) | copy-start | bytes 9220
  2.1 7.6 %collective-permute-start = (bf16[272,512]{1,0:T(8,128)(2,1)S(1)}, bf16[272,512]{1,0:T(8,128)(2,1)S(1)}, u32[]{:S(2)}, u32[]{:S(2)}) collective-permute-start(bf16[272,512]{1,0:T(8,128)(2,1)S(1)} %get-tuple-element.42), channel_id=1, source_target_pairs={{0,4},{8,12},{16,20},{24,28},{4,0},{12,8},{20,16},{28,24},{1,5},{9... | collective-permute-start | bytes 835592 | tf_op jit(solution)/shard_map/ppermute | solution.py:18
  2.6 7.1 %collective-permute-start.1 = (bf16[272,512]{1,0:T(8,128)(2,1)S(1)}, bf16[272,512]{1,0:T(8,128)(2,1)S(1)}, u32[]{:S(2)}, u32[]{:S(2)}) collective-permute-start(bf16[272,512]{1,0:T(8,128)(2,1)S(1)} %get-tuple-element.43), channel_id=1, source_target_pairs={{4,8},{12,16},{20,24},{8,4},{16,12},{24,20},{5,9},{13,17},{21,25},... | collective-permute-start | bytes 835592 | tf_op jit(solution)/shard_map/ppermute | solution.py:18
  3.4 7.8 %collective-permute-start.2 = (bf16[272,512]{1,0:T(8,128)(2,1)S(1)}, bf16[272,512]{1,0:T(8,128)(2,1)S(1)}, u32[]{:S(2)}, u32[]{:S(2)}) collective-permute-start(bf16[272,512]{1,0:T(8,128)(2,1)S(1)} %get-tuple-element.44), channel_id=1, source_target_pairs={{0,1},{2,3},{1,0},{3,2},{4,5},{6,7},{5,4},{7,6},{8,9},{10,11},{9,8... | collective-permute-start | bytes 835592 | tf_op jit(solution)/shard_map/ppermute | solution.py:18
  6.1 5.2 %collective-permute-start.3 = (bf16[272,512]{1,0:T(8,128)(2,1)S(1)}, bf16[272,512]{1,0:T(8,128)(2,1)S(1)}, u32[]{:S(2)}, u32[]{:S(2)}) collective-permute-start(bf16[272,512]{1,0:T(8,128)(2,1)S(1)} %get-tuple-element.45), channel_id=1, source_target_pairs={{1,2},{2,1},{5,6},{6,5},{9,10},{10,9},{13,14},{14,13},{17,18},{18,... | collective-permute-start | bytes 835592 | tf_op jit(solution)/shard_map/ppermute | solution.py:18
  15.5 4.8 %collective-permute-start.4 = (bf16[1152,512]{1,0:T(8,128)(2,1)S(1)}, bf16[1152,512]{1,0:T(8,128)(2,1)S(1)}, u32[]{:S(2)}, u32[]{:S(2)}) collective-permute-start(bf16[1152,512]{1,0:T(8,128)(2,1)S(1)} %get-tuple-element.53), channel_id=1, source_target_pairs={{0,4},{8,12},{16,20},{24,28},{4,0},{12,8},{20,16},{28,24},{1,5},{9... | collective-permute-start | bytes 3538952 | tf_op jit(solution)/shard_map/ppermute | solution.py:18
  20.5 11.1 %collective-permute-start.8 = (bf16[256,512]{1,0:T(8,128)(2,1)S(1)}, bf16[256,512]{1,0:T(8,128)(2,1)S(1)}, u32[]{:S(2)}, u32[]{:S(2)}) collective-permute-start(bf16[256,512]{1,0:T(8,128)(2,1)S(1)} %get-tuple-element.59), channel_id=1, source_target_pairs={{0,8},{4,12},{8,0},{12,4},{16,24},{20,28},{24,16},{28,20},{1,9},{5... | collective-permute-start | bytes 786440 | tf_op jit(solution)/shard_map/ppermute | solution.py:23
  23.8 13.6 %collective-permute-start.9 = (bf16[256,512]{1,0:T(8,128)(2,1)S(1)}, bf16[256,512]{1,0:T(8,128)(2,1)S(1)}, u32[]{:S(2)}, u32[]{:S(2)}) collective-permute-start(bf16[256,512]{1,0:T(8,128)(2,1)S(1)} %get-tuple-element.60), channel_id=1, source_target_pairs={{0,16},{4,20},{8,24},{12,28},{16,0},{20,4},{24,8},{28,12},{1,17},{... | collective-permute-start | bytes 786440 | tf_op jit(solution)/shard_map/ppermute | solution.py:23
  24.8 13.3 %collective-permute-start.10 = (bf16[256,512]{1,0:T(8,128)(2,1)S(1)}, bf16[256,512]{1,0:T(8,128)(2,1)S(1)}, u32[]{:S(2)}, u32[]{:S(2)}) collective-permute-start(bf16[256,512]{1,0:T(8,128)(2,1)S(1)} %get-tuple-element.61), channel_id=1, source_target_pairs={{0,24},{4,28},{8,16},{12,20},{16,8},{20,12},{24,0},{28,4},{1,25},{... | collective-permute-start | bytes 786440 | tf_op jit(solution)/shard_map/ppermute | solution.py:23
  26.2 18.2 %collective-permute-start.5 = (bf16[128,512]{1,0:T(8,128)(2,1)S(1)}, bf16[128,512]{1,0:T(8,128)(2,1)S(1)}, u32[]{:S(2)}, u32[]{:S(2)}) collective-permute-start(bf16[128,512]{1,0:T(8,128)(2,1)S(1)} %get-tuple-element.54), channel_id=1, source_target_pairs={{4,8},{12,16},{20,24},{8,4},{16,12},{24,20},{5,9},{13,17},{21,25},... | collective-permute-start | bytes 393224 | tf_op jit(solution)/shard_map/ppermute | solution.py:18
  26.9 19.0 %collective-permute-start.6 = (bf16[128,512]{1,0:T(8,128)(2,1)S(1)}, bf16[128,512]{1,0:T(8,128)(2,1)S(1)}, u32[]{:S(2)}, u32[]{:S(2)}) collective-permute-start(bf16[128,512]{1,0:T(8,128)(2,1)S(1)} %get-tuple-element.55), channel_id=1, source_target_pairs={{0,1},{2,3},{1,0},{3,2},{4,5},{6,7},{5,4},{7,6},{8,9},{10,11},{9,8... | collective-permute-start | bytes 393224 | tf_op jit(solution)/shard_map/ppermute | solution.py:18
  31.6 14.3 %collective-permute-start.7 = (bf16[128,512]{1,0:T(8,128)(2,1)S(1)}, bf16[128,512]{1,0:T(8,128)(2,1)S(1)}, u32[]{:S(2)}, u32[]{:S(2)}) collective-permute-start(bf16[128,512]{1,0:T(8,128)(2,1)S(1)} %get-tuple-element.56), channel_id=1, source_target_pairs={{1,2},{2,1},{5,6},{6,5},{9,10},{10,9},{13,14},{14,13},{17,18},{18,... | collective-permute-start | bytes 393224 | tf_op jit(solution)/shard_map/ppermute | solution.py:18
  38.3 8.8 %collective-permute-start.11 = (bf16[64,512]{1,0:T(8,128)(2,1)S(1)}, bf16[64,512]{1,0:T(8,128)(2,1)S(1)}, u32[]{:S(2)}, u32[]{:S(2)}) collective-permute-start(bf16[64,512]{1,0:T(8,128)(2,1)S(1)} %get-tuple-element.63), channel_id=1, source_target_pairs={{0,1},{1,0},{2,3},{3,2},{4,5},{5,4},{6,7},{7,6},{8,9},{9,8},{10,11... | collective-permute-start | bytes 196616 | tf_op jit(solution)/shard_map/ppermute | solution.py:23
  43.2 6.6 %collective-permute-start.12 = (bf16[64,512]{1,0:T(8,128)(2,1)S(1)}, bf16[64,512]{1,0:T(8,128)(2,1)S(1)}, u32[]{:S(2)}, u32[]{:S(2)}) collective-permute-start(bf16[64,512]{1,0:T(8,128)(2,1)S(1)} %get-tuple-element.64), channel_id=1, source_target_pairs={{0,2},{1,3},{2,0},{3,1},{4,6},{5,7},{6,4},{7,5},{8,10},{9,11},{10,... | collective-permute-start | bytes 196616 | tf_op jit(solution)/shard_map/ppermute | solution.py:23
  44.5 6.1 %collective-permute-start.13 = (bf16[64,512]{1,0:T(8,128)(2,1)S(1)}, bf16[64,512]{1,0:T(8,128)(2,1)S(1)}, u32[]{:S(2)}, u32[]{:S(2)}) collective-permute-start(bf16[64,512]{1,0:T(8,128)(2,1)S(1)} %get-tuple-element.65), channel_id=1, source_target_pairs={{0,3},{1,2},{2,1},{3,0},{4,7},{5,6},{6,5},{7,4},{8,11},{9,10},{10,... | collective-permute-start | bytes 196616 | tf_op jit(solution)/shard_map/ppermute | solution.py:23

commit v5 on v4

--- a/solution.py
+++ b/solution.py
@@ -390,25 +390,31 @@
     out_ref[...] = result.astype(BF16).reshape(out_ref.shape)
 
 
-def pair_sum_kernel(keep_ref, received_ref, kept_ref, *send_refs):
-    rows = kept_ref.shape[0]
-    kept_ref[...] = keep_ref[0] + received_ref[:rows].astype(F32)
-    for index, send_ref in enumerate(send_refs, 1):
-        send_ref[...] = (keep_ref[index] + received_ref[index * rows : (index + 1) * rows].astype(F32)).astype(BF16)
-
-
-def plane_sum_kernel(groups, keep_ref, *refs):
-    received, kept_ref, send_refs = refs[: groups[0] - 1], refs[groups[0] - 1], refs[groups[0] :]
-    chunk = kept_ref.shape[0]
-    for index in range(groups[1]):
+def pair_sum_kernel(keep_ref, received_ref, near_kept_ref, far_kept_ref, *send_refs):
+    near, far = near_kept_ref.shape[0], far_kept_ref.shape[0]
+    planes = len(send_refs) // 2 + 1
+    for plane in range(planes):
+        start = plane * (near + far)
+        for first, size, kept_ref, sends in (
+            (near, far, far_kept_ref, send_refs[: planes - 1]),
+            (0, near, near_kept_ref, send_refs[planes - 1 :]),
+        ):
+            total = keep_ref[plane, first : first + size] + received_ref[start + first : start + first + size].astype(F32)
+            if plane == 0:
+                kept_ref[...] = total
+            else:
+                sends[plane - 1][...] = total.astype(BF16)
+
+
+def plane_sum_kernel(received, *refs):
+    kept_ref, arrived, outs = refs[0], refs[1 : received + 1], refs[received + 1 :]
+    chunk = outs[0].shape[0]
+    for index, out in enumerate(outs):
         here = slice(index * chunk, (index + 1) * chunk)
-        total = keep_ref[here]
-        for ref in received:
+        total = kept_ref[here]
+        for ref in arrived:
             total = total + ref[here].astype(F32)
-        if index == 0:
-            kept_ref[...] = total
-        else:
-            send_refs[index - 1][...] = total.astype(BF16)
+        out[...] = total.astype(out.dtype)
 
 
 def last_sum_kernel(keep_ref, *refs):
@@ -472,6 +478,7 @@
         and firsts % 2 == 0
         and firsts & (firsts - 1) == 0
         and seconds & (seconds - 1) == 0
+        and seconds > 1
     )
     planes = firsts // 2
     outs = [(node_features.shape, BF16), (face_first, BF16), (face_second, BF16), (face_second, BF16)]
@@ -525,18 +532,29 @@
         node_part = lax.psum_scatter(total[3 * features :].reshape(-1), ("gx", "gy"), scatter_dimension=0, tiled=True)
         return new_nodes, node_grad, edge_part, node_part
 
-    block = (seconds * chunk, features)
-    kept, *sends = call(pair_sum_kernel, [(block, F32)] + [(block, BF16)] * (planes - 1), [keep, received])
+    near, far = (seconds // 2 * chunk, features), ((seconds - seconds // 2) * chunk, features)
+    near_kept, far_kept, *sends = call(
+        pair_sum_kernel, [(near, F32), (far, F32)] + [(far, BF16)] * (planes - 1) + [(near, BF16)] * (planes - 1), [keep, received]
+    )
+
+    def over_planes(values):
+        arrived = []
+        for index, value in enumerate(values):
+            arrived.append(exchanged(value, "gx", 2 * (index + 1)))
+        return arrived
+
+    far_arrived, near_arrived = over_planes(sends[: planes - 1]), over_planes(sends[planes - 1 :])
+    piece = ((chunk, features), BF16)
+    far_sends = call(
+        functools.partial(plane_sum_kernel, planes - 1), [piece] * (seconds - seconds // 2), [far_kept, *far_arrived]
+    )
+    kept, *near_sends = call(
+        functools.partial(plane_sum_kernel, planes - 1),
+        [((chunk, features), F32)] + [piece] * (seconds // 2 - 1),
+        [near_kept, *near_arrived],
+    )
     arrived = []
-    for index, value in enumerate(sends):
-        arrived.append(exchanged(value, "gx", 2 * (index + 1)))
-    kept, *sends = call(
-        functools.partial(plane_sum_kernel, (planes, seconds)),
-        [((chunk, features), F32)] + [((chunk, features), BF16)] * (seconds - 1),
-        [kept, *arrived],
-    )
-    arrived = []
-    for index, value in enumerate(sends):
+    for index, value in enumerate([*near_sends, *far_sends]):
         arrived.append(exchanged(value, "gy", index + 1))
     pieces = features // 128
     edge_part, node_part = call(

time: 51.4 us -> 52.2 us (1.016)
  starting transfers between devices: 26.3 us -> 30 us
  waiting for transfers between devices: 13.4 us -> 10.4 us
    ppermute x6 -> x9, starting transfers between devices: 13.3 us -> 16.5 us  [exchanged(): lax.ppermute(value, axis, [(source, source ^ flip) for source in range(co...]
    ppermute x6 -> x9, waiting for transfers between devices: 9.38 us -> 6.39 us  [exchanged(): lax.ppermute(value, axis, [(source, source ^ flip) for source in range(co...]
    ppermute x8, starting transfers between devices: 13 us -> 13.6 us  [swapped(): lax.ppermute(value, axis, [(at, at + 1) for at in lower] + [(at + 1, at)...]
    pallas_call x7 -> x8, Pallas kernels: 10.7 us -> 10.7 us  [call(): pl.pallas_call(kernel, out_shape=[jax.ShapeDtypeStruct(shape, dtype) for...]
  transfers between devices with their start and end apart: 14 -> 17, of which waited for: 6 -> 5; matrix products, arithmetic and copies ran while one was open for 0% -> 0% of each run, Pallas kernels for 8% -> 8%
where the time goes in v5:
time: 52.2 us; the launch traced here: 52 us
  starting transfers between devices  30 us (57%)
  Pallas kernels  10.7 us (20%)
  waiting for transfers between devices  10.4 us (20%)
  between operations  0.81 us (2%)
    ppermute x9, starting transfers between devices, exchanged(): lax.ppermute(value, axis, [(source, source ^ flip) for source in range(co...  16.5 us
    ppermute x8, starting transfers between devices, swapped(): lax.ppermute(value, axis, [(at, at + 1) for at in lower] + [(at + 1, at)...  13.6 us
    pallas_call x8, Pallas kernels, call(): pl.pallas_call(kernel, out_shape=[jax.ShapeDtypeStruct(shape, dtype) for...  10.7 us
    ppermute x9, waiting for transfers between devices, exchanged(): lax.ppermute(value, axis, [(source, source ^ flip) for source in range(co...  6.39 us
    ppermute x8, waiting for transfers between devices, swapped(): lax.ppermute(value, axis, [(at, at + 1) for at in lower] + [(at + 1, at)...  4.04 us
  transfers between devices with their start and end apart: 17, of which 5 were waited for; matrix products, arithmetic and copies ran while one was open for 0% of the time, Pallas kernels for 8%

profile of v5, /device:TPU:0, one launch (start us, length us, event | category | flops | bytes accessed | tf_op | source)
XLA Modules:
  0.0 52.0 jit_solution(18327714524986269577)
XLA Ops:
  0.6 0.0 copy-start.3
  0.6 0.0 copy-start.4
  0.7 1.4 %shard_map.94 = (bf16[272,512]{1,0:T(8,128)(2,1)S(1)}, bf16[272,512]{1,0:T(8,128)(2,1)S(1)}, bf16[272,512]{1,0:T(8,128)(2,1)S(1)}, bf16[272,512]{1,0:T(8,128)(2,1)S(1)}) custom-call(bf16[2,2,64,512]{3,2,1,0:T(8,128)(2,1)} %refs_8_.1, bf16[3,2,2,64,512]{4,3,2,1,0:T(8,128)(2,1)} %refs_9_.1, s32[3,2,2,64]{3,2,1,0:T(2,128)} %refs_10_.1), custom_call_target="tpu_custom_call" | custom-call | tf_op jit(solution)/shard_map/pallas_call | solution.py:52
  2.0 0.0 copy-start
  2.0 0.0 copy-start.1
  2.0 0.0 copy-start.2
  2.0 0.0 copy-start.5
  2.1 0.6 %collective-permute-start = (bf16[272,512]{1,0:T(8,128)(2,1)S(1)}, bf16[272,512]{1,0:T(8,128)(2,1)S(1)}, u32[]{:S(2)}, u32[]{:S(2)}) collective-permute-start(bf16[272,512]{1,0:T(8,128)(2,1)S(1)} %get-tuple-element.46), channel_id=1, source_target_pairs={{0,4},{8,12},{16,20},{24,28},{4,0},{12,8},{20,16},{28,24},{1,5},{9... | collective-permute-start | bytes 835592 | tf_op jit(solution)/shard_map/ppermute | solution.py:18
  2.6 0.8 %collective-permute-start.1 = (bf16[272,512]{1,0:T(8,128)(2,1)S(1)}, bf16[272,512]{1,0:T(8,128)(2,1)S(1)}, u32[]{:S(2)}, u32[]{:S(2)}) collective-permute-start(bf16[272,512]{1,0:T(8,128)(2,1)S(1)} %get-tuple-element.47), channel_id=1, source_target_pairs={{4,8},{12,16},{20,24},{8,4},{16,12},{24,20},{5,9},{13,17},{21,25},... | collective-permute-start | bytes 835592 | tf_op jit(solution)/shard_map/ppermute | solution.py:18
  3.4 2.6 %collective-permute-start.2 = (bf16[272,512]{1,0:T(8,128)(2,1)S(1)}, bf16[272,512]{1,0:T(8,128)(2,1)S(1)}, u32[]{:S(2)}, u32[]{:S(2)}) collective-permute-start(bf16[272,512]{1,0:T(8,128)(2,1)S(1)} %get-tuple-element.48), channel_id=1, source_target_pairs={{0,1},{2,3},{1,0},{3,2},{4,5},{6,7},{5,4},{7,6},{8,9},{10,11},{9,8... | collective-permute-start | bytes 835592 | tf_op jit(solution)/shard_map/ppermute | solution.py:18
  6.1 0.7 %collective-permute-start.3 = (bf16[272,512]{1,0:T(8,128)(2,1)S(1)}, bf16[272,512]{1,0:T(8,128)(2,1)S(1)}, u32[]{:S(2)}, u32[]{:S(2)}) collective-permute-start(bf16[272,512]{1,0:T(8,128)(2,1)S(1)} %get-tuple-element.49), channel_id=1, source_target_pairs={{1,2},{2,1},{5,6},{6,5},{9,10},{10,9},{13,14},{14,13},{17,18},{18,... | collective-permute-start | bytes 835592 | tf_op jit(solution)/shard_map/ppermute | solution.py:18
  6.7 2.9 %shard_map.93 = (f32[256,512]{1,0:T(8,128)S(1)}, f32[3,256,512]{2,1,0:T(8,128)S(1)}, f32[128,512]{1,0:T(8,128)S(1)}, f32[128,512]{1,0:T(8,128)S(1)}, f32[128,512]{1,0:T(8,128)S(1)}, /*index=5*/f32[128,512]{1,0:T(8,128)S(1)}) custom-call(bf16[2,2,64,512]{3,2,1,0:T(8,128)(2,1)} %refs_8_.1, bf16[3,2,2,64,512]{4,3,2,1,0:T(8,128)(2,1)} %refs_9_.1, ...), custom_call_target="tpu_custom_call" | custom-call | tf_op jit(solution)/shard_map/pallas_call | solution.py:52
  9.7 0.0 collective-permute-done.refs_12_
  9.7 0.0 collective-permute-done.1.refs_13_
  9.7 1.5 %collective-permute-done.2.refs_14_ = bf16[272,512]{1,0:T(8,128)(2,1)S(1)} collective-permute-done((bf16[272,512]{1,0:T(8,128)(2,1)S(1)}, bf16[272,512]{1,0:T(8,128)(2,1)S(1)}, u32[]{:S(2)}, u32[]{:S(2)}) %collective-permute-start.2) | collective-permute-done | bytes 278560 | tf_op jit(solution)/shard_map/ppermute | solution.py:18
  11.3 0.0 collective-permute-done.3.refs_15_
  11.3 4.1 %shard_map.95 = (bf16[2,2,64,512]{3,2,1,0:T(8,128)(2,1)}, bf16[128,512]{1,0:T(8,128)(2,1)S(1)}, bf16[128,512]{1,0:T(8,128)(2,1)S(1)}, bf16[128,512]{1,0:T(8,128)...) custom-call(f32[256,512]{1,0:T(8,128)S(1)} %get-tuple-element.40.ref, ...), custom_call_target="tpu_custom_call" | custom-call | tf_op jit(solution)/shard_map/pallas_call | solution.py:52
  15.5 2.3 %collective-permute-start.4 = (bf16[1152,512]{1,0:T(8,128)(2,1)S(1)}, bf16[1152,512]{1,0:T(8,128)(2,1)S(1)}, u32[]{:S(2)}, u32[]{:S(2)}) collective-permute-start(bf16[1152,512]{1,0:T(8,128)(2,1)S(1)} %get-tuple-element.57), channel_id=1, source_target_pairs={{0,4},{8,12},{16,20},{24,28},{4,0},{12,8},{20,16},{28,24},{1,5},{9... | collective-permute-start | bytes 3538952 | tf_op jit(solution)/shard_map/ppermute | solution.py:18
  17.8 2.5 %collective-permute-done.4.pair_first_ref.received_ref = bf16[1152,512]{1,0:T(8,128)(2,1)S(1)} collective-permute-done((bf16[1152,512]{1,0:T(8,128)(2,1)S(1)}, bf16[1152,512]{1,0:T(8,128)(2,1)S(1)}, u32[]{:S(2)}, u32[]{:S(2)}) %collective-permute-start.4) | collective-permute-done | bytes 1179680 | tf_op jit(solution)/shard_map/ppermute | solution.py:18
  20.3 0.2 shard_map.97
  20.5 3.4 %collective-permute-start.8 = (bf16[128,512]{1,0:T(8,128)(2,1)S(1)}, bf16[128,512]{1,0:T(8,128)(2,1)S(1)}, u32[]{:S(2)}, u32[]{:S(2)}) collective-permute-start(bf16[128,512]{1,0:T(8,128)(2,1)S(1)} %get-tuple-element.63), channel_id=1, source_target_pairs={{0,8},{4,12},{8,0},{12,4},{16,24},{20,28},{24,16},{28,20},{1,9},{5... | collective-permute-start | bytes 393224 | tf_op jit(solution)/shard_map/ppermute | solution.py:23
  23.8 1.0 %collective-permute-start.9 = (bf16[128,512]{1,0:T(8,128)(2,1)S(1)}, bf16[128,512]{1,0:T(8,128)(2,1)S(1)}, u32[]{:S(2)}, u32[]{:S(2)}) collective-permute-start(bf16[128,512]{1,0:T(8,128)(2,1)S(1)} %get-tuple-element.64), channel_id=1, source_target_pairs={{0,16},{4,20},{8,24},{12,28},{16,0},{20,4},{24,8},{28,12},{1,17},{... | collective-permute-start | bytes 393224 | tf_op jit(solution)/shard_map/ppermute | solution.py:23
  24.8 1.4 %collective-permute-start.10 = (bf16[128,512]{1,0:T(8,128)(2,1)S(1)}, bf16[128,512]{1,0:T(8,128)(2,1)S(1)}, u32[]{:S(2)}, u32[]{:S(2)}) collective-permute-start(bf16[128,512]{1,0:T(8,128)(2,1)S(1)} %get-tuple-element.65), channel_id=1, source_target_pairs={{0,24},{4,28},{8,16},{12,20},{16,8},{20,12},{24,0},{28,4},{1,25},{... | collective-permute-start | bytes 393224 | tf_op jit(solution)/shard_map/ppermute | solution.py:23
  26.2 1.1 %collective-permute-start.12 = (bf16[128,512]{1,0:T(8,128)(2,1)S(1)}, bf16[128,512]{1,0:T(8,128)(2,1)S(1)}, u32[]{:S(2)}, u32[]{:S(2)}) collective-permute-start(bf16[128,512]{1,0:T(8,128)(2,1)S(1)} %get-tuple-element.69), channel_id=1, source_target_pairs={{0,8},{4,12},{8,0},{12,4},{16,24},{20,28},{24,16},{28,20},{1,9},{5... | collective-permute-start | bytes 393224 | tf_op jit(solution)/shard_map/ppermute | solution.py:23
  27.3 1.0 %collective-permute-start.13 = (bf16[128,512]{1,0:T(8,128)(2,1)S(1)}, bf16[128,512]{1,0:T(8,128)(2,1)S(1)}, u32[]{:S(2)}, u32[]{:S(2)}) collective-permute-start(bf16[128,512]{1,0:T(8,128)(2,1)S(1)} %get-tuple-element.70), channel_id=1, source_target_pairs={{0,16},{4,20},{8,24},{12,28},{16,0},{20,4},{24,8},{28,12},{1,17},{... | collective-permute-start | bytes 393224 | tf_op jit(solution)/shard_map/ppermute | solution.py:23
  28.3 0.0 collective-permute-done.8.refs_1_
  28.3 1.9 %collective-permute-start.14 = (bf16[128,512]{1,0:T(8,128)(2,1)S(1)}, bf16[128,512]{1,0:T(8,128)(2,1)S(1)}, u32[]{:S(2)}, u32[]{:S(2)}) collective-permute-start(bf16[128,512]{1,0:T(8,128)(2,1)S(1)} %get-tuple-element.71), channel_id=1, source_target_pairs={{0,24},{4,28},{8,16},{12,20},{16,8},{20,12},{24,0},{28,4},{1,25},{... | collective-permute-start | bytes 393224 | tf_op jit(solution)/shard_map/ppermute | solution.py:23
  30.2 1.3 %collective-permute-done.9.refs_2_ = bf16[128,512]{1,0:T(8,128)(2,1)S(1)} collective-permute-done((bf16[128,512]{1,0:T(8,128)(2,1)S(1)}, bf16[128,512]{1,0:T(8,128)(2,1)S(1)}, u32[]{:S(2)}, u32[]{:S(2)}) %collective-permute-start.9) | collective-permute-done | bytes 131104 | tf_op jit(solution)/shard_map/ppermute | solution.py:23
  31.5 0.7 %collective-permute-start.5 = (bf16[128,512]{1,0:T(8,128)(2,1)S(1)}, bf16[128,512]{1,0:T(8,128)(2,1)S(1)}, u32[]{:S(2)}, u32[]{:S(2)}) collective-permute-start(bf16[128,512]{1,0:T(8,128)(2,1)S(1)} %get-tuple-element.58), channel_id=1, source_target_pairs={{4,8},{12,16},{20,24},{8,4},{16,12},{24,20},{5,9},{13,17},{21,25},... | collective-permute-start | bytes 393224 | tf_op jit(solution)/shard_map/ppermute | solution.py:18
  32.2 1.2 %collective-permute-done.10.refs_3_ = bf16[128,512]{1,0:T(8,128)(2,1)S(1)} collective-permute-done((bf16[128,512]{1,0:T(8,128)(2,1)S(1)}, bf16[128,512]{1,0:T(8,128)(2,1)S(1)}, u32[]{:S(2)}, u32[]{:S(2)}) %collective-permute-start.10) | collective-permute-done | bytes 131104 | tf_op jit(solution)/shard_map/ppermute | solution.py:23
  33.4 5.3 %collective-permute-start.6 = (bf16[128,512]{1,0:T(8,128)(2,1)S(1)}, bf16[128,512]{1,0:T(8,128)(2,1)S(1)}, u32[]{:S(2)}, u32[]{:S(2)}) collective-permute-start(bf16[128,512]{1,0:T(8,128)(2,1)S(1)} %get-tuple-element.59), channel_id=1, source_target_pairs={{0,1},{2,3},{1,0},{3,2},{4,5},{6,7},{5,4},{7,6},{8,9},{10,11},{9,8... | collective-permute-start | bytes 393224 | tf_op jit(solution)/shard_map/ppermute | solution.py:18
  38.7 0.0 collective-permute-done.12.refs_1_
  38.7 0.7 %collective-permute-start.7 = (bf16[128,512]{1,0:T(8,128)(2,1)S(1)}, bf16[128,512]{1,0:T(8,128)(2,1)S(1)}, u32[]{:S(2)}, u32[]{:S(2)}) collective-permute-start(bf16[128,512]{1,0:T(8,128)(2,1)S(1)} %get-tuple-element.60), channel_id=1, source_target_pairs={{1,2},{2,1},{5,6},{6,5},{9,10},{10,9},{13,14},{14,13},{17,18},{18,... | collective-permute-start | bytes 393224 | tf_op jit(solution)/shard_map/ppermute | solution.py:18
  39.3 0.1 shard_map.98
  39.4 0.0 collective-permute-done.13.refs_2_
  39.4 4.3 %collective-permute-start.11 = (bf16[64,512]{1,0:T(8,128)(2,1)S(1)}, bf16[64,512]{1,0:T(8,128)(2,1)S(1)}, u32[]{:S(2)}, u32[]{:S(2)}) collective-permute-start(bf16[64,512]{1,0:T(8,128)(2,1)S(1)} %get-tuple-element.67), channel_id=1, source_target_pairs={{0,1},{1,0},{2,3},{3,2},{4,5},{5,4},{6,7},{7,6},{8,9},{9,8},{10,11... | collective-permute-start | bytes 196616 | tf_op jit(solution)/shard_map/ppermute | solution.py:23
  43.8 0.0 collective-permute-done.14.refs_3_
  43.8 0.1 shard_map.99
  43.8 0.5 collective-permute-start.15
  44.3 0.0 collective-permute-done.5.odd_first_ref
  44.3 2.0 %collective-permute-start.16 = (bf16[64,512]{1,0:T(8,128)(2,1)S(1)}, bf16[64,512]{1,0:T(8,128)(2,1)S(1)}, u32[]{:S(2)}, u32[]{:S(2)}) collective-permute-start(bf16[64,512]{1,0:T(8,128)(2,1)S(1)} %get-tuple-element.73), channel_id=1, source_target_pairs={{0,3},{1,2},{2,1},{3,0},{4,7},{5,6},{6,5},{7,4},{8,11},{9,10},{10,... | collective-permute-start | bytes 196616 | tf_op jit(solution)/shard_map/ppermute | solution.py:23
  46.3 0.0 collective-permute-done.6.pair_second_ref
  46.3 0.0 collective-permute-done.7.odd_second_ref
  46.3 1.2 %shard_map.96 = bf16[2,2,64,512]{3,2,1,0:T(8,128)(2,1)} custom-call(f32[256,512]{1,0:T(8,128)S(1)} %get-tuple-element.51.own_ref, f32[256,512]{1,0:T(8,128)S(1)} %get-tuple-element.52.enter_ref, f32[128,512]{1,0:T(8,128)S(1)} %get-tuple-element.53.slope_top_first_ref, f32[128,512]{1,0:T(8,128)S(1)} %get-tuple-element.54.slope_low_first_ref, ...), custom_call_target="tpu_custom_call" | custom-call | tf_op jit(solution)/shard_map/pallas_call | solution.py:52
  47.5 0.0 collective-permute-done.11.refs_0_
  47.5 3.8 %collective-permute-done.15.refs_1_ = bf16[64,512]{1,0:T(8,128)(2,1)S(1)} collective-permute-done((bf16[64,512]{1,0:T(8,128)(2,1)S(1)}, bf16[64,512]{1,0:T(8,128)(2,1)S(1)}, u32[]{:S(2)}, u32[]{:S(2)}) %collective-permute-start.15) | collective-permute-done | bytes 65568 | tf_op jit(solution)/shard_map/ppermute | solution.py:23
  51.3 0.0 collective-permute-done.16.refs_2_
  51.3 0.7 %shard_map.100 = (f32[192,128]{1,0:T(8,128)}, f32[64,128]{1,0:T(8,128)}) custom-call(f32[64,512]{1,0:T(8,128)S(1)} %get-tuple-element.66.keep_ref, bf16[64,512]{1,0:T(8,128)(2,1)S(1)} %collective-permute-done.11.refs_0_, bf16[64,512]{1,0:T(8,128)(2,1)S(1)} %collective-permute-done.15.refs_1_, bf16[64,512]{1,0:T(8,128)(2,1)S(1)} %collective-permute-done.16.refs_2_), custom_call_target="tpu_custom_call" | custom-call | tf_op jit(solution)/shard_map/pallas_call | solution.py:52
  (6 shorter events, 0.0 us)
Async XLA Ops:
  0.6 10.6 %copy-start.3 = (bf16[2,2,64,512]{3,2,1,0:T(8,128)(2,1)S(1)}, bf16[2,2,64,512]{3,2,1,0:T(8,128)(2,1)}, u32[]{:S(2)}) copy-start(bf16[2,2,64,512]{3,2,1,0:T(8,128)(2,1)} %cotangent_ref.1) | copy-start | bytes 786436
  0.6 10.6 %copy-start.4 = (bf16[512,512]{1,0:T(8,128)(2,1)S(1)}, bf16[512,512]{1,0:T(8,128)(2,1)}, u32[]{:S(2)}) copy-start(bf16[512,512]{1,0:T(8,128)(2,1)} %refs_7_.1) | copy-start | bytes 1572868
  2.0 9.3 %copy-start = (bf16[1536,512]{1,0:T(8,128)(2,1)S(1)}, bf16[1536,512]{1,0:T(8,128)(2,1)}, u32[]{:S(2)}) copy-start(bf16[1536,512]{1,0:T(8,128)(2,1)} %weight_ref.3) | copy-start | bytes 4718596
  2.0 9.3 %copy-start.1 = (bf16[3,2,2,64,512]{4,3,2,1,0:T(8,128)(2,1)S(1)}, bf16[3,2,2,64,512]{4,3,2,1,0:T(8,128)(2,1)}, u32[]{:S(2)}) copy-start(bf16[3,2,2,64,512]{4,3,2,1,0:T(8,128)(2,1)} %refs_9_.1) | copy-start | bytes 2359300
  2.0 9.3 %copy-start.2 = (bf16[2,2,64,512]{3,2,1,0:T(8,128)(2,1)S(1)}, bf16[2,2,64,512]{3,2,1,0:T(8,128)(2,1)}, u32[]{:S(2)}) copy-start(bf16[2,2,64,512]{3,2,1,0:T(8,128)(2,1)} %refs_8_.1) | copy-start | bytes 786436
  2.0 9.3 %copy-start.5 = (s32[3,2,2,64]{3,2,1,0:T(2,128)S(1)}, s32[3,2,2,64]{3,2,1,0:T(2,128)}, u32[]{:S(2)}) copy-start(s32[3,2,2,64]{3,2,1,0:T(2,128)} %refs_10_.1) | copy-start | bytes 9220
  2.1 7.6 %collective-permute-start = (bf16[272,512]{1,0:T(8,128)(2,1)S(1)}, bf16[272,512]{1,0:T(8,128)(2,1)S(1)}, u32[]{:S(2)}, u32[]{:S(2)}) collective-permute-start(bf16[272,512]{1,0:T(8,128)(2,1)S(1)} %get-tuple-element.46), channel_id=1, source_target_pairs={{0,4},{8,12},{16,20},{24,28},{4,0},{12,8},{20,16},{28,24},{1,5},{9... | collective-permute-start | bytes 835592 | tf_op jit(solution)/shard_map/ppermute | solution.py:18
  2.6 7.1 %collective-permute-start.1 = (bf16[272,512]{1,0:T(8,128)(2,1)S(1)}, bf16[272,512]{1,0:T(8,128)(2,1)S(1)}, u32[]{:S(2)}, u32[]{:S(2)}) collective-permute-start(bf16[272,512]{1,0:T(8,128)(2,1)S(1)} %get-tuple-element.47), channel_id=1, source_target_pairs={{4,8},{12,16},{20,24},{8,4},{16,12},{24,20},{5,9},{13,17},{21,25},... | collective-permute-start | bytes 835592 | tf_op jit(solution)/shard_map/ppermute | solution.py:18
  3.4 7.8 %collective-permute-start.2 = (bf16[272,512]{1,0:T(8,128)(2,1)S(1)}, bf16[272,512]{1,0:T(8,128)(2,1)S(1)}, u32[]{:S(2)}, u32[]{:S(2)}) collective-permute-start(bf16[272,512]{1,0:T(8,128)(2,1)S(1)} %get-tuple-element.48), channel_id=1, source_target_pairs={{0,1},{2,3},{1,0},{3,2},{4,5},{6,7},{5,4},{7,6},{8,9},{10,11},{9,8... | collective-permute-start | bytes 835592 | tf_op jit(solution)/shard_map/ppermute | solution.py:18
  6.1 5.2 %collective-permute-start.3 = (bf16[272,512]{1,0:T(8,128)(2,1)S(1)}, bf16[272,512]{1,0:T(8,128)(2,1)S(1)}, u32[]{:S(2)}, u32[]{:S(2)}) collective-permute-start(bf16[272,512]{1,0:T(8,128)(2,1)S(1)} %get-tuple-element.49), channel_id=1, source_target_pairs={{1,2},{2,1},{5,6},{6,5},{9,10},{10,9},{13,14},{14,13},{17,18},{18,... | collective-permute-start | bytes 835592 | tf_op jit(solution)/shard_map/ppermute | solution.py:18
  15.5 4.8 %collective-permute-start.4 = (bf16[1152,512]{1,0:T(8,128)(2,1)S(1)}, bf16[1152,512]{1,0:T(8,128)(2,1)S(1)}, u32[]{:S(2)}, u32[]{:S(2)}) collective-permute-start(bf16[1152,512]{1,0:T(8,128)(2,1)S(1)} %get-tuple-element.57), channel_id=1, source_target_pairs={{0,4},{8,12},{16,20},{24,28},{4,0},{12,8},{20,16},{28,24},{1,5},{9... | collective-permute-start | bytes 3538952 | tf_op jit(solution)/shard_map/ppermute | solution.py:18
  20.5 7.8 %collective-permute-start.8 = (bf16[128,512]{1,0:T(8,128)(2,1)S(1)}, bf16[128,512]{1,0:T(8,128)(2,1)S(1)}, u32[]{:S(2)}, u32[]{:S(2)}) collective-permute-start(bf16[128,512]{1,0:T(8,128)(2,1)S(1)} %get-tuple-element.63), channel_id=1, source_target_pairs={{0,8},{4,12},{8,0},{12,4},{16,24},{20,28},{24,16},{28,20},{1,9},{5... | collective-permute-start | bytes 393224 | tf_op jit(solution)/shard_map/ppermute | solution.py:23
  23.8 7.7 %collective-permute-start.9 = (bf16[128,512]{1,0:T(8,128)(2,1)S(1)}, bf16[128,512]{1,0:T(8,128)(2,1)S(1)}, u32[]{:S(2)}, u32[]{:S(2)}) collective-permute-start(bf16[128,512]{1,0:T(8,128)(2,1)S(1)} %get-tuple-element.64), channel_id=1, source_target_pairs={{0,16},{4,20},{8,24},{12,28},{16,0},{20,4},{24,8},{28,12},{1,17},{... | collective-permute-start | bytes 393224 | tf_op jit(solution)/shard_map/ppermute | solution.py:23
  24.8 8.6 %collective-permute-start.10 = (bf16[128,512]{1,0:T(8,128)(2,1)S(1)}, bf16[128,512]{1,0:T(8,128)(2,1)S(1)}, u32[]{:S(2)}, u32[]{:S(2)}) collective-permute-start(bf16[128,512]{1,0:T(8,128)(2,1)S(1)} %get-tuple-element.65), channel_id=1, source_target_pairs={{0,24},{4,28},{8,16},{12,20},{16,8},{20,12},{24,0},{28,4},{1,25},{... | collective-permute-start | bytes 393224 | tf_op jit(solution)/shard_map/ppermute | solution.py:23
  26.2 12.5 %collective-permute-start.12 = (bf16[128,512]{1,0:T(8,128)(2,1)S(1)}, bf16[128,512]{1,0:T(8,128)(2,1)S(1)}, u32[]{:S(2)}, u32[]{:S(2)}) collective-permute-start(bf16[128,512]{1,0:T(8,128)(2,1)S(1)} %get-tuple-element.69), channel_id=1, source_target_pairs={{0,8},{4,12},{8,0},{12,4},{16,24},{20,28},{24,16},{28,20},{1,9},{5... | collective-permute-start | bytes 393224 | tf_op jit(solution)/shard_map/ppermute | solution.py:23
  27.3 12.1 %collective-permute-start.13 = (bf16[128,512]{1,0:T(8,128)(2,1)S(1)}, bf16[128,512]{1,0:T(8,128)(2,1)S(1)}, u32[]{:S(2)}, u32[]{:S(2)}) collective-permute-start(bf16[128,512]{1,0:T(8,128)(2,1)S(1)} %get-tuple-element.70), channel_id=1, source_target_pairs={{0,16},{4,20},{8,24},{12,28},{16,0},{20,4},{24,8},{28,12},{1,17},{... | collective-permute-start | bytes 393224 | tf_op jit(solution)/shard_map/ppermute | solution.py:23
  28.3 15.4 %collective-permute-start.14 = (bf16[128,512]{1,0:T(8,128)(2,1)S(1)}, bf16[128,512]{1,0:T(8,128)(2,1)S(1)}, u32[]{:S(2)}, u32[]{:S(2)}) collective-permute-start(bf16[128,512]{1,0:T(8,128)(2,1)S(1)} %get-tuple-element.71), channel_id=1, source_target_pairs={{0,24},{4,28},{8,16},{12,20},{16,8},{20,12},{24,0},{28,4},{1,25},{... | collective-permute-start | bytes 393224 | tf_op jit(solution)/shard_map/ppermute | solution.py:23
  31.5 12.8 %collective-permute-start.5 = (bf16[128,512]{1,0:T(8,128)(2,1)S(1)}, bf16[128,512]{1,0:T(8,128)(2,1)S(1)}, u32[]{:S(2)}, u32[]{:S(2)}) collective-permute-start(bf16[128,512]{1,0:T(8,128)(2,1)S(1)} %get-tuple-element.58), channel_id=1, source_target_pairs={{4,8},{12,16},{20,24},{8,4},{16,12},{24,20},{5,9},{13,17},{21,25},... | collective-permute-start | bytes 393224 | tf_op jit(solution)/shard_map/ppermute | solution.py:18
  33.4 12.9 %collective-permute-start.6 = (bf16[128,512]{1,0:T(8,128)(2,1)S(1)}, bf16[128,512]{1,0:T(8,128)(2,1)S(1)}, u32[]{:S(2)}, u32[]{:S(2)}) collective-permute-start(bf16[128,512]{1,0:T(8,128)(2,1)S(1)} %get-tuple-element.59), channel_id=1, source_target_pairs={{0,1},{2,3},{1,0},{3,2},{4,5},{6,7},{5,4},{7,6},{8,9},{10,11},{9,8... | collective-permute-start | bytes 393224 | tf_op jit(solution)/shard_map/ppermute | solution.py:18
  38.7 7.6 %collective-permute-start.7 = (bf16[128,512]{1,0:T(8,128)(2,1)S(1)}, bf16[128,512]{1,0:T(8,128)(2,1)S(1)}, u32[]{:S(2)}, u32[]{:S(2)}) collective-permute-start(bf16[128,512]{1,0:T(8,128)(2,1)S(1)} %get-tuple-element.60), channel_id=1, source_target_pairs={{1,2},{2,1},{5,6},{6,5},{9,10},{10,9},{13,14},{14,13},{17,18},{18,... | collective-permute-start | bytes 393224 | tf_op jit(solution)/shard_map/ppermute | solution.py:18
  39.4 8.1 %collective-permute-start.11 = (bf16[64,512]{1,0:T(8,128)(2,1)S(1)}, bf16[64,512]{1,0:T(8,128)(2,1)S(1)}, u32[]{:S(2)}, u32[]{:S(2)}) collective-permute-start(bf16[64,512]{1,0:T(8,128)(2,1)S(1)} %get-tuple-element.67), channel_id=1, source_target_pairs={{0,1},{1,0},{2,3},{3,2},{4,5},{5,4},{6,7},{7,6},{8,9},{9,8},{10,11... | collective-permute-start | bytes 196616 | tf_op jit(solution)/shard_map/ppermute | solution.py:23
  43.8 7.5 %collective-permute-start.15 = (bf16[64,512]{1,0:T(8,128)(2,1)S(1)}, bf16[64,512]{1,0:T(8,128)(2,1)S(1)}, u32[]{:S(2)}, u32[]{:S(2)}) collective-permute-start(bf16[64,512]{1,0:T(8,128)(2,1)S(1)} %get-tuple-element.72), channel_id=1, source_target_pairs={{0,2},{1,3},{2,0},{3,1},{4,6},{5,7},{6,4},{7,5},{8,10},{9,11},{10,... | collective-permute-start | bytes 196616 | tf_op jit(solution)/shard_map/ppermute | solution.py:23
  44.3 7.0 %collective-permute-start.16 = (bf16[64,512]{1,0:T(8,128)(2,1)S(1)}, bf16[64,512]{1,0:T(8,128)(2,1)S(1)}, u32[]{:S(2)}, u32[]{:S(2)}) collective-permute-start(bf16[64,512]{1,0:T(8,128)(2,1)S(1)} %get-tuple-element.73), channel_id=1, source_target_pairs={{0,3},{1,2},{2,1},{3,0},{4,7},{5,6},{6,5},{7,4},{8,11},{9,10},{10,... | collective-permute-start | bytes 196616 | tf_op jit(solution)/shard_map/ppermute | solution.py:23

commit v6 on v5

--- a/solution.py
+++ b/solution.py
@@ -209,7 +209,7 @@
     pair_first_ref, odd_first_ref, pair_second_ref, odd_second_ref,
     new_ref, grad_odd_first_ref, grad_pair_second_ref, grad_odd_second_ref,
     own_ref, enter_ref, slope_top_first_ref, slope_low_first_ref, slope_top_second_ref, slope_low_second_ref,
-    grad_pair_first_ref, send_ref, keep_ref,
+    grad_pair_first_ref, far_send_ref, near_send_ref, keep_ref,
     summed_ref, update_ref, grad_ref, grad_low_ref, grads_ref, total_ref,
 ):
     ex, ey, nz, features = dims
@@ -263,7 +263,9 @@
     cotangent = cotangent_ref[...].reshape(-1, features).astype(F32)
     update_ref[...] = (cotangent * (gate * (1.0 + update * (1.0 - gate)))).astype(BF16)
     grad_summed = dot_nt(update_ref[...], node_weight_ref[...]).astype(BF16)
-    pair_target, extra = (grad_pair_first_ref, 0) if send_ref is None else (send_ref, send_ref.shape[0] - rows_first)
+    pair_target, extra = grad_pair_first_ref, 0
+    if near_send_ref is not None:
+        pair_target, extra = near_send_ref, near_send_ref.shape[0] - rows_first
     for y in range(ey):
         low, top = grad_summed[rows(0, y)], grad_summed[rows(ex - 1, y)]
         pair_target[extra + y * nz : extra + (y + 1) * nz] = jnp.where(even_first, top, low)
@@ -328,7 +330,7 @@
     )
     total_ref[3 * features :] = dot_tn(summed_ref[...], update_ref[...])
 
-    if send_ref is None:
+    if near_send_ref is None:
         keep_ref[...] = total_ref[...]
         return
     planes = keep_ref.shape[0]
@@ -347,7 +349,11 @@
                     keep_ref[block, start : start + edge_rows] = edge
                     keep_ref[block, start + edge_rows : start + chunk] = node
                 else:
-                    send_at = block * seconds * chunk + start
+                    near = seconds // 2
+                    if second < near:
+                        send_ref, send_at = near_send_ref, (block * near + second) * chunk
+                    else:
+                        send_ref, send_at = far_send_ref, (block * (seconds - near) + second - near) * chunk
                     send_ref[send_at : send_at + edge_rows] = edge.astype(BF16)
                     send_ref[send_at + edge_rows : send_at + chunk] = node.astype(BF16)
 
@@ -390,20 +396,14 @@
     out_ref[...] = result.astype(BF16).reshape(out_ref.shape)
 
 
-def pair_sum_kernel(keep_ref, received_ref, near_kept_ref, far_kept_ref, *send_refs):
-    near, far = near_kept_ref.shape[0], far_kept_ref.shape[0]
-    planes = len(send_refs) // 2 + 1
-    for plane in range(planes):
-        start = plane * (near + far)
-        for first, size, kept_ref, sends in (
-            (near, far, far_kept_ref, send_refs[: planes - 1]),
-            (0, near, near_kept_ref, send_refs[planes - 1 :]),
-        ):
-            total = keep_ref[plane, first : first + size] + received_ref[start + first : start + first + size].astype(F32)
-            if plane == 0:
-                kept_ref[...] = total
-            else:
-                sends[plane - 1][...] = total.astype(BF16)
+def pair_sum_kernel(first, keep_ref, received_ref, kept_ref, *send_refs):
+    size = kept_ref.shape[0]
+    for plane in range(len(send_refs) + 1):
+        total = keep_ref[plane, first : first + size] + received_ref[plane * size : (plane + 1) * size].astype(F32)
+        if plane == 0:
+            kept_ref[...] = total
+        else:
+            send_refs[plane - 1][...] = total.astype(BF16)
 
 
 def plane_sum_kernel(received, *refs):
@@ -484,7 +484,9 @@
     outs = [(node_features.shape, BF16), (face_first, BF16), (face_second, BF16), (face_second, BF16)]
     outs += [((count, features), F32)] * 2 + [(face_first, F32)] * 2 + [(face_second, F32)] * 2
     if by_hand:
-        outs += [((planes * seconds * chunk + ey * nz, features), BF16), ((planes, seconds * chunk, features), F32)]
+        near, far = seconds // 2 * chunk, (seconds - seconds // 2) * chunk
+        outs += [((planes * far, features), BF16), ((planes * near + ey * nz, features), BF16)]
+        outs += [((planes, near + far, features), F32)]
 
         def kernel(*refs):
             layer_kernel(dims, *refs[:26], None, *refs[26:])
@@ -493,7 +495,7 @@
         outs += [(face_first, BF16), ((total_rows, features), F32)]
 
         def kernel(*refs):
-            layer_kernel(dims, *refs[:27], None, *refs[27:])
+            layer_kernel(dims, *refs[:27], None, None, *refs[27:])
 
     low_rows = (ex + ey) * nz
     results = call(
@@ -514,8 +516,10 @@
         limit=14 << 20,
     )
     new_nodes, odd_first, pair_second, odd_second = results[:4]
-    received, keep = results[10:]
-    received = swapped(received, "gx", 0)
+    keep = results[-1]
+    if by_hand:
+        far_received = swapped(results[10], "gx", 0)
+    received = swapped(results[-2], "gx", 0)
     pair_second = swapped(pair_second, "gy", 0)
     odd_second = swapped(odd_second, "gy", 1)
     odd_first = swapped(odd_first, "gx", 1)
@@ -532,10 +536,15 @@
         node_part = lax.psum_scatter(total[3 * features :].reshape(-1), ("gx", "gy"), scatter_dimension=0, tiled=True)
         return new_nodes, node_grad, edge_part, node_part
 
-    near, far = (seconds // 2 * chunk, features), ((seconds - seconds // 2) * chunk, features)
-    near_kept, far_kept, *sends = call(
-        pair_sum_kernel, [(near, F32), (far, F32)] + [(far, BF16)] * (planes - 1) + [(near, BF16)] * (planes - 1), [keep, received]
-    )
+    def summed_pairs(first, size, arrived):
+        return call(
+            functools.partial(pair_sum_kernel, first),
+            [((size, features), F32)] + [((size, features), BF16)] * (planes - 1),
+            [keep, arrived],
+        )
+
+    far_kept, *far_sends = summed_pairs(near, far, far_received)
+    near_kept, *near_sends = summed_pairs(0, near, received)
 
     def over_planes(values):
         arrived = []
@@ -543,7 +552,7 @@
             arrived.append(exchanged(value, "gx", 2 * (index + 1)))
         return arrived
 
-    far_arrived, near_arrived = over_planes(sends[: planes - 1]), over_planes(sends[planes - 1 :])
+    far_arrived, near_arrived = over_planes(far_sends), over_planes(near_sends)
     piece = ((chunk, features), BF16)
     far_sends = call(
         functools.partial(plane_sum_kernel, planes - 1), [piece] * (seconds - seconds // 2), [far_kept, *far_arrived]

time: 52.2 us -> 52.6 us (level)
    ppermute x8 -> x9, starting transfers between devices: 13.6 us -> 13.3 us  [swapped(): lax.ppermute(value, axis, [(at, at + 1) for at in lower] + [(at + 1, at)...]
    pallas_call x8 -> x9, Pallas kernels: 10.7 us -> 10.7 us  [call(): pl.pallas_call(kernel, out_shape=[jax.ShapeDtypeStruct(shape, dtype) for...]
    ppermute x8 -> x9, waiting for transfers between devices: 4.04 us -> 4.04 us  [swapped(): lax.ppermute(value, axis, [(at, at + 1) for at in lower] + [(at + 1, at)...]
  transfers between devices with their start and end apart: 17 -> 18, of which waited for: 5 -> 6; matrix products, arithmetic and copies ran while one was open for 0% -> 0% of each run, Pallas kernels for 8% -> 9%
where the time goes in v6:
time: 52.6 us; the launch traced here: 52.3 us
  starting transfers between devices  29.9 us (57%)
  waiting for transfers between devices  10.9 us (21%)
  Pallas kernels  10.7 us (20%)
  between operations  0.84 us (2%)
    ppermute x9, starting transfers between devices, exchanged(): lax.ppermute(value, axis, [(source, source ^ flip) for source in range(co...  16.6 us
    ppermute x9, starting transfers between devices, swapped(): lax.ppermute(value, axis, [(at, at + 1) for at in lower] + [(at + 1, at)...  13.3 us
    pallas_call x9, Pallas kernels, call(): pl.pallas_call(kernel, out_shape=[jax.ShapeDtypeStruct(shape, dtype) for...  10.7 us
    ppermute x9, waiting for transfers between devices, exchanged(): lax.ppermute(value, axis, [(source, source ^ flip) for source in range(co...  6.83 us
    ppermute x9, waiting for transfers between devices, swapped(): lax.ppermute(value, axis, [(at, at + 1) for at in lower] + [(at + 1, at)...  4.04 us
  transfers between devices with their start and end apart: 18, of which 6 were waited for; matrix products, arithmetic and copies ran while one was open for 0% of the time, Pallas kernels for 9%

profile of v6, /device:TPU:0, one launch (start us, length us, event | category | flops | bytes accessed | tf_op | source)
XLA Modules:
  0.0 52.3 jit_solution(16876208340700438599)
XLA Ops:
  0.7 1.4 %shard_map.94 = (bf16[272,512]{1,0:T(8,128)(2,1)S(1)}, bf16[272,512]{1,0:T(8,128)(2,1)S(1)}, bf16[272,512]{1,0:T(8,128)(2,1)S(1)}, bf16[272,512]{1,0:T(8,128)(2,1)S(1)}) custom-call(bf16[2,2,64,512]{3,2,1,0:T(8,128)(2,1)} %refs_8_.1, bf16[3,2,2,64,512]{4,3,2,1,0:T(8,128)(2,1)} %refs_9_.1, s32[3,2,2,64]{3,2,1,0:T(2,128)} %refs_10_.1), custom_call_target="tpu_custom_call" | custom-call | tf_op jit(solution)/shard_map/pallas_call | solution.py:52
  2.0 0.0 copy-start
  2.0 0.0 copy-start.1
  2.0 0.0 copy-start.2
  2.0 0.0 copy-start.5
  2.1 0.6 %collective-permute-start = (bf16[272,512]{1,0:T(8,128)(2,1)S(1)}, bf16[272,512]{1,0:T(8,128)(2,1)S(1)}, u32[]{:S(2)}, u32[]{:S(2)}) collective-permute-start(bf16[272,512]{1,0:T(8,128)(2,1)S(1)} %get-tuple-element.47), channel_id=1, source_target_pairs={{0,4},{8,12},{16,20},{24,28},{4,0},{12,8},{20,16},{28,24},{1,5},{9... | collective-permute-start | bytes 835592 | tf_op jit(solution)/shard_map/ppermute | solution.py:18
  2.6 0.8 %collective-permute-start.1 = (bf16[272,512]{1,0:T(8,128)(2,1)S(1)}, bf16[272,512]{1,0:T(8,128)(2,1)S(1)}, u32[]{:S(2)}, u32[]{:S(2)}) collective-permute-start(bf16[272,512]{1,0:T(8,128)(2,1)S(1)} %get-tuple-element.48), channel_id=1, source_target_pairs={{4,8},{12,16},{20,24},{8,4},{16,12},{24,20},{5,9},{13,17},{21,25},... | collective-permute-start | bytes 835592 | tf_op jit(solution)/shard_map/ppermute | solution.py:18
  3.4 2.6 %collective-permute-start.2 = (bf16[272,512]{1,0:T(8,128)(2,1)S(1)}, bf16[272,512]{1,0:T(8,128)(2,1)S(1)}, u32[]{:S(2)}, u32[]{:S(2)}) collective-permute-start(bf16[272,512]{1,0:T(8,128)(2,1)S(1)} %get-tuple-element.49), channel_id=1, source_target_pairs={{0,1},{2,3},{1,0},{3,2},{4,5},{6,7},{5,4},{7,6},{8,9},{10,11},{9,8... | collective-permute-start | bytes 835592 | tf_op jit(solution)/shard_map/ppermute | solution.py:18
  6.1 0.7 %collective-permute-start.3 = (bf16[272,512]{1,0:T(8,128)(2,1)S(1)}, bf16[272,512]{1,0:T(8,128)(2,1)S(1)}, u32[]{:S(2)}, u32[]{:S(2)}) collective-permute-start(bf16[272,512]{1,0:T(8,128)(2,1)S(1)} %get-tuple-element.50), channel_id=1, source_target_pairs={{1,2},{2,1},{5,6},{6,5},{9,10},{10,9},{13,14},{14,13},{17,18},{18,... | collective-permute-start | bytes 835592 | tf_op jit(solution)/shard_map/ppermute | solution.py:18
  6.7 2.9 %shard_map.93 = (f32[256,512]{1,0:T(8,128)S(1)}, f32[3,256,512]{2,1,0:T(8,128)S(1)}, f32[128,512]{1,0:T(8,128)S(1)}, f32[128,512]{1,0:T(8,128)S(1)}, f32[128,512]{1,0:T(8,128)S(1)}, /*index=5*/f32[128,512]{1,0:T(8,128)S(1)}) custom-call(bf16[2,2,64,512]{3,2,1,0:T(8,128)(2,1)} %refs_8_.1, bf16[3,2,2,64,512]{4,3,2,1,0:T(8,128)(2,1)} %refs_9_.1, ...), custom_call_target="tpu_custom_call" | custom-call | tf_op jit(solution)/shard_map/pallas_call | solution.py:52
  9.7 0.0 collective-permute-done.refs_12_
  9.7 0.0 collective-permute-done.1.refs_13_
  9.7 1.5 %collective-permute-done.2.refs_14_ = bf16[272,512]{1,0:T(8,128)(2,1)S(1)} collective-permute-done((bf16[272,512]{1,0:T(8,128)(2,1)S(1)}, bf16[272,512]{1,0:T(8,128)(2,1)S(1)}, u32[]{:S(2)}, u32[]{:S(2)}) %collective-permute-start.2) | collective-permute-done | bytes 278560 | tf_op jit(solution)/shard_map/ppermute | solution.py:18
  11.3 0.0 collective-permute-done.3.refs_15_
  11.3 4.1 %shard_map.95 = (bf16[2,2,64,512]{3,2,1,0:T(8,128)(2,1)}, bf16[128,512]{1,0:T(8,128)(2,1)S(1)}, bf16[128,512]{1,0:T(8,128)(2,1)S(1)}, bf16[128,512]{1,0:T(8,128)...) custom-call(f32[256,512]{1,0:T(8,128)S(1)} %get-tuple-element.41.ref, ...), custom_call_target="tpu_custom_call" | custom-call | tf_op jit(solution)/shard_map/pallas_call | solution.py:52
  15.5 2.3 %collective-permute-start.4 = (bf16[640,512]{1,0:T(8,128)(2,1)S(1)}, bf16[640,512]{1,0:T(8,128)(2,1)S(1)}, u32[]{:S(2)}, u32[]{:S(2)}) collective-permute-start(bf16[640,512]{1,0:T(8,128)(2,1)S(1)} %get-tuple-element.58), channel_id=1, source_target_pairs={{0,4},{8,12},{16,20},{24,28},{4,0},{12,8},{20,16},{28,24},{1,5},{9... | collective-permute-start | bytes 1966088 | tf_op jit(solution)/shard_map/ppermute | solution.py:18
  17.8 0.0 collective-permute-start.12
  17.8 2.5 %collective-permute-done.12.received_ref = bf16[512,512]{1,0:T(8,128)(2,1)S(1)} collective-permute-done((bf16[512,512]{1,0:T(8,128)(2,1)S(1)}, bf16[512,512]{1,0:T(8,128)(2,1)S(1)}, u32[]{:S(2)}, u32[]{:S(2)}) %collective-permute-start.12) | collective-permute-done | bytes 524320 | tf_op jit(solution)/shard_map/ppermute | solution.py:18
  20.2 0.1 shard_map.99
  20.4 3.4 %collective-permute-start.13 = (bf16[128,512]{1,0:T(8,128)(2,1)S(1)}, bf16[128,512]{1,0:T(8,128)(2,1)S(1)}, u32[]{:S(2)}, u32[]{:S(2)}) collective-permute-start(bf16[128,512]{1,0:T(8,128)(2,1)S(1)} %get-tuple-element.71), channel_id=1, source_target_pairs={{0,8},{4,12},{8,0},{12,4},{16,24},{20,28},{24,16},{28,20},{1,9},{5... | collective-permute-start | bytes 393224 | tf_op jit(solution)/shard_map/ppermute | solution.py:23
  23.7 1.0 %collective-permute-start.14 = (bf16[128,512]{1,0:T(8,128)(2,1)S(1)}, bf16[128,512]{1,0:T(8,128)(2,1)S(1)}, u32[]{:S(2)}, u32[]{:S(2)}) collective-permute-start(bf16[128,512]{1,0:T(8,128)(2,1)S(1)} %get-tuple-element.72), channel_id=1, source_target_pairs={{0,16},{4,20},{8,24},{12,28},{16,0},{20,4},{24,8},{28,12},{1,17},{... | collective-permute-start | bytes 393224 | tf_op jit(solution)/shard_map/ppermute | solution.py:23
  24.7 1.4 %collective-permute-start.15 = (bf16[128,512]{1,0:T(8,128)(2,1)S(1)}, bf16[128,512]{1,0:T(8,128)(2,1)S(1)}, u32[]{:S(2)}, u32[]{:S(2)}) collective-permute-start(bf16[128,512]{1,0:T(8,128)(2,1)S(1)} %get-tuple-element.73), channel_id=1, source_target_pairs={{0,24},{4,28},{8,16},{12,20},{16,8},{20,12},{24,0},{28,4},{1,25},{... | collective-permute-start | bytes 393224 | tf_op jit(solution)/shard_map/ppermute | solution.py:23
  26.1 0.0 collective-permute-done.4.pair_first_ref.received_ref
  26.1 0.1 shard_map.97
  26.2 1.2 %collective-permute-start.8 = (bf16[128,512]{1,0:T(8,128)(2,1)S(1)}, bf16[128,512]{1,0:T(8,128)(2,1)S(1)}, u32[]{:S(2)}, u32[]{:S(2)}) collective-permute-start(bf16[128,512]{1,0:T(8,128)(2,1)S(1)} %get-tuple-element.64), channel_id=1, source_target_pairs={{0,8},{4,12},{8,0},{12,4},{16,24},{20,28},{24,16},{28,20},{1,9},{5... | collective-permute-start | bytes 393224 | tf_op jit(solution)/shard_map/ppermute | solution.py:23
  27.4 1.0 %collective-permute-start.9 = (bf16[128,512]{1,0:T(8,128)(2,1)S(1)}, bf16[128,512]{1,0:T(8,128)(2,1)S(1)}, u32[]{:S(2)}, u32[]{:S(2)}) collective-permute-start(bf16[128,512]{1,0:T(8,128)(2,1)S(1)} %get-tuple-element.65), channel_id=1, source_target_pairs={{0,16},{4,20},{8,24},{12,28},{16,0},{20,4},{24,8},{28,12},{1,17},{... | collective-permute-start | bytes 393224 | tf_op jit(solution)/shard_map/ppermute | solution.py:23
  28.4 0.0 collective-permute-done.13.refs_1_
  28.4 1.7 %collective-permute-start.10 = (bf16[128,512]{1,0:T(8,128)(2,1)S(1)}, bf16[128,512]{1,0:T(8,128)(2,1)S(1)}, u32[]{:S(2)}, u32[]{:S(2)}) collective-permute-start(bf16[128,512]{1,0:T(8,128)(2,1)S(1)} %get-tuple-element.66), channel_id=1, source_target_pairs={{0,24},{4,28},{8,16},{12,20},{16,8},{20,12},{24,0},{28,4},{1,25},{... | collective-permute-start | bytes 393224 | tf_op jit(solution)/shard_map/ppermute | solution.py:23
  30.1 1.3 %collective-permute-done.14.refs_2_ = bf16[128,512]{1,0:T(8,128)(2,1)S(1)} collective-permute-done((bf16[128,512]{1,0:T(8,128)(2,1)S(1)}, bf16[128,512]{1,0:T(8,128)(2,1)S(1)}, u32[]{:S(2)}, u32[]{:S(2)}) %collective-permute-start.14) | collective-permute-done | bytes 131104 | tf_op jit(solution)/shard_map/ppermute | solution.py:23
  31.4 0.7 %collective-permute-start.5 = (bf16[128,512]{1,0:T(8,128)(2,1)S(1)}, bf16[128,512]{1,0:T(8,128)(2,1)S(1)}, u32[]{:S(2)}, u32[]{:S(2)}) collective-permute-start(bf16[128,512]{1,0:T(8,128)(2,1)S(1)} %get-tuple-element.59), channel_id=1, source_target_pairs={{4,8},{12,16},{20,24},{8,4},{16,12},{24,20},{5,9},{13,17},{21,25},... | collective-permute-start | bytes 393224 | tf_op jit(solution)/shard_map/ppermute | solution.py:18
  32.1 1.2 %collective-permute-done.15.refs_3_ = bf16[128,512]{1,0:T(8,128)(2,1)S(1)} collective-permute-done((bf16[128,512]{1,0:T(8,128)(2,1)S(1)}, bf16[128,512]{1,0:T(8,128)(2,1)S(1)}, u32[]{:S(2)}, u32[]{:S(2)}) %collective-permute-start.15) | collective-permute-done | bytes 131104 | tf_op jit(solution)/shard_map/ppermute | solution.py:23
  33.3 5.0 %collective-permute-start.6 = (bf16[128,512]{1,0:T(8,128)(2,1)S(1)}, bf16[128,512]{1,0:T(8,128)(2,1)S(1)}, u32[]{:S(2)}, u32[]{:S(2)}) collective-permute-start(bf16[128,512]{1,0:T(8,128)(2,1)S(1)} %get-tuple-element.60), channel_id=1, source_target_pairs={{0,1},{2,3},{1,0},{3,2},{4,5},{6,7},{5,4},{7,6},{8,9},{10,11},{9,8... | collective-permute-start | bytes 393224 | tf_op jit(solution)/shard_map/ppermute | solution.py:18
  38.3 0.0 collective-permute-done.8.refs_1_
  38.3 0.7 %collective-permute-start.7 = (bf16[128,512]{1,0:T(8,128)(2,1)S(1)}, bf16[128,512]{1,0:T(8,128)(2,1)S(1)}, u32[]{:S(2)}, u32[]{:S(2)}) collective-permute-start(bf16[128,512]{1,0:T(8,128)(2,1)S(1)} %get-tuple-element.61), channel_id=1, source_target_pairs={{1,2},{2,1},{5,6},{6,5},{9,10},{10,9},{13,14},{14,13},{17,18},{18,... | collective-permute-start | bytes 393224 | tf_op jit(solution)/shard_map/ppermute | solution.py:18
  39.0 0.1 shard_map.100
  39.1 0.0 collective-permute-done.9.refs_2_
  39.1 5.0 %collective-permute-start.16 = (bf16[64,512]{1,0:T(8,128)(2,1)S(1)}, bf16[64,512]{1,0:T(8,128)(2,1)S(1)}, u32[]{:S(2)}, u32[]{:S(2)}) collective-permute-start(bf16[64,512]{1,0:T(8,128)(2,1)S(1)} %get-tuple-element.74), channel_id=1, source_target_pairs={{0,2},{1,3},{2,0},{3,1},{4,6},{5,7},{6,4},{7,5},{8,10},{9,11},{10,... | collective-permute-start | bytes 196616 | tf_op jit(solution)/shard_map/ppermute | solution.py:23
  44.1 0.0 collective-permute-done.10.refs_3_
  44.1 1.9 %collective-permute-start.17 = (bf16[64,512]{1,0:T(8,128)(2,1)S(1)}, bf16[64,512]{1,0:T(8,128)(2,1)S(1)}, u32[]{:S(2)}, u32[]{:S(2)}) collective-permute-start(bf16[64,512]{1,0:T(8,128)(2,1)S(1)} %get-tuple-element.75), channel_id=1, source_target_pairs={{0,3},{1,2},{2,1},{3,0},{4,7},{5,6},{6,5},{7,4},{8,11},{9,10},{10,... | collective-permute-start | bytes 196616 | tf_op jit(solution)/shard_map/ppermute | solution.py:23
  46.0 0.1 shard_map.98
  46.1 0.0 collective-permute-done.5.odd_first_ref
  46.1 0.1 collective-permute-start.11
  46.2 0.0 collective-permute-done.6.pair_second_ref
  46.2 0.0 collective-permute-done.7.odd_second_ref
  46.2 1.2 %shard_map.96 = bf16[2,2,64,512]{3,2,1,0:T(8,128)(2,1)} custom-call(f32[256,512]{1,0:T(8,128)S(1)} %get-tuple-element.52.own_ref, f32[256,512]{1,0:T(8,128)S(1)} %get-tuple-element.53.enter_ref, f32[128,512]{1,0:T(8,128)S(1)} %get-tuple-element.54.slope_top_first_ref, f32[128,512]{1,0:T(8,128)S(1)} %get-tuple-element.55.slope_low_first_ref, ...), custom_call_target="tpu_custom_call" | custom-call | tf_op jit(solution)/shard_map/pallas_call | solution.py:52
  47.4 3.6 %collective-permute-done.16.refs_1_ = bf16[64,512]{1,0:T(8,128)(2,1)S(1)} collective-permute-done((bf16[64,512]{1,0:T(8,128)(2,1)S(1)}, bf16[64,512]{1,0:T(8,128)(2,1)S(1)}, u32[]{:S(2)}, u32[]{:S(2)}) %collective-permute-start.16) | collective-permute-done | bytes 65568 | tf_op jit(solution)/shard_map/ppermute | solution.py:23
  51.1 0.6 %collective-permute-done.11.refs_0_ = bf16[64,512]{1,0:T(8,128)(2,1)S(1)} collective-permute-done((bf16[64,512]{1,0:T(8,128)(2,1)S(1)}, bf16[64,512]{1,0:T(8,128)(2,1)S(1)}, u32[]{:S(2)}, u32[]{:S(2)}) %collective-permute-start.11) | collective-permute-done | bytes 65568 | tf_op jit(solution)/shard_map/ppermute | solution.py:23
  51.7 0.7 %shard_map.101 = (f32[192,128]{1,0:T(8,128)}, f32[64,128]{1,0:T(8,128)}) custom-call(f32[64,512]{1,0:T(8,128)S(1)} %get-tuple-element.67.keep_ref, bf16[64,512]{1,0:T(8,128)(2,1)S(1)} %collective-permute-done.11.refs_0_, bf16[64,512]{1,0:T(8,128)(2,1)S(1)} %collective-permute-done.16.refs_1_, bf16[64,512]{1,0:T(8,128)(2,1)S(1)} %collective-permute-done.17.refs_2_), custom_call_target="tpu_custom_call" | custom-call | tf_op jit(solution)/shard_map/pallas_call | solution.py:52
  (9 shorter events, 0.0 us)
Async XLA Ops:
  0.6 10.6 %copy-start.3 = (bf16[2,2,64,512]{3,2,1,0:T(8,128)(2,1)S(1)}, bf16[2,2,64,512]{3,2,1,0:T(8,128)(2,1)}, u32[]{:S(2)}) copy-start(bf16[2,2,64,512]{3,2,1,0:T(8,128)(2,1)} %cotangent_ref.1) | copy-start | bytes 786436
  0.6 10.6 %copy-start.4 = (bf16[512,512]{1,0:T(8,128)(2,1)S(1)}, bf16[512,512]{1,0:T(8,128)(2,1)}, u32[]{:S(2)}) copy-start(bf16[512,512]{1,0:T(8,128)(2,1)} %refs_7_.1) | copy-start | bytes 1572868
  2.0 9.3 %copy-start = (bf16[1536,512]{1,0:T(8,128)(2,1)S(1)}, bf16[1536,512]{1,0:T(8,128)(2,1)}, u32[]{:S(2)}) copy-start(bf16[1536,512]{1,0:T(8,128)(2,1)} %weight_ref.3) | copy-start | bytes 4718596
  2.0 9.3 %copy-start.1 = (bf16[3,2,2,64,512]{4,3,2,1,0:T(8,128)(2,1)S(1)}, bf16[3,2,2,64,512]{4,3,2,1,0:T(8,128)(2,1)}, u32[]{:S(2)}) copy-start(bf16[3,2,2,64,512]{4,3,2,1,0:T(8,128)(2,1)} %refs_9_.1) | copy-start | bytes 2359300
  2.0 9.3 %copy-start.2 = (bf16[2,2,64,512]{3,2,1,0:T(8,128)(2,1)S(1)}, bf16[2,2,64,512]{3,2,1,0:T(8,128)(2,1)}, u32[]{:S(2)}) copy-start(bf16[2,2,64,512]{3,2,1,0:T(8,128)(2,1)} %refs_8_.1) | copy-start | bytes 786436
  2.0 9.3 %copy-start.5 = (s32[3,2,2,64]{3,2,1,0:T(2,128)S(1)}, s32[3,2,2,64]{3,2,1,0:T(2,128)}, u32[]{:S(2)}) copy-start(s32[3,2,2,64]{3,2,1,0:T(2,128)} %refs_10_.1) | copy-start | bytes 9220
  2.1 7.6 %collective-permute-start = (bf16[272,512]{1,0:T(8,128)(2,1)S(1)}, bf16[272,512]{1,0:T(8,128)(2,1)S(1)}, u32[]{:S(2)}, u32[]{:S(2)}) collective-permute-start(bf16[272,512]{1,0:T(8,128)(2,1)S(1)} %get-tuple-element.47), channel_id=1, source_target_pairs={{0,4},{8,12},{16,20},{24,28},{4,0},{12,8},{20,16},{28,24},{1,5},{9... | collective-permute-start | bytes 835592 | tf_op jit(solution)/shard_map/ppermute | solution.py:18
  2.6 7.1 %collective-permute-start.1 = (bf16[272,512]{1,0:T(8,128)(2,1)S(1)}, bf16[272,512]{1,0:T(8,128)(2,1)S(1)}, u32[]{:S(2)}, u32[]{:S(2)}) collective-permute-start(bf16[272,512]{1,0:T(8,128)(2,1)S(1)} %get-tuple-element.48), channel_id=1, source_target_pairs={{4,8},{12,16},{20,24},{8,4},{16,12},{24,20},{5,9},{13,17},{21,25},... | collective-permute-start | bytes 835592 | tf_op jit(solution)/shard_map/ppermute | solution.py:18
  3.4 7.8 %collective-permute-start.2 = (bf16[272,512]{1,0:T(8,128)(2,1)S(1)}, bf16[272,512]{1,0:T(8,128)(2,1)S(1)}, u32[]{:S(2)}, u32[]{:S(2)}) collective-permute-start(bf16[272,512]{1,0:T(8,128)(2,1)S(1)} %get-tuple-element.49), channel_id=1, source_target_pairs={{0,1},{2,3},{1,0},{3,2},{4,5},{6,7},{5,4},{7,6},{8,9},{10,11},{9,8... | collective-permute-start | bytes 835592 | tf_op jit(solution)/shard_map/ppermute | solution.py:18
  6.1 5.2 %collective-permute-start.3 = (bf16[272,512]{1,0:T(8,128)(2,1)S(1)}, bf16[272,512]{1,0:T(8,128)(2,1)S(1)}, u32[]{:S(2)}, u32[]{:S(2)}) collective-permute-start(bf16[272,512]{1,0:T(8,128)(2,1)S(1)} %get-tuple-element.50), channel_id=1, source_target_pairs={{1,2},{2,1},{5,6},{6,5},{9,10},{10,9},{13,14},{14,13},{17,18},{18,... | collective-permute-start | bytes 835592 | tf_op jit(solution)/shard_map/ppermute | solution.py:18
  15.5 10.7 %collective-permute-start.4 = (bf16[640,512]{1,0:T(8,128)(2,1)S(1)}, bf16[640,512]{1,0:T(8,128)(2,1)S(1)}, u32[]{:S(2)}, u32[]{:S(2)}) collective-permute-start(bf16[640,512]{1,0:T(8,128)(2,1)S(1)} %get-tuple-element.58), channel_id=1, source_target_pairs={{0,4},{8,12},{16,20},{24,28},{4,0},{12,8},{20,16},{28,24},{1,5},{9... | collective-permute-start | bytes 1966088 | tf_op jit(solution)/shard_map/ppermute | solution.py:18
  17.8 2.5 %collective-permute-start.12 = (bf16[512,512]{1,0:T(8,128)(2,1)S(1)}, bf16[512,512]{1,0:T(8,128)(2,1)S(1)}, u32[]{:S(2)}, u32[]{:S(2)}) collective-permute-start(bf16[512,512]{1,0:T(8,128)(2,1)S(1)} %get-tuple-element.69), channel_id=1, source_target_pairs={{0,4},{8,12},{16,20},{24,28},{4,0},{12,8},{20,16},{28,24},{1,5},{9... | collective-permute-start | bytes 1572872 | tf_op jit(solution)/shard_map/ppermute | solution.py:18
  20.4 8.0 %collective-permute-start.13 = (bf16[128,512]{1,0:T(8,128)(2,1)S(1)}, bf16[128,512]{1,0:T(8,128)(2,1)S(1)}, u32[]{:S(2)}, u32[]{:S(2)}) collective-permute-start(bf16[128,512]{1,0:T(8,128)(2,1)S(1)} %get-tuple-element.71), channel_id=1, source_target_pairs={{0,8},{4,12},{8,0},{12,4},{16,24},{20,28},{24,16},{28,20},{1,9},{5... | collective-permute-start | bytes 393224 | tf_op jit(solution)/shard_map/ppermute | solution.py:23
  23.7 7.7 %collective-permute-start.14 = (bf16[128,512]{1,0:T(8,128)(2,1)S(1)}, bf16[128,512]{1,0:T(8,128)(2,1)S(1)}, u32[]{:S(2)}, u32[]{:S(2)}) collective-permute-start(bf16[128,512]{1,0:T(8,128)(2,1)S(1)} %get-tuple-element.72), channel_id=1, source_target_pairs={{0,16},{4,20},{8,24},{12,28},{16,0},{20,4},{24,8},{28,12},{1,17},{... | collective-permute-start | bytes 393224 | tf_op jit(solution)/shard_map/ppermute | solution.py:23
  24.7 8.6 %collective-permute-start.15 = (bf16[128,512]{1,0:T(8,128)(2,1)S(1)}, bf16[128,512]{1,0:T(8,128)(2,1)S(1)}, u32[]{:S(2)}, u32[]{:S(2)}) collective-permute-start(bf16[128,512]{1,0:T(8,128)(2,1)S(1)} %get-tuple-element.73), channel_id=1, source_target_pairs={{0,24},{4,28},{8,16},{12,20},{16,8},{20,12},{24,0},{28,4},{1,25},{... | collective-permute-start | bytes 393224 | tf_op jit(solution)/shard_map/ppermute | solution.py:23
  26.2 12.1 %collective-permute-start.8 = (bf16[128,512]{1,0:T(8,128)(2,1)S(1)}, bf16[128,512]{1,0:T(8,128)(2,1)S(1)}, u32[]{:S(2)}, u32[]{:S(2)}) collective-permute-start(bf16[128,512]{1,0:T(8,128)(2,1)S(1)} %get-tuple-element.64), channel_id=1, source_target_pairs={{0,8},{4,12},{8,0},{12,4},{16,24},{20,28},{24,16},{28,20},{1,9},{5... | collective-permute-start | bytes 393224 | tf_op jit(solution)/shard_map/ppermute | solution.py:23
  27.4 11.6 %collective-permute-start.9 = (bf16[128,512]{1,0:T(8,128)(2,1)S(1)}, bf16[128,512]{1,0:T(8,128)(2,1)S(1)}, u32[]{:S(2)}, u32[]{:S(2)}) collective-permute-start(bf16[128,512]{1,0:T(8,128)(2,1)S(1)} %get-tuple-element.65), channel_id=1, source_target_pairs={{0,16},{4,20},{8,24},{12,28},{16,0},{20,4},{24,8},{28,12},{1,17},{... | collective-permute-start | bytes 393224 | tf_op jit(solution)/shard_map/ppermute | solution.py:23
  28.4 15.7 %collective-permute-start.10 = (bf16[128,512]{1,0:T(8,128)(2,1)S(1)}, bf16[128,512]{1,0:T(8,128)(2,1)S(1)}, u32[]{:S(2)}, u32[]{:S(2)}) collective-permute-start(bf16[128,512]{1,0:T(8,128)(2,1)S(1)} %get-tuple-element.66), channel_id=1, source_target_pairs={{0,24},{4,28},{8,16},{12,20},{16,8},{20,12},{24,0},{28,4},{1,25},{... | collective-permute-start | bytes 393224 | tf_op jit(solution)/shard_map/ppermute | solution.py:23
  31.4 14.7 %collective-permute-start.5 = (bf16[128,512]{1,0:T(8,128)(2,1)S(1)}, bf16[128,512]{1,0:T(8,128)(2,1)S(1)}, u32[]{:S(2)}, u32[]{:S(2)}) collective-permute-start(bf16[128,512]{1,0:T(8,128)(2,1)S(1)} %get-tuple-element.59), channel_id=1, source_target_pairs={{4,8},{12,16},{20,24},{8,4},{16,12},{24,20},{5,9},{13,17},{21,25},... | collective-permute-start | bytes 393224 | tf_op jit(solution)/shard_map/ppermute | solution.py:18
  33.3 12.9 %collective-permute-start.6 = (bf16[128,512]{1,0:T(8,128)(2,1)S(1)}, bf16[128,512]{1,0:T(8,128)(2,1)S(1)}, u32[]{:S(2)}, u32[]{:S(2)}) collective-permute-start(bf16[128,512]{1,0:T(8,128)(2,1)S(1)} %get-tuple-element.60), channel_id=1, source_target_pairs={{0,1},{2,3},{1,0},{3,2},{4,5},{6,7},{5,4},{7,6},{8,9},{10,11},{9,8... | collective-permute-start | bytes 393224 | tf_op jit(solution)/shard_map/ppermute | solution.py:18
  38.3 7.9 %collective-permute-start.7 = (bf16[128,512]{1,0:T(8,128)(2,1)S(1)}, bf16[128,512]{1,0:T(8,128)(2,1)S(1)}, u32[]{:S(2)}, u32[]{:S(2)}) collective-permute-start(bf16[128,512]{1,0:T(8,128)(2,1)S(1)} %get-tuple-element.61), channel_id=1, source_target_pairs={{1,2},{2,1},{5,6},{6,5},{9,10},{10,9},{13,14},{14,13},{17,18},{18,... | collective-permute-start | bytes 393224 | tf_op jit(solution)/shard_map/ppermute | solution.py:18
  39.1 12.0 %collective-permute-start.16 = (bf16[64,512]{1,0:T(8,128)(2,1)S(1)}, bf16[64,512]{1,0:T(8,128)(2,1)S(1)}, u32[]{:S(2)}, u32[]{:S(2)}) collective-permute-start(bf16[64,512]{1,0:T(8,128)(2,1)S(1)} %get-tuple-element.74), channel_id=1, source_target_pairs={{0,2},{1,3},{2,0},{3,1},{4,6},{5,7},{6,4},{7,5},{8,10},{9,11},{10,... | collective-permute-start | bytes 196616 | tf_op jit(solution)/shard_map/ppermute | solution.py:23
  44.1 7.0 %collective-permute-start.17 = (bf16[64,512]{1,0:T(8,128)(2,1)S(1)}, bf16[64,512]{1,0:T(8,128)(2,1)S(1)}, u32[]{:S(2)}, u32[]{:S(2)}) collective-permute-start(bf16[64,512]{1,0:T(8,128)(2,1)S(1)} %get-tuple-element.75), channel_id=1, source_target_pairs={{0,3},{1,2},{2,1},{3,0},{4,7},{5,6},{6,5},{7,4},{8,11},{9,10},{10,... | collective-permute-start | bytes 196616 | tf_op jit(solution)/shard_map/ppermute | solution.py:23
  46.1 5.6 %collective-permute-start.11 = (bf16[64,512]{1,0:T(8,128)(2,1)S(1)}, bf16[64,512]{1,0:T(8,128)(2,1)S(1)}, u32[]{:S(2)}, u32[]{:S(2)}) collective-permute-start(bf16[64,512]{1,0:T(8,128)(2,1)S(1)} %get-tuple-element.68), channel_id=1, source_target_pairs={{0,1},{1,0},{2,3},{3,2},{4,5},{5,4},{6,7},{7,6},{8,9},{9,8},{10,11... | collective-permute-start | bytes 196616 | tf_op jit(solution)/shard_map/ppermute | solution.py:23

commit v7 on v5

--- a/solution.py
+++ b/solution.py
@@ -209,8 +209,8 @@
     pair_first_ref, odd_first_ref, pair_second_ref, odd_second_ref,
     new_ref, grad_odd_first_ref, grad_pair_second_ref, grad_odd_second_ref,
     own_ref, enter_ref, slope_top_first_ref, slope_low_first_ref, slope_top_second_ref, slope_low_second_ref,
-    grad_pair_first_ref, send_ref, keep_ref,
-    summed_ref, update_ref, grad_ref, grad_low_ref, grads_ref, total_ref,
+    grad_pair_first_ref, far_send_ref, total_ref,
+    summed_ref, update_ref, grad_ref, grad_low_ref, grads_ref,
 ):
     ex, ey, nz, features = dims
     at_first, at_second = lax.axis_index("gx"), lax.axis_index("gy")
@@ -263,10 +263,9 @@
     cotangent = cotangent_ref[...].reshape(-1, features).astype(F32)
     update_ref[...] = (cotangent * (gate * (1.0 + update * (1.0 - gate)))).astype(BF16)
     grad_summed = dot_nt(update_ref[...], node_weight_ref[...]).astype(BF16)
-    pair_target, extra = (grad_pair_first_ref, 0) if send_ref is None else (send_ref, send_ref.shape[0] - rows_first)
     for y in range(ey):
         low, top = grad_summed[rows(0, y)], grad_summed[rows(ex - 1, y)]
-        pair_target[extra + y * nz : extra + (y + 1) * nz] = jnp.where(even_first, top, low)
+        grad_pair_first_ref[part(y)] = jnp.where(even_first, top, low)
         grad_odd_first_ref[part(y)] = jnp.where(even_first, low, top)
     for x in range(ex):
         low, top = grad_summed[rows(x, 0)], grad_summed[rows(x, ey - 1)]
@@ -328,28 +327,35 @@
     )
     total_ref[3 * features :] = dot_tn(summed_ref[...], update_ref[...])
 
-    if send_ref is None:
-        keep_ref[...] = total_ref[...]
-        return
-    planes = keep_ref.shape[0]
-    seconds, chunk = lax.axis_size("gy"), keep_ref.shape[1] // lax.axis_size("gy")
-    edge_rows, node_rows = chunk * 3 // 4, chunk // 4
-    core, plane = at_first % 2, at_first // 2
-    for block in range(planes):
-        for second in range(seconds):
-            there = (plane ^ block) * 2
-            start = second * chunk
-            for flip in (core, 1 - core):
-                device = (there + flip) * seconds + (at_second ^ second)
-                edge = total_ref[pl.ds(pl.multiple_of(device * edge_rows, 8), edge_rows)]
-                node = total_ref[pl.ds(pl.multiple_of(3 * features + device * node_rows, 8), node_rows)]
-                if flip is core:
-                    keep_ref[block, start : start + edge_rows] = edge
-                    keep_ref[block, start + edge_rows : start + chunk] = node
-                else:
-                    send_at = block * seconds * chunk + start
-                    send_ref[send_at : send_at + edge_rows] = edge.astype(BF16)
-                    send_ref[send_at + edge_rows : send_at + chunk] = node.astype(BF16)
+    if far_send_ref is not None:
+        seconds = lax.axis_size("gy")
+        send_chunks(total_ref, far_send_ref, range(seconds // 2, seconds))
+
+
+def chunk_of(total_ref, flip, plane, second):
+    devices = lax.axis_size("gx") * lax.axis_size("gy")
+    node_rows = total_ref.shape[0] // 4 // devices
+    edge_rows = 3 * node_rows
+    at_first, at_second = lax.axis_index("gx"), lax.axis_index("gy")
+    first = ((at_first // 2) ^ plane) * 2 + (1 - at_first % 2 if flip else at_first % 2)
+    device = first * lax.axis_size("gy") + (at_second ^ second)
+    edge_at = pl.multiple_of(device * edge_rows, PAD)
+    node_at = pl.multiple_of(total_ref.shape[0] * 3 // 4 + device * node_rows, PAD)
+    return (edge_at, edge_rows), (node_at, node_rows)
+
+
+def send_chunks(total_ref, send_ref, seconds):
+    at = 0
+    for plane in range(lax.axis_size("gx") // 2):
+        for second in seconds:
+            for start, size in chunk_of(total_ref, True, plane, second):
+                send_ref[at : at + size] = total_ref[pl.ds(start, size)].astype(BF16)
+                at += size
+
+
+def near_pack_kernel(total_ref, grad_ref, send_ref):
+    send_chunks(total_ref, send_ref, range(lax.axis_size("gy") // 2))
+    send_ref[send_ref.shape[0] - grad_ref.shape[0] :] = grad_ref[...]
 
 
 def node_grad_kernel(
@@ -390,20 +396,15 @@
     out_ref[...] = result.astype(BF16).reshape(out_ref.shape)
 
 
-def pair_sum_kernel(keep_ref, received_ref, near_kept_ref, far_kept_ref, *send_refs):
-    near, far = near_kept_ref.shape[0], far_kept_ref.shape[0]
-    planes = len(send_refs) // 2 + 1
-    for plane in range(planes):
-        start = plane * (near + far)
-        for first, size, kept_ref, sends in (
-            (near, far, far_kept_ref, send_refs[: planes - 1]),
-            (0, near, near_kept_ref, send_refs[planes - 1 :]),
-        ):
-            total = keep_ref[plane, first : first + size] + received_ref[start + first : start + first + size].astype(F32)
-            if plane == 0:
-                kept_ref[...] = total
-            else:
-                sends[plane - 1][...] = total.astype(BF16)
+def pair_sum_kernel(seconds, total_ref, received_ref, kept_ref, *send_refs):
+    at = 0
+    for plane, out in enumerate((kept_ref, *send_refs)):
+        here = 0
+        for second in seconds:
+            for start, size in chunk_of(total_ref, False, plane, second):
+                total = total_ref[pl.ds(start, size)] + received_ref[at : at + size].astype(F32)
+                out[here : here + size] = total.astype(out.dtype)
+                at, here = at + size, here + size
 
 
 def plane_sum_kernel(received, *refs):
@@ -483,14 +484,14 @@
     planes = firsts // 2
     outs = [(node_features.shape, BF16), (face_first, BF16), (face_second, BF16), (face_second, BF16)]
     outs += [((count, features), F32)] * 2 + [(face_first, F32)] * 2 + [(face_second, F32)] * 2
+    outs += [(face_first, BF16)]
+    total_out = ((total_rows, features), F32)
+    near, far = seconds // 2 * chunk, (seconds - seconds // 2) * chunk
     if by_hand:
-        outs += [((planes * seconds * chunk + ey * nz, features), BF16), ((planes, seconds * chunk, features), F32)]
-
-        def kernel(*refs):
-            layer_kernel(dims, *refs[:26], None, *refs[26:])
-
+        outs += [((planes * far, features), BF16), total_out]
+        kernel = functools.partial(layer_kernel, dims)
     else:
-        outs += [(face_first, BF16), ((total_rows, features), F32)]
+        outs += [total_out]
 
         def kernel(*refs):
             layer_kernel(dims, *refs[:27], None, *refs[27:])
@@ -509,12 +510,14 @@
             pltpu.VMEM((3, count, features), F32),
             pltpu.VMEM((low_rows, features), F32),
             pltpu.VMEM((3 * count + low_rows, features), BF16),
-            pltpu.VMEM((total_rows, features), F32),
         ],
         limit=14 << 20,
     )
     new_nodes, odd_first, pair_second, odd_second = results[:4]
-    received, keep = results[10:]
+    received, total = results[10], results[-1]
+    if by_hand:
+        far_received = swapped(results[11], "gx", 0)
+        (received,) = call(near_pack_kernel, [((planes * near + ey * nz, features), BF16)], [total, received])
     received = swapped(received, "gx", 0)
     pair_second = swapped(pair_second, "gy", 0)
     odd_second = swapped(odd_second, "gy", 1)
@@ -527,15 +530,19 @@
         ],
     )
     if not by_hand:
-        total = keep
         edge_part = lax.psum_scatter(total[: 3 * features].reshape(-1), ("gx", "gy"), scatter_dimension=0, tiled=True)
         node_part = lax.psum_scatter(total[3 * features :].reshape(-1), ("gx", "gy"), scatter_dimension=0, tiled=True)
         return new_nodes, node_grad, edge_part, node_part
 
-    near, far = (seconds // 2 * chunk, features), ((seconds - seconds // 2) * chunk, features)
-    near_kept, far_kept, *sends = call(
-        pair_sum_kernel, [(near, F32), (far, F32)] + [(far, BF16)] * (planes - 1) + [(near, BF16)] * (planes - 1), [keep, received]
-    )
+    def summed_pairs(places, size, arrived):
+        return call(
+            functools.partial(pair_sum_kernel, places),
+            [((size, features), F32)] + [((size, features), BF16)] * (planes - 1),
+            [total, arrived],
+        )
+
+    far_kept, *far_sends = summed_pairs(range(seconds // 2, seconds), far, far_received)
+    near_kept, *near_sends = summed_pairs(range(seconds // 2), near, received)
 
     def over_planes(values):
         arrived = []
@@ -543,7 +550,7 @@
             arrived.append(exchanged(value, "gx", 2 * (index + 1)))
         return arrived
 
-    far_arrived, near_arrived = over_planes(sends[: planes - 1]), over_planes(sends[planes - 1 :])
+    far_arrived, near_arrived = over_planes(far_sends), over_planes(near_sends)
     piece = ((chunk, features), BF16)
     far_sends = call(
         functools.partial(plane_sum_kernel, planes - 1), [piece] * (seconds - seconds // 2), [far_kept, *far_arrived]

time: 52.2 us -> 51.8 us (level)
  Pallas kernels: 10.7 us -> 9.88 us
    pallas_call x8 -> x10, Pallas kernels: 10.7 us -> 9.88 us  [call(): pl.pallas_call(kernel, out_shape=[jax.ShapeDtypeStruct(shape, dtype) for...]
    ppermute x8 -> x9, starting transfers between devices: 13.6 us -> 13.5 us  [swapped(): lax.ppermute(value, axis, [(at, at + 1) for at in lower] + [(at + 1, at)...]
    ppermute x8 -> x9, waiting for transfers between devices: 4.04 us -> 3.96 us  [swapped(): lax.ppermute(value, axis, [(at, at + 1) for at in lower] + [(at + 1, at)...]
  transfers between devices with their start and end apart: 17 -> 18, of which waited for: 5 -> 6; matrix products, arithmetic and copies ran while one was open for 0% -> 0% of each run, Pallas kernels for 8% -> 9%
where the time goes in v7:
time: 51.8 us; the launch traced here: 51.6 us
  starting transfers between devices  30 us (58%)
  waiting for transfers between devices  10.8 us (21%)
  Pallas kernels  9.88 us (19%)
  between operations  0.86 us (2%)
    ppermute x9, starting transfers between devices, exchanged(): lax.ppermute(value, axis, [(source, source ^ flip) for source in range(co...  16.6 us
    ppermute x9, starting transfers between devices, swapped(): lax.ppermute(value, axis, [(at, at + 1) for at in lower] + [(at + 1, at)...  13.5 us
    pallas_call x10, Pallas kernels, call(): pl.pallas_call(kernel, out_shape=[jax.ShapeDtypeStruct(shape, dtype) for...  9.88 us
    ppermute x9, waiting for transfers between devices, exchanged(): lax.ppermute(value, axis, [(source, source ^ flip) for source in range(co...  6.83 us
    ppermute x9, waiting for transfers between devices, swapped(): lax.ppermute(value, axis, [(at, at + 1) for at in lower] + [(at + 1, at)...  3.96 us
  transfers between devices with their start and end apart: 18, of which 6 were waited for; matrix products, arithmetic and copies ran while one was open for 0% of the time, Pallas kernels for 9%

profile of v7, /device:TPU:0, one launch (start us, length us, event | category | flops | bytes accessed | tf_op | source)
XLA Modules:
  0.0 51.6 jit_solution(13537768285208499906)
XLA Ops:
  0.7 1.4 %shard_map.94 = (bf16[272,512]{1,0:T(8,128)(2,1)S(1)}, bf16[272,512]{1,0:T(8,128)(2,1)S(1)}, bf16[272,512]{1,0:T(8,128)(2,1)S(1)}, bf16[272,512]{1,0:T(8,128)(2,1)S(1)}) custom-call(bf16[2,2,64,512]{3,2,1,0:T(8,128)(2,1)} %node_ref.5, bf16[3,2,2,64,512]{4,3,2,1,0:T(8,128)(2,1)} %edge_ref.5, s32[3,2,2,64]{3,2,1,0:T(2,128)} %open_ref.1), custom_call_target="tpu_custom_call" | custom-call | tf_op jit(solution)/shard_map/pallas_call | solution.py:52
  2.0 0.0 copy-start
  2.0 0.0 copy-start.1
  2.0 0.0 copy-start.2
  2.0 0.0 copy-start.5
  2.1 0.6 %collective-permute-start = (bf16[272,512]{1,0:T(8,128)(2,1)S(1)}, bf16[272,512]{1,0:T(8,128)(2,1)S(1)}, u32[]{:S(2)}, u32[]{:S(2)}) collective-permute-start(bf16[272,512]{1,0:T(8,128)(2,1)S(1)} %get-tuple-element.47), channel_id=1, source_target_pairs={{0,4},{8,12},{16,20},{24,28},{4,0},{12,8},{20,16},{28,24},{1,5},{9... | collective-permute-start | bytes 835592 | tf_op jit(solution)/shard_map/ppermute | solution.py:18
  2.6 0.8 %collective-permute-start.1 = (bf16[272,512]{1,0:T(8,128)(2,1)S(1)}, bf16[272,512]{1,0:T(8,128)(2,1)S(1)}, u32[]{:S(2)}, u32[]{:S(2)}) collective-permute-start(bf16[272,512]{1,0:T(8,128)(2,1)S(1)} %get-tuple-element.48), channel_id=1, source_target_pairs={{4,8},{12,16},{20,24},{8,4},{16,12},{24,20},{5,9},{13,17},{21,25},... | collective-permute-start | bytes 835592 | tf_op jit(solution)/shard_map/ppermute | solution.py:18
  3.4 2.6 %collective-permute-start.2 = (bf16[272,512]{1,0:T(8,128)(2,1)S(1)}, bf16[272,512]{1,0:T(8,128)(2,1)S(1)}, u32[]{:S(2)}, u32[]{:S(2)}) collective-permute-start(bf16[272,512]{1,0:T(8,128)(2,1)S(1)} %get-tuple-element.49), channel_id=1, source_target_pairs={{0,1},{2,3},{1,0},{3,2},{4,5},{6,7},{5,4},{7,6},{8,9},{10,11},{9,8... | collective-permute-start | bytes 835592 | tf_op jit(solution)/shard_map/ppermute | solution.py:18
  6.1 0.7 %collective-permute-start.3 = (bf16[272,512]{1,0:T(8,128)(2,1)S(1)}, bf16[272,512]{1,0:T(8,128)(2,1)S(1)}, u32[]{:S(2)}, u32[]{:S(2)}) collective-permute-start(bf16[272,512]{1,0:T(8,128)(2,1)S(1)} %get-tuple-element.50), channel_id=1, source_target_pairs={{1,2},{2,1},{5,6},{6,5},{9,10},{10,9},{13,14},{14,13},{17,18},{18,... | collective-permute-start | bytes 835592 | tf_op jit(solution)/shard_map/ppermute | solution.py:18
  6.7 2.9 %shard_map.93 = (f32[256,512]{1,0:T(8,128)S(1)}, f32[3,256,512]{2,1,0:T(8,128)S(1)}, f32[128,512]{1,0:T(8,128)S(1)}, f32[128,512]{1,0:T(8,128)S(1)}, f32[128,512]{1,0:T(8,128)S(1)}, /*index=5*/f32[128,512]{1,0:T(8,128)S(1)}) custom-call(bf16[2,2,64,512]{3,2,1,0:T(8,128)(2,1)} %node_ref.5, bf16[3,2,2,64,512]{4,3,2,1,0:T(8,128)(2,1)} %edge_ref.5, ...), custom_call_target="tpu_custom_call" | custom-call | tf_op jit(solution)/shard_map/pallas_call | solution.py:52
  9.7 0.0 collective-permute-done.pair_first_ref
  9.7 0.0 collective-permute-done.1.odd_first_ref
  9.7 1.5 %collective-permute-done.2.pair_second_ref = bf16[272,512]{1,0:T(8,128)(2,1)S(1)} collective-permute-done((bf16[272,512]{1,0:T(8,128)(2,1)S(1)}, bf16[272,512]{1,0:T(8,128)(2,1)S(1)}, u32[]{:S(2)}, u32[]{:S(2)}) %collective-permute-start.2) | collective-permute-done | bytes 278560 | tf_op jit(solution)/shard_map/ppermute | solution.py:18
  11.3 0.0 collective-permute-done.3.odd_second_ref
  11.3 3.3 %shard_map.95 = (bf16[2,2,64,512]{3,2,1,0:T(8,128)(2,1)}, bf16[128,512]{1,0:T(8,128)(2,1)S(1)}, bf16[128,512]{1,0:T(8,128)(2,1)S(1)}, bf16[128,512]{1,0:T(8,128)...) custom-call(f32[256,512]{1,0:T(8,128)S(1)} %get-tuple-element.41.sum, ...), custom_call_target="tpu_custom_call" | custom-call | tf_op jit(solution)/shard_map/pallas_call | solution.py:52
  14.6 0.1 shard_map.96
  14.7 2.4 %collective-permute-start.4 = (bf16[640,512]{1,0:T(8,128)(2,1)S(1)}, bf16[640,512]{1,0:T(8,128)(2,1)S(1)}, u32[]{:S(2)}, u32[]{:S(2)}) collective-permute-start(bf16[640,512]{1,0:T(8,128)(2,1)S(1)} %shard_map.96), channel_id=1, source_target_pairs={{0,4},{8,12},{16,20},{24,28},{4,0},{12,8},{20,16},{28,24},{1,5},{9... | collective-permute-start | bytes 1966088 | tf_op jit(solution)/shard_map/ppermute | solution.py:18
  17.0 0.1 collective-permute-start.12
  17.1 2.4 %collective-permute-done.12.received_ref = bf16[512,512]{1,0:T(8,128)(2,1)S(1)} collective-permute-done((bf16[512,512]{1,0:T(8,128)(2,1)S(1)}, bf16[512,512]{1,0:T(8,128)(2,1)S(1)}, u32[]{:S(2)}, u32[]{:S(2)}) %collective-permute-start.12) | collective-permute-done | bytes 524320 | tf_op jit(solution)/shard_map/ppermute | solution.py:18
  19.5 0.1 shard_map.100
  19.6 3.4 %collective-permute-start.13 = (bf16[128,512]{1,0:T(8,128)(2,1)S(1)}, bf16[128,512]{1,0:T(8,128)(2,1)S(1)}, u32[]{:S(2)}, u32[]{:S(2)}) collective-permute-start(bf16[128,512]{1,0:T(8,128)(2,1)S(1)} %get-tuple-element.71), channel_id=1, source_target_pairs={{0,8},{4,12},{8,0},{12,4},{16,24},{20,28},{24,16},{28,20},{1,9},{5... | collective-permute-start | bytes 393224 | tf_op jit(solution)/shard_map/ppermute | solution.py:23
  23.0 1.0 %collective-permute-start.14 = (bf16[128,512]{1,0:T(8,128)(2,1)S(1)}, bf16[128,512]{1,0:T(8,128)(2,1)S(1)}, u32[]{:S(2)}, u32[]{:S(2)}) collective-permute-start(bf16[128,512]{1,0:T(8,128)(2,1)S(1)} %get-tuple-element.72), channel_id=1, source_target_pairs={{0,16},{4,20},{8,24},{12,28},{16,0},{20,4},{24,8},{28,12},{1,17},{... | collective-permute-start | bytes 393224 | tf_op jit(solution)/shard_map/ppermute | solution.py:23
  24.0 1.4 %collective-permute-start.15 = (bf16[128,512]{1,0:T(8,128)(2,1)S(1)}, bf16[128,512]{1,0:T(8,128)(2,1)S(1)}, u32[]{:S(2)}, u32[]{:S(2)}) collective-permute-start(bf16[128,512]{1,0:T(8,128)(2,1)S(1)} %get-tuple-element.73), channel_id=1, source_target_pairs={{0,24},{4,28},{8,16},{12,20},{16,8},{20,12},{24,0},{28,4},{1,25},{... | collective-permute-start | bytes 393224 | tf_op jit(solution)/shard_map/ppermute | solution.py:23
  25.4 0.0 collective-permute-done.4.pair_first_ref.received_ref
  25.4 0.1 shard_map.98
  25.5 1.2 %collective-permute-start.8 = (bf16[128,512]{1,0:T(8,128)(2,1)S(1)}, bf16[128,512]{1,0:T(8,128)(2,1)S(1)}, u32[]{:S(2)}, u32[]{:S(2)}) collective-permute-start(bf16[128,512]{1,0:T(8,128)(2,1)S(1)} %get-tuple-element.64), channel_id=1, source_target_pairs={{0,8},{4,12},{8,0},{12,4},{16,24},{20,28},{24,16},{28,20},{1,9},{5... | collective-permute-start | bytes 393224 | tf_op jit(solution)/shard_map/ppermute | solution.py:23
  26.7 1.0 %collective-permute-start.9 = (bf16[128,512]{1,0:T(8,128)(2,1)S(1)}, bf16[128,512]{1,0:T(8,128)(2,1)S(1)}, u32[]{:S(2)}, u32[]{:S(2)}) collective-permute-start(bf16[128,512]{1,0:T(8,128)(2,1)S(1)} %get-tuple-element.65), channel_id=1, source_target_pairs={{0,16},{4,20},{8,24},{12,28},{16,0},{20,4},{24,8},{28,12},{1,17},{... | collective-permute-start | bytes 393224 | tf_op jit(solution)/shard_map/ppermute | solution.py:23
  27.7 0.0 collective-permute-done.13.refs_1_
  27.7 1.7 %collective-permute-start.10 = (bf16[128,512]{1,0:T(8,128)(2,1)S(1)}, bf16[128,512]{1,0:T(8,128)(2,1)S(1)}, u32[]{:S(2)}, u32[]{:S(2)}) collective-permute-start(bf16[128,512]{1,0:T(8,128)(2,1)S(1)} %get-tuple-element.66), channel_id=1, source_target_pairs={{0,24},{4,28},{8,16},{12,20},{16,8},{20,12},{24,0},{28,4},{1,25},{... | collective-permute-start | bytes 393224 | tf_op jit(solution)/shard_map/ppermute | solution.py:23
  29.3 1.3 %collective-permute-done.14.refs_2_ = bf16[128,512]{1,0:T(8,128)(2,1)S(1)} collective-permute-done((bf16[128,512]{1,0:T(8,128)(2,1)S(1)}, bf16[128,512]{1,0:T(8,128)(2,1)S(1)}, u32[]{:S(2)}, u32[]{:S(2)}) %collective-permute-start.14) | collective-permute-done | bytes 131104 | tf_op jit(solution)/shard_map/ppermute | solution.py:23
  30.7 0.7 %collective-permute-start.5 = (bf16[128,512]{1,0:T(8,128)(2,1)S(1)}, bf16[128,512]{1,0:T(8,128)(2,1)S(1)}, u32[]{:S(2)}, u32[]{:S(2)}) collective-permute-start(bf16[128,512]{1,0:T(8,128)(2,1)S(1)} %get-tuple-element.60), channel_id=1, source_target_pairs={{4,8},{12,16},{20,24},{8,4},{16,12},{24,20},{5,9},{13,17},{21,25},... | collective-permute-start | bytes 393224 | tf_op jit(solution)/shard_map/ppermute | solution.py:18
  31.4 1.2 %collective-permute-done.15.refs_3_ = bf16[128,512]{1,0:T(8,128)(2,1)S(1)} collective-permute-done((bf16[128,512]{1,0:T(8,128)(2,1)S(1)}, bf16[128,512]{1,0:T(8,128)(2,1)S(1)}, u32[]{:S(2)}, u32[]{:S(2)}) %collective-permute-start.15) | collective-permute-done | bytes 131104 | tf_op jit(solution)/shard_map/ppermute | solution.py:23
  32.6 5.0 %collective-permute-start.6 = (bf16[128,512]{1,0:T(8,128)(2,1)S(1)}, bf16[128,512]{1,0:T(8,128)(2,1)S(1)}, u32[]{:S(2)}, u32[]{:S(2)}) collective-permute-start(bf16[128,512]{1,0:T(8,128)(2,1)S(1)} %get-tuple-element.61), channel_id=1, source_target_pairs={{0,1},{2,3},{1,0},{3,2},{4,5},{6,7},{5,4},{7,6},{8,9},{10,11},{9,8... | collective-permute-start | bytes 393224 | tf_op jit(solution)/shard_map/ppermute | solution.py:18
  37.6 0.0 collective-permute-done.8.refs_1_
  37.6 0.7 %collective-permute-start.7 = (bf16[128,512]{1,0:T(8,128)(2,1)S(1)}, bf16[128,512]{1,0:T(8,128)(2,1)S(1)}, u32[]{:S(2)}, u32[]{:S(2)}) collective-permute-start(bf16[128,512]{1,0:T(8,128)(2,1)S(1)} %get-tuple-element.62), channel_id=1, source_target_pairs={{1,2},{2,1},{5,6},{6,5},{9,10},{10,9},{13,14},{14,13},{17,18},{18,... | collective-permute-start | bytes 393224 | tf_op jit(solution)/shard_map/ppermute | solution.py:18
  38.3 0.1 shard_map.101
  38.3 0.0 collective-permute-done.9.refs_2_
  38.3 5.0 %collective-permute-start.16 = (bf16[64,512]{1,0:T(8,128)(2,1)S(1)}, bf16[64,512]{1,0:T(8,128)(2,1)S(1)}, u32[]{:S(2)}, u32[]{:S(2)}) collective-permute-start(bf16[64,512]{1,0:T(8,128)(2,1)S(1)} %get-tuple-element.74), channel_id=1, source_target_pairs={{0,2},{1,3},{2,0},{3,1},{4,6},{5,7},{6,4},{7,5},{8,10},{9,11},{10,... | collective-permute-start | bytes 196616 | tf_op jit(solution)/shard_map/ppermute | solution.py:23
  43.3 0.0 collective-permute-done.10.refs_3_
  43.3 1.9 %collective-permute-start.17 = (bf16[64,512]{1,0:T(8,128)(2,1)S(1)}, bf16[64,512]{1,0:T(8,128)(2,1)S(1)}, u32[]{:S(2)}, u32[]{:S(2)}) collective-permute-start(bf16[64,512]{1,0:T(8,128)(2,1)S(1)} %get-tuple-element.75), channel_id=1, source_target_pairs={{0,3},{1,2},{2,1},{3,0},{4,7},{5,6},{6,5},{7,4},{8,11},{9,10},{10,... | collective-permute-start | bytes 196616 | tf_op jit(solution)/shard_map/ppermute | solution.py:23
  45.3 0.1 shard_map.99
  45.3 0.0 collective-permute-done.5.odd_first_ref
  45.3 0.1 collective-permute-start.11
  45.4 0.0 collective-permute-done.6.pair_second_ref
  45.4 1.2 %shard_map.97 = bf16[2,2,64,512]{3,2,1,0:T(8,128)(2,1)} custom-call(f32[256,512]{1,0:T(8,128)S(1)} %get-tuple-element.52.own_ref, f32[256,512]{1,0:T(8,128)S(1)} %get-tuple-element.53.enter_ref, f32[128,512]{1,0:T(8,128)S(1)} %get-tuple-element.54.slope_top_first_ref, f32[128,512]{1,0:T(8,128)S(1)} %get-tuple-element.55.slope_low_first_ref, ...), custom_call_target="tpu_custom_call" | custom-call | tf_op jit(solution)/shard_map/pallas_call | solution.py:52
  46.7 3.6 %collective-permute-done.16.refs_1_ = bf16[64,512]{1,0:T(8,128)(2,1)S(1)} collective-permute-done((bf16[64,512]{1,0:T(8,128)(2,1)S(1)}, bf16[64,512]{1,0:T(8,128)(2,1)S(1)}, u32[]{:S(2)}, u32[]{:S(2)}) %collective-permute-start.16) | collective-permute-done | bytes 65568 | tf_op jit(solution)/shard_map/ppermute | solution.py:23
  50.3 0.6 %collective-permute-done.11.refs_0_ = bf16[64,512]{1,0:T(8,128)(2,1)S(1)} collective-permute-done((bf16[64,512]{1,0:T(8,128)(2,1)S(1)}, bf16[64,512]{1,0:T(8,128)(2,1)S(1)}, u32[]{:S(2)}, u32[]{:S(2)}) %collective-permute-start.11) | collective-permute-done | bytes 65568 | tf_op jit(solution)/shard_map/ppermute | solution.py:23
  50.9 0.7 %shard_map.102 = (f32[192,128]{1,0:T(8,128)}, f32[64,128]{1,0:T(8,128)}) custom-call(f32[64,512]{1,0:T(8,128)S(1)} %get-tuple-element.67.keep_ref, bf16[64,512]{1,0:T(8,128)(2,1)S(1)} %collective-permute-done.11.refs_0_, bf16[64,512]{1,0:T(8,128)(2,1)S(1)} %collective-permute-done.16.refs_1_, bf16[64,512]{1,0:T(8,128)(2,1)S(1)} %collective-permute-done.17.refs_2_), custom_call_target="tpu_custom_call" | custom-call | tf_op jit(solution)/shard_map/pallas_call | solution.py:52
  (10 shorter events, 0.0 us)
Async XLA Ops:
  0.6 10.6 %copy-start.3 = (bf16[2,2,64,512]{3,2,1,0:T(8,128)(2,1)S(1)}, bf16[2,2,64,512]{3,2,1,0:T(8,128)(2,1)}, u32[]{:S(2)}) copy-start(bf16[2,2,64,512]{3,2,1,0:T(8,128)(2,1)} %cotangent_ref.3) | copy-start | bytes 786436
  0.6 10.6 %copy-start.4 = (bf16[512,512]{1,0:T(8,128)(2,1)S(1)}, bf16[512,512]{1,0:T(8,128)(2,1)}, u32[]{:S(2)}) copy-start(bf16[512,512]{1,0:T(8,128)(2,1)} %node_weight_ref.1) | copy-start | bytes 1572868
  2.0 9.3 %copy-start = (bf16[1536,512]{1,0:T(8,128)(2,1)S(1)}, bf16[1536,512]{1,0:T(8,128)(2,1)}, u32[]{:S(2)}) copy-start(bf16[1536,512]{1,0:T(8,128)(2,1)} %weight_ref.5) | copy-start | bytes 4718596
  2.0 9.3 %copy-start.1 = (bf16[3,2,2,64,512]{4,3,2,1,0:T(8,128)(2,1)S(1)}, bf16[3,2,2,64,512]{4,3,2,1,0:T(8,128)(2,1)}, u32[]{:S(2)}) copy-start(bf16[3,2,2,64,512]{4,3,2,1,0:T(8,128)(2,1)} %edge_ref.5) | copy-start | bytes 2359300
  2.0 9.3 %copy-start.2 = (bf16[2,2,64,512]{3,2,1,0:T(8,128)(2,1)S(1)}, bf16[2,2,64,512]{3,2,1,0:T(8,128)(2,1)}, u32[]{:S(2)}) copy-start(bf16[2,2,64,512]{3,2,1,0:T(8,128)(2,1)} %node_ref.5) | copy-start | bytes 786436
  2.0 9.3 %copy-start.5 = (s32[3,2,2,64]{3,2,1,0:T(2,128)S(1)}, s32[3,2,2,64]{3,2,1,0:T(2,128)}, u32[]{:S(2)}) copy-start(s32[3,2,2,64]{3,2,1,0:T(2,128)} %open_ref.1) | copy-start | bytes 9220
  2.1 7.6 %collective-permute-start = (bf16[272,512]{1,0:T(8,128)(2,1)S(1)}, bf16[272,512]{1,0:T(8,128)(2,1)S(1)}, u32[]{:S(2)}, u32[]{:S(2)}) collective-permute-start(bf16[272,512]{1,0:T(8,128)(2,1)S(1)} %get-tuple-element.47), channel_id=1, source_target_pairs={{0,4},{8,12},{16,20},{24,28},{4,0},{12,8},{20,16},{28,24},{1,5},{9... | collective-permute-start | bytes 835592 | tf_op jit(solution)/shard_map/ppermute | solution.py:18
  2.6 7.1 %collective-permute-start.1 = (bf16[272,512]{1,0:T(8,128)(2,1)S(1)}, bf16[272,512]{1,0:T(8,128)(2,1)S(1)}, u32[]{:S(2)}, u32[]{:S(2)}) collective-permute-start(bf16[272,512]{1,0:T(8,128)(2,1)S(1)} %get-tuple-element.48), channel_id=1, source_target_pairs={{4,8},{12,16},{20,24},{8,4},{16,12},{24,20},{5,9},{13,17},{21,25},... | collective-permute-start | bytes 835592 | tf_op jit(solution)/shard_map/ppermute | solution.py:18
  3.4 7.8 %collective-permute-start.2 = (bf16[272,512]{1,0:T(8,128)(2,1)S(1)}, bf16[272,512]{1,0:T(8,128)(2,1)S(1)}, u32[]{:S(2)}, u32[]{:S(2)}) collective-permute-start(bf16[272,512]{1,0:T(8,128)(2,1)S(1)} %get-tuple-element.49), channel_id=1, source_target_pairs={{0,1},{2,3},{1,0},{3,2},{4,5},{6,7},{5,4},{7,6},{8,9},{10,11},{9,8... | collective-permute-start | bytes 835592 | tf_op jit(solution)/shard_map/ppermute | solution.py:18
  6.1 5.2 %collective-permute-start.3 = (bf16[272,512]{1,0:T(8,128)(2,1)S(1)}, bf16[272,512]{1,0:T(8,128)(2,1)S(1)}, u32[]{:S(2)}, u32[]{:S(2)}) collective-permute-start(bf16[272,512]{1,0:T(8,128)(2,1)S(1)} %get-tuple-element.50), channel_id=1, source_target_pairs={{1,2},{2,1},{5,6},{6,5},{9,10},{10,9},{13,14},{14,13},{17,18},{18,... | collective-permute-start | bytes 835592 | tf_op jit(solution)/shard_map/ppermute | solution.py:18
  14.7 10.7 %collective-permute-start.4 = (bf16[640,512]{1,0:T(8,128)(2,1)S(1)}, bf16[640,512]{1,0:T(8,128)(2,1)S(1)}, u32[]{:S(2)}, u32[]{:S(2)}) collective-permute-start(bf16[640,512]{1,0:T(8,128)(2,1)S(1)} %shard_map.96), channel_id=1, source_target_pairs={{0,4},{8,12},{16,20},{24,28},{4,0},{12,8},{20,16},{28,24},{1,5},{9... | collective-permute-start | bytes 1966088 | tf_op jit(solution)/shard_map/ppermute | solution.py:18
  17.0 2.5 %collective-permute-start.12 = (bf16[512,512]{1,0:T(8,128)(2,1)S(1)}, bf16[512,512]{1,0:T(8,128)(2,1)S(1)}, u32[]{:S(2)}, u32[]{:S(2)}) collective-permute-start(bf16[512,512]{1,0:T(8,128)(2,1)S(1)} %get-tuple-element.69), channel_id=1, source_target_pairs={{0,4},{8,12},{16,20},{24,28},{4,0},{12,8},{20,16},{28,24},{1,5},{9... | collective-permute-start | bytes 1572872 | tf_op jit(solution)/shard_map/ppermute | solution.py:18
  19.6 8.0 %collective-permute-start.13 = (bf16[128,512]{1,0:T(8,128)(2,1)S(1)}, bf16[128,512]{1,0:T(8,128)(2,1)S(1)}, u32[]{:S(2)}, u32[]{:S(2)}) collective-permute-start(bf16[128,512]{1,0:T(8,128)(2,1)S(1)} %get-tuple-element.71), channel_id=1, source_target_pairs={{0,8},{4,12},{8,0},{12,4},{16,24},{20,28},{24,16},{28,20},{1,9},{5... | collective-permute-start | bytes 393224 | tf_op jit(solution)/shard_map/ppermute | solution.py:23
  23.0 7.7 %collective-permute-start.14 = (bf16[128,512]{1,0:T(8,128)(2,1)S(1)}, bf16[128,512]{1,0:T(8,128)(2,1)S(1)}, u32[]{:S(2)}, u32[]{:S(2)}) collective-permute-start(bf16[128,512]{1,0:T(8,128)(2,1)S(1)} %get-tuple-element.72), channel_id=1, source_target_pairs={{0,16},{4,20},{8,24},{12,28},{16,0},{20,4},{24,8},{28,12},{1,17},{... | collective-permute-start | bytes 393224 | tf_op jit(solution)/shard_map/ppermute | solution.py:23
  24.0 8.6 %collective-permute-start.15 = (bf16[128,512]{1,0:T(8,128)(2,1)S(1)}, bf16[128,512]{1,0:T(8,128)(2,1)S(1)}, u32[]{:S(2)}, u32[]{:S(2)}) collective-permute-start(bf16[128,512]{1,0:T(8,128)(2,1)S(1)} %get-tuple-element.73), channel_id=1, source_target_pairs={{0,24},{4,28},{8,16},{12,20},{16,8},{20,12},{24,0},{28,4},{1,25},{... | collective-permute-start | bytes 393224 | tf_op jit(solution)/shard_map/ppermute | solution.py:23
  25.5 12.1 %collective-permute-start.8 = (bf16[128,512]{1,0:T(8,128)(2,1)S(1)}, bf16[128,512]{1,0:T(8,128)(2,1)S(1)}, u32[]{:S(2)}, u32[]{:S(2)}) collective-permute-start(bf16[128,512]{1,0:T(8,128)(2,1)S(1)} %get-tuple-element.64), channel_id=1, source_target_pairs={{0,8},{4,12},{8,0},{12,4},{16,24},{20,28},{24,16},{28,20},{1,9},{5... | collective-permute-start | bytes 393224 | tf_op jit(solution)/shard_map/ppermute | solution.py:23
  26.7 11.7 %collective-permute-start.9 = (bf16[128,512]{1,0:T(8,128)(2,1)S(1)}, bf16[128,512]{1,0:T(8,128)(2,1)S(1)}, u32[]{:S(2)}, u32[]{:S(2)}) collective-permute-start(bf16[128,512]{1,0:T(8,128)(2,1)S(1)} %get-tuple-element.65), channel_id=1, source_target_pairs={{0,16},{4,20},{8,24},{12,28},{16,0},{20,4},{24,8},{28,12},{1,17},{... | collective-permute-start | bytes 393224 | tf_op jit(solution)/shard_map/ppermute | solution.py:23
  27.7 15.7 %collective-permute-start.10 = (bf16[128,512]{1,0:T(8,128)(2,1)S(1)}, bf16[128,512]{1,0:T(8,128)(2,1)S(1)}, u32[]{:S(2)}, u32[]{:S(2)}) collective-permute-start(bf16[128,512]{1,0:T(8,128)(2,1)S(1)} %get-tuple-element.66), channel_id=1, source_target_pairs={{0,24},{4,28},{8,16},{12,20},{16,8},{20,12},{24,0},{28,4},{1,25},{... | collective-permute-start | bytes 393224 | tf_op jit(solution)/shard_map/ppermute | solution.py:23
  30.7 14.7 %collective-permute-start.5 = (bf16[128,512]{1,0:T(8,128)(2,1)S(1)}, bf16[128,512]{1,0:T(8,128)(2,1)S(1)}, u32[]{:S(2)}, u32[]{:S(2)}) collective-permute-start(bf16[128,512]{1,0:T(8,128)(2,1)S(1)} %get-tuple-element.60), channel_id=1, source_target_pairs={{4,8},{12,16},{20,24},{8,4},{16,12},{24,20},{5,9},{13,17},{21,25},... | collective-permute-start | bytes 393224 | tf_op jit(solution)/shard_map/ppermute | solution.py:18
  32.6 12.9 %collective-permute-start.6 = (bf16[128,512]{1,0:T(8,128)(2,1)S(1)}, bf16[128,512]{1,0:T(8,128)(2,1)S(1)}, u32[]{:S(2)}, u32[]{:S(2)}) collective-permute-start(bf16[128,512]{1,0:T(8,128)(2,1)S(1)} %get-tuple-element.61), channel_id=1, source_target_pairs={{0,1},{2,3},{1,0},{3,2},{4,5},{6,7},{5,4},{7,6},{8,9},{10,11},{9,8... | collective-permute-start | bytes 393224 | tf_op jit(solution)/shard_map/ppermute | solution.py:18
  37.6 7.8 %collective-permute-start.7 = (bf16[128,512]{1,0:T(8,128)(2,1)S(1)}, bf16[128,512]{1,0:T(8,128)(2,1)S(1)}, u32[]{:S(2)}, u32[]{:S(2)}) collective-permute-start(bf16[128,512]{1,0:T(8,128)(2,1)S(1)} %get-tuple-element.62), channel_id=1, source_target_pairs={{1,2},{2,1},{5,6},{6,5},{9,10},{10,9},{13,14},{14,13},{17,18},{18,... | collective-permute-start | bytes 393224 | tf_op jit(solution)/shard_map/ppermute | solution.py:18
  38.3 12.0 %collective-permute-start.16 = (bf16[64,512]{1,0:T(8,128)(2,1)S(1)}, bf16[64,512]{1,0:T(8,128)(2,1)S(1)}, u32[]{:S(2)}, u32[]{:S(2)}) collective-permute-start(bf16[64,512]{1,0:T(8,128)(2,1)S(1)} %get-tuple-element.74), channel_id=1, source_target_pairs={{0,2},{1,3},{2,0},{3,1},{4,6},{5,7},{6,4},{7,5},{8,10},{9,11},{10,... | collective-permute-start | bytes 196616 | tf_op jit(solution)/shard_map/ppermute | solution.py:23
  43.3 7.0 %collective-permute-start.17 = (bf16[64,512]{1,0:T(8,128)(2,1)S(1)}, bf16[64,512]{1,0:T(8,128)(2,1)S(1)}, u32[]{:S(2)}, u32[]{:S(2)}) collective-permute-start(bf16[64,512]{1,0:T(8,128)(2,1)S(1)} %get-tuple-element.75), channel_id=1, source_target_pairs={{0,3},{1,2},{2,1},{3,0},{4,7},{5,6},{6,5},{7,4},{8,11},{9,10},{10,... | collective-permute-start | bytes 196616 | tf_op jit(solution)/shard_map/ppermute | solution.py:23
  45.3 5.6 %collective-permute-start.11 = (bf16[64,512]{1,0:T(8,128)(2,1)S(1)}, bf16[64,512]{1,0:T(8,128)(2,1)S(1)}, u32[]{:S(2)}, u32[]{:S(2)}) collective-permute-start(bf16[64,512]{1,0:T(8,128)(2,1)S(1)} %get-tuple-element.68), channel_id=1, source_target_pairs={{0,1},{1,0},{2,3},{3,2},{4,5},{5,4},{6,7},{7,6},{8,9},{9,8},{10,11... | collective-permute-start | bytes 196616 | tf_op jit(solution)/shard_map/ppermute | solution.py:23
